TPU v7x, 32 devices: a whole 2x2x4 slice. The times are simulated.
32 devices in a mesh: dp: 16 (over z, y, x), tensor: 2 (over core).
Axes of the slice: x: 2, y: 2, z: 4, core: 2. Of those that a mesh axis runs over, the one named last changes fastest.
Arguments:
- inputs: bfloat16 [16, 1024, 768], P('dp', 'tensor'), may hold values from -6 to 6
- cotangent: bfloat16 [16, 1024, 768], P('dp', 'tensor'), may hold values from -6 to 6
- qkv_weight: bfloat16 [3, 768, 768], P(None, 'dp', 'tensor'), may hold values from -0.3125 to 0.3125
- out_weight: bfloat16 [768, 768], P('tensor', 'dp'), may hold values from -2.5 to 2.5
- fc1_weight: bfloat16 [768, 3072], P('dp', 'tensor'), may hold values from -0.21875 to 0.21875
- fc2_weight: bfloat16 [3072, 768], P('tensor', 'dp'), may hold values from -0.109375 to 0.109375
- norm_gains: bfloat16 [2, 768], P(None, 'dp'), may hold values from 0.25 to 1.75
- shifts: bfloat16 [4, 768], P(None, 'dp'), may hold values from -3 to 3
- qv_bias: bfloat16 [2, 768], P(None, 'tensor'), may hold values from -3 to 3
- fc1_bias: bfloat16 [3072], P('tensor'), may hold values from -3 to 3
Outputs:
- outputs: float32 [16, 1024, 768], P('dp', 'tensor')
- input_grad: float32 [16, 1024, 768], P('dp', 'tensor')
- qkv_grad: float32 [3, 768, 768], P(None, 'dp', 'tensor')
- out_grad: float32 [768, 768], P('tensor', 'dp')
- fc1_grad: float32 [768, 3072], P('dp', 'tensor')
- fc2_grad: float32 [3072, 768], P('tensor', 'dp')
- gains_grad: float32 [2, 768], P(None, 'dp')
- shifts_grad: float32 [4, 768], P(None, 'dp')
- qv_grad: float32 [2, 768], P(None, 'tensor')
- fc1_bias_grad: float32 [3072], P('tensor')
All inputs are finite; a program needn't handle non-finite values.
Results may differ from a plain program's by a relative error of at most 0.012.
The roundings to bfloat16 on the way count: a program that leaves them out, or rounds other values in their place, can miss the bound.
Values may be sent and summed in bfloat16 or wider, within the bound.
No kernel may reach another device: no remote copies, remote signals or barrier semaphores. Data moves between devices by JAX's collectives and lax.ppermute only.
A program may use at most 192 MiB of HBM per device.

v0:
```python
import functools

import jax
import jax.numpy as jnp
from jax import lax
from jax.experimental import pallas as pl
from jax.experimental.pallas import tpu as pltpu
from jax.sharding import PartitionSpec as P

HEAD = 64
PAIR = 2 * HEAD
ATTEND_VMEM = 20 * 2**20
BACK_VMEM = 24 * 2**20
ROWS_VMEM = 16 * 2**20
PIECES = 2
ROW_BLOCK = 256
COLUMN_BLOCK = 384
FREE = pl.CostEstimate(flops=0, bytes_accessed=0, transcendentals=0)
EPS = 1e-05
BF = jnp.bfloat16
F32 = jnp.float32


def after(x, *others):
    return lax.optimization_barrier((x, others))[0]


def stage(*values):
    return lax.optimization_barrier(values)


def digits_of(n):
    low = 4 if n % 4 == 0 else n
    found, stride = [(1, low)], low
    while stride < n:
        found.append((stride, 2))
        stride *= 2
    return found


def swap_dp(x, step):
    n = lax.axis_size("dp")
    return lax.ppermute(x, "dp", [(i, i ^ step) for i in range(n)])


def swap_core(x):
    return lax.ppermute(x, "tensor", [(0, 1), (1, 0)])


def position(own):
    n = lax.axis_size("dp")
    me = lax.axis_index("dp")
    bits = [(me >> i) & 1 for i in range(n.bit_length() - 1)]
    low = me & 3
    return {
        "bits": [(me & (1 << i)) != 0 for i in range(len(bits))],
        "low": [low ^ k for k in range(4)],
        "high": [[bit, 1 - bit] for bit in bits[2:]],
        "digit": low.reshape(1),
        "start": (me * own).reshape(1),
    }


def pick(options, bits):
    for bit in bits:
        options = [jnp.where(bit, b, a) for a, b in zip(options[0::2], options[1::2])]
    return options[0]


def place(got, stride, at):
    radix = len(got)
    first = stride.bit_length() - 1
    bits = at["bits"][first : first + radix.bit_length() - 1]
    placed = [pick([got[i ^ m] for m in range(radix)], bits) for i in range(radix)]
    return jnp.stack(placed, axis=1).reshape((-1,) + got[0].shape[1:])


def gather_high_at_once(x, at):
    n = lax.axis_size("dp")
    low = digits_of(n)[0][1]
    stride = n // 4
    cur = place([x[None]] + [swap_dp(x[None], stride * k) for k in range(1, 4)], stride, at)
    while stride > low:
        stride //= 2
        cur = place([cur, swap_dp(cur, stride)], stride, at)
    return cur


def gather_near(cur):
    return swap_dp(cur, 1), swap_dp(cur, 2)


def gather_far(near):
    half = near[0].shape[0] // 2
    return swap_dp(near[0][:half], 2), swap_dp(near[1][half:], 1)


def gather_low(cur):
    return [swap_dp(cur, k) for k in range(1, digits_of(lax.axis_size("dp"))[0][1])]


def rows_kernel(start, mine_ref, *refs):
    sources, out_ref = refs[:-1], refs[-1]
    high, _, _, columns = out_ref.shape
    mine = mine_ref[0]
    here = pl.ds(start, columns)
    for i in range(high):
        for k, source in enumerate(sources[:3]):
            out_ref[i, mine ^ k] = source[i, :, here]
        far = sources[3 + i * (len(sources) - 3) // high]
        out_ref[i, mine ^ 3] = far[i % far.shape[0]]


def all_rows(sources, start, columns, at):
    high, rows, _ = sources[0].shape
    full = pl.pallas_call(
        functools.partial(rows_kernel, start),
        in_specs=[pl.BlockSpec(memory_space=pltpu.SMEM)]
        + [pl.BlockSpec(memory_space=pltpu.VMEM)] * len(sources),
        out_specs=pl.BlockSpec(memory_space=pltpu.VMEM),
        out_shape=jax.ShapeDtypeStruct((high, 4, rows, columns), BF),
        cost_estimate=FREE,
        compiler_params=pltpu.CompilerParams(vmem_limit_bytes=ROWS_VMEM),
        name="all_rows",
    )(at["digit"], *sources)
    return full.reshape(-1, columns)


def part_of(view, index, first=0, count=0):
    sizes = (count or view.shape[0], 1) + view.shape[2:]
    starts = [jnp.int32(first), index] + [jnp.int32(0)] * (view.ndim - 2)
    piece = lax.dynamic_slice(view, starts, sizes, allow_negative_indices=False)
    return piece.reshape(sizes[:1] + sizes[2:])


def total_of(parts):
    total = parts[0].astype(F32)
    for part in parts[1:]:
        total = total + part.astype(F32)
    return total


def scatter_operands(x, at):
    n = lax.axis_size("dp")
    view = x.reshape(n // 4, 4, x.shape[0] // n, x.shape[1])
    half = view.shape[0] // 2
    one, two, across = (
        [part_of(view, index, first, half) for first in (0, half)] for index in at["low"][1:]
    )
    return (part_of(view, at["low"][0]), one, two), across


def scatter_low_across(operands):
    return swap_dp(operands[0], 1), swap_dp(operands[1], 2)


def near_operands(parts, across):
    mine, one, two = parts
    one = jnp.concatenate([one[0], total_of([one[1], across[1]]).astype(BF)], axis=0)
    two = jnp.concatenate([total_of([two[0], across[0]]).astype(BF), two[1]], axis=0)
    return mine, one, two


def scatter_low_near(operands):
    mine, one, two = operands
    return mine, swap_dp(one, 1), swap_dp(two, 2)


def high_operands(cur, index, at):
    view = cur.reshape((-1, 2) + cur.shape[1:])
    kept, sent = (part_of(view, i) for i in at["high"][index])
    return kept, sent.astype(BF)


def scatter_high_step(operands, index):
    stride, _ = digits_of(lax.axis_size("dp"))[1 + index]
    return operands[0] + swap_dp(operands[1], stride).astype(F32)


def scatter_high_last(cur, index, at):
    digits = digits_of(lax.axis_size("dp"))[1:]
    for i in range(index, len(digits) - 1):
        cur = scatter_high_step(high_operands(cur, i, at), i)
    kept, sent = high_operands(cur, len(digits) - 1, at)
    return kept[0], swap_dp(sent, digits[-1][0])[0]


def sum_over(x, steps):
    for step in steps:
        x = x + swap_dp(x, step)
    return x


def swap_pieces(x, count):
    rows = x.shape[0] // count
    return [swap_core(x[i * rows : (i + 1) * rows]) for i in range(count)]


def dot(a, b, ca, cb):
    return lax.dot_general(a, b, (((ca,), (cb,)), ((), ())), preferred_element_type=F32)


def attend_kernel(qkv_ref, *refs):
    out_ref, lse_ref = refs[-2:]
    queries = qkv_ref[:, :PAIR]
    keys_all = qkv_ref[:, PAIR : 2 * PAIR] * jnp.asarray(HEAD**-0.5, BF)
    values = qkv_ref[:, 2 * PAIR :]
    first = lax.broadcasted_iota(jnp.int32, (1, PAIR), 1) < HEAD
    outs, logs = [], []
    for own in (first, ~first):
        here = jnp.where(own, queries, jnp.zeros_like(queries))
        scores = dot(keys_all, here, 1, 1)
        row_max = jnp.max(scores, axis=0, keepdims=True)
        powers = jnp.exp(scores - row_max)
        summed = jnp.sum(powers, axis=0, keepdims=True)
        probs = (powers * (1.0 / summed)).astype(BF)
        outs.append(dot(values, probs, 0, 0))
        logs.append(row_max + jnp.log(summed))
    both = jnp.concatenate([outs[0][:HEAD], outs[1][HEAD:]], axis=0)
    out_ref[...] = both.T.astype(BF)
    lse_ref[...] = jnp.concatenate(logs, axis=0)[None]


def attend(qkv, start, count, kept=()):
    n, width = qkv.shape
    pairs = width // (3 * PAIR)
    return pl.pallas_call(
        attend_kernel,
        grid=(count,),
        in_specs=[pl.BlockSpec((n, 3 * PAIR), lambda p: (0, p + start))]
        + [pl.BlockSpec(memory_space=pl.ANY)] * len(kept),
        out_specs=[
            pl.BlockSpec((n, PAIR), lambda p: (0, p + start)),
            pl.BlockSpec((1, 2, n), lambda p: (p + start, 0, 0)),
        ],
        out_shape=[
            jax.ShapeDtypeStruct((n, pairs * PAIR), BF),
            jax.ShapeDtypeStruct((pairs, 2, n), F32),
        ],
        input_output_aliases={1 + i: i for i in range(len(kept))},
        compiler_params=pltpu.CompilerParams(vmem_limit_bytes=ATTEND_VMEM),
        cost_estimate=FREE,
        name="attend",
    )(qkv, *kept)


def attend_back_kernel(qkv_ref, lse_ref, grad_ref, *refs):
    out_ref, sum_ref = refs[-2:]
    factor = jnp.asarray(HEAD**-0.5, BF)
    queries = qkv_ref[:, :PAIR]
    keys_small = qkv_ref[:, PAIR : 2 * PAIR] * factor
    values = qkv_ref[:, 2 * PAIR :]
    grad = grad_ref[...]
    first = lax.broadcasted_iota(jnp.int32, (1, PAIR), 1) < HEAD
    parts = []
    for own in (first, ~first):
        q_here = jnp.where(own, queries, jnp.zeros_like(queries))
        g_here = jnp.where(own, grad, jnp.zeros_like(grad))
        parts.append((q_here, g_here, dot(keys_small, q_here, 1, 1), dot(values, g_here, 1, 1)))
    d_q, d_k, d_v = [], [], []
    for head, (q_here, g_here, scores, d_probs) in enumerate(parts):
        probs = jnp.exp(scores - lse_ref[0, head : head + 1, :])
        product = probs * d_probs
        row_sum = jnp.sum(product, axis=0, keepdims=True)
        d_scores = (product - probs * row_sum).astype(BF)
        d_v.append(dot(probs.astype(BF), g_here, 1, 0))
        d_k.append(dot(d_scores, q_here, 1, 0))
        d_q.append(dot(keys_small, d_scores, 0, 0))
    queries_t = jnp.concatenate([d_q[0][:HEAD], d_q[1][HEAD:]], axis=0)
    d_queries = queries_t.T.astype(BF)
    d_keys = ((d_k[0] + d_k[1]) * HEAD**-0.5).astype(BF)
    d_values = (d_v[0] + d_v[1]).astype(BF)
    for i, x in enumerate((d_queries, d_keys, d_values)):
        out_ref[:, i * PAIR : (i + 1) * PAIR] = x
        sum_ref[0, :, i * PAIR : (i + 1) * PAIR] = jnp.sum(x.astype(F32), axis=0, keepdims=True)


def attend_back(qkv, lse, grad, start, count, kept=()):
    n, width = qkv.shape
    pairs = width // (3 * PAIR)
    return pl.pallas_call(
        attend_back_kernel,
        grid=(count,),
        in_specs=[
            pl.BlockSpec((n, 3 * PAIR), lambda p: (0, p + start)),
            pl.BlockSpec((1, 2, n), lambda p: (p + start, 0, 0)),
            pl.BlockSpec((n, PAIR), lambda p: (0, p + start)),
        ]
        + [pl.BlockSpec(memory_space=pl.ANY)] * len(kept),
        out_specs=[
            pl.BlockSpec((n, 3 * PAIR), lambda p: (0, p + start)),
            pl.BlockSpec((1, 1, 3 * PAIR), lambda p: (p + start, 0, 0)),
        ],
        out_shape=[
            jax.ShapeDtypeStruct((n, width), BF),
            jax.ShapeDtypeStruct((pairs, 1, 3 * PAIR), F32),
        ],
        input_output_aliases={3 + i: i for i in range(len(kept))},
        compiler_params=pltpu.CompilerParams(vmem_limit_bytes=BACK_VMEM),
        cost_estimate=FREE,
        name="attend_back",
    )(qkv, lse, grad, *kept)


def rows_call(kernel, out_shape, name):
    return pl.pallas_call(
        kernel,
        out_shape=out_shape,
        cost_estimate=FREE,
        compiler_params=pltpu.CompilerParams(vmem_limit_bytes=ROWS_VMEM),
        name=name,
    )


def each_block(rows, step):
    @pl.loop(0, rows // ROW_BLOCK)
    def _(i):
        step(pl.ds(pl.multiple_of(i * ROW_BLOCK, ROW_BLOCK), ROW_BLOCK))


def pack_kernel(qkv_ref, out_ref, gains_ref, shifts_ref, packed_ref, small_ref):
    rows, wide = out_ref.shape
    for pair in range(wide // PAIR):
        for i in range(3):
            start = (3 * pair + i) * PAIR
            packed_ref[:, start : start + PAIR] = qkv_ref[i, :, pair * PAIR : (pair + 1) * PAIR]
    packed_ref[:, 3 * wide : 4 * wide] = out_ref[...]
    small_ref[...] = jnp.zeros_like(small_ref)
    small_ref[0:2, :rows] = gains_ref[...].astype(F32)
    small_ref[2:6, :rows] = shifts_ref[...].astype(F32)
    packed_ref[:, 4 * wide :] = jnp.zeros_like(packed_ref[:, 4 * wide :])
    packed_ref[:, 4 * wide : 4 * wide + 8] = small_ref[...].T[:rows].astype(BF)


def pack(qkv_weight, out_weight, gains, shifts):
    rows, wide = out_weight.shape
    args = (qkv_weight, out_weight, gains, shifts)
    shape = (rows, 4 * wide + PAIR)
    return pl.pallas_call(
        pack_kernel,
        out_shape=jax.ShapeDtypeStruct(shape, BF),
        scratch_shapes=[pltpu.VMEM((8, PAIR), F32)],
        cost_estimate=FREE,
        compiler_params=pltpu.CompilerParams(vmem_limit_bytes=4 * 2**20),
        name="pack",
    )(*args)


def finish_qkv_kernel(kept_ref, got_ref, out_ref):
    total = kept_ref[...] + got_ref[...].astype(F32)
    for pair in range(out_ref.shape[2] // PAIR):
        for i in range(3):
            start = (3 * pair + i) * PAIR
            out_ref[i, :, pair * PAIR : (pair + 1) * PAIR] = total[:, start : start + PAIR]


def finish_ff_kernel(kept_ref, got_ref, *out_refs):
    total = kept_ref[...] + got_ref[...].astype(F32)
    start = 0
    for out_ref in out_refs:
        columns = out_ref.shape[1]
        out_ref[...] = total[:, start : start + columns]
        start += columns


def finish_sums_kernel(kept_ref, got_ref, start_ref, gains_ref, shifts_ref, qv_ref, bias_ref):
    own = gains_ref.shape[1]
    total = kept_ref[...] + got_ref[...]
    columns = total.shape[1]
    rows = pltpu.roll(total[:8], columns - start_ref[0], 1)[:, :own]
    gains_ref[...] = jnp.concatenate([rows[0:1], rows[2:3]], axis=0)
    shifts_ref[...] = jnp.concatenate([rows[1:2], rows[3:6]], axis=0)
    pairs = qv_ref.shape[1] // PAIR
    for pair in range(pairs):
        for i in range(2):
            here = slice(2 * i * PAIR, (2 * i + 1) * PAIR)
            qv_ref[i : i + 1, pair * PAIR : (pair + 1) * PAIR] = total[6 + pair : 7 + pair, here]
    bias_ref[...] = total[6 + pairs :]


def finish_sums(kept, got, start, shapes):
    return pl.pallas_call(
        finish_sums_kernel,
        in_specs=[pl.BlockSpec(memory_space=pltpu.VMEM)] * 2
        + [pl.BlockSpec(memory_space=pltpu.SMEM)],
        out_specs=[pl.BlockSpec(memory_space=pltpu.VMEM)] * 4,
        out_shape=[jax.ShapeDtypeStruct(x, F32) for x in shapes],
        cost_estimate=FREE,
        compiler_params=pltpu.CompilerParams(vmem_limit_bytes=4 * 2**20),
        name="finish_sums",
    )(kept, got, start)


def finish(kernel, kept, got, shapes, name):
    return pl.pallas_call(
        kernel,
        out_shape=[jax.ShapeDtypeStruct(x, F32) for x in shapes],
        cost_estimate=FREE,
        compiler_params=pltpu.CompilerParams(vmem_limit_bytes=8 * 2**20),
        name=name,
    )(kept, got)


def join_kernel(mine_ref, other_ref, out_ref):
    half = mine_ref.shape[0]
    out_ref[:half] = mine_ref[...]
    out_ref[half:] = other_ref[...]


def join(mine, other):
    rows, columns = mine.shape
    shape = jax.ShapeDtypeStruct((2 * rows, columns), mine.dtype)
    return rows_call(join_kernel, shape, "join")(mine, other)


def standardized(x):
    center = x - jnp.mean(x, axis=-1, keepdims=True)
    inv_std = lax.rsqrt(jnp.mean(center * center, axis=-1, keepdims=True) + EPS)
    return center * inv_std, inv_std


def project_kernel(x_ref, weight_ref, bias_ref, normed_ref, qkv_ref, vectors_ref):
    width = qkv_ref.shape[1]
    small = weight_ref.shape[1] - PAIR
    vectors = weight_ref[:, small:].astype(F32).T[:8]
    vectors_ref[...] = vectors

    def step(here):
        unit, _ = standardized(x_ref[here].astype(F32))
        normed = (unit * vectors_ref[0:1] + vectors_ref[2:3]).astype(BF)
        normed_ref[here] = normed
        qkv_ref[here] = (dot(normed, weight_ref[:, :width], 1, 0) + bias_ref[...]).astype(BF)

    for i in range(0, x_ref.shape[0], ROW_BLOCK):
        step(pl.ds(i, ROW_BLOCK))


def project(x, first_full, bias, width):
    rows, columns = x.shape
    shapes = [
        jax.ShapeDtypeStruct((rows, columns), BF),
        jax.ShapeDtypeStruct((rows, width), BF),
        jax.ShapeDtypeStruct((8, columns), F32),
    ]
    return rows_call(project_kernel, shapes, "project")(x, first_full, bias)


def halves_of(refs, others):
    half = others[0].shape[0]
    return [
        ([ref.at[pl.ds(i * half, half)] for ref in refs], others[1 - i]) for i in range(PIECES)
    ]


def mid_norm_kernel(x_ref, mine_ref, vectors_ref, *refs):
    others, (hidden_ref, normed_ref) = refs[:PIECES], refs[PIECES:]
    for refs, other_ref in halves_of((x_ref, mine_ref, hidden_ref, normed_ref), others):
        frames, mine, hidden_half, normed_half = refs

        def step(here):
            branch = mine[here].astype(F32) + other_ref[here].astype(F32)
            hidden = frames[here].astype(F32) + (branch + vectors_ref[3:4])
            hidden_half[here] = hidden
            unit, _ = standardized(hidden)
            normed_half[here] = (unit * vectors_ref[1:2] + vectors_ref[4:5]).astype(BF)

        each_block(other_ref.shape[0], step)


def mid_norm(x, mine, others, vectors):
    shapes = [jax.ShapeDtypeStruct(x.shape, t) for t in (F32, BF)]
    return rows_call(mid_norm_kernel, shapes, "mid_norm")(x, mine, vectors, *others)


def act_back_kernel(d_out_ref, weight_ref, slope_ref, d_pre_ref, sums_ref):
    @pl.loop(0, d_pre_ref.shape[1] // COLUMN_BLOCK)
    def _(i):
        here = pl.ds(pl.multiple_of(i * COLUMN_BLOCK, COLUMN_BLOCK), COLUMN_BLOCK)
        d_act = dot(d_out_ref[...], weight_ref[:, here], 1, 0)
        d_pre = (d_act * slope_ref[:, here].astype(F32)).astype(BF)
        d_pre_ref[:, here] = d_pre
        sums_ref[:, here] = total_rows(d_pre.astype(F32))


def act_back(d_out, weight, slope):
    shapes = [jax.ShapeDtypeStruct(slope.shape, BF), jax.ShapeDtypeStruct((1, slope.shape[1]), F32)]
    return rows_call(act_back_kernel, shapes, "act_back")(d_out, weight, slope)


def norm_back(unit, inv_std, gain, grad):
    scaled = grad * gain
    return inv_std * (
        scaled
        - jnp.mean(scaled, axis=-1, keepdims=True)
        - unit * jnp.mean(scaled * unit, axis=-1, keepdims=True)
    )


def total_rows(x):
    return jnp.sum(x, axis=0, keepdims=True)


def mid_norm_back_kernel(mine_ref, hidden_ref, d_out_ref, vectors_ref, *refs):
    others, (branch_ref, d_hidden_ref, sums_ref) = refs[:PIECES], refs[PIECES:]
    sums_ref[...] = jnp.zeros_like(sums_ref)
    halves = halves_of((mine_ref, hidden_ref, d_out_ref, branch_ref), others)
    for i, (refs, other_ref) in enumerate(halves):
        mine, hidden, d_outs, branch = refs

        def step(here):
            grad = mine[here].astype(F32) + other_ref[here].astype(F32)
            unit, inv_std = standardized(hidden[here])
            d_out = d_outs[here].astype(F32)
            d_hidden = d_out + norm_back(unit, inv_std, vectors_ref[1:2], grad)
            d_branch = d_hidden.astype(BF)
            branch[here] = d_branch
            if i == 0:
                d_hidden_ref[here] = d_hidden
                terms = (grad * unit, d_branch.astype(F32), grad, d_out)
                sums_ref[...] += jnp.concatenate([total_rows(x) for x in terms], axis=0)

        each_block(other_ref.shape[0], step)


def mid_norm_back(mine, others, hidden, d_out, vectors):
    rows, columns = hidden.shape
    shapes = [
        jax.ShapeDtypeStruct((rows, columns), BF),
        jax.ShapeDtypeStruct((rows // 2, columns), F32),
        jax.ShapeDtypeStruct((4, columns), F32),
    ]
    return rows_call(mid_norm_back_kernel, shapes, "mid_norm_back")(
        mine, hidden, d_out, vectors, *others
    )


def first_norm_back_kernel(
    qkv_ref, weight_ref, x_ref, d_hidden_ref, vectors_ref, first_ref, second_ref, grad_ref, sums_ref
):
    sums = [jnp.zeros((1, x_ref.shape[1]), F32)] * 2
    width = qkv_ref.shape[1]
    rows = first_ref.shape[0]
    for i in range(x_ref.shape[0] // ROW_BLOCK):
        here = pl.ds(i * ROW_BLOCK, ROW_BLOCK)
        other_ref = (first_ref, second_ref)[i * ROW_BLOCK // rows]
        other = other_ref[pl.ds(i * ROW_BLOCK % rows, ROW_BLOCK)].astype(F32)
        grad = dot(qkv_ref[here], weight_ref[:, :width], 1, 1) + other
        unit, inv_std = standardized(x_ref[here].astype(F32))
        grad_ref[here] = d_hidden_ref[here] + norm_back(unit, inv_std, vectors_ref[0:1], grad)
        sums = [a + total_rows(b) for a, b in zip(sums, (grad * unit, grad))]
    sums_ref[...] = jnp.concatenate(sums, axis=0)


def first_norm_back(d_qkv, first_full, others, x, d_hidden, vectors):
    rows, columns = x.shape
    shapes = [jax.ShapeDtypeStruct((n, columns), F32) for n in (rows, 2)]
    return rows_call(first_norm_back_kernel, shapes, "first_norm_back")(
        d_qkv, first_full, x, d_hidden, vectors, *others
    )


def mm(spec, a, b):
    return jnp.einsum(spec, a, b, preferred_element_type=F32)


def body(
    inputs,
    cotangent,
    qkv_weight,
    out_weight,
    fc1_weight,
    fc2_weight,
    norm_gains,
    shifts,
    qv_bias,
    fc1_bias,
):
    inputs = inputs[0]
    cotangent = cotangent[0]
    own = norm_gains.shape[1]
    wide = qkv_weight.shape[2]
    pairs = wide // PAIR

    first_own = pack(qkv_weight, out_weight.T, norm_gains, shifts)
    at = position(own)
    zeros = jnp.zeros((wide,), BF)
    qkv_bias = jnp.stack([qv_bias[0], zeros, qv_bias[1]]).reshape(3, pairs, PAIR)
    qkv_bias = qkv_bias.transpose(1, 0, 2).reshape(1, 3 * wide).astype(F32)
    half = inputs.shape[0]
    hidden_n = fc1_weight.shape[1]
    high = [stride for stride, _ in reversed(digits_of(lax.axis_size("dp"))[1:])]
    first_own, at, qkv_bias = stage(first_own, at, qkv_bias)
    first_part = gather_high_at_once(first_own, at)
    inputs_other = swap_core(inputs)

    ff_own = jnp.concatenate([fc1_weight, fc2_weight.T], axis=1)

    first_part, inputs_other, ff_part = stage(first_part, inputs_other, ff_own[None])
    first_near = gather_near(first_part)
    inputs_all = join(inputs, inputs_other)
    for stride in high[:-1]:
        ff_part = place([ff_part, swap_dp(ff_part, stride)], stride, at)

    first_part, first_near, ff_part, inputs_all = stage(
        first_part, first_near, ff_part, inputs_all
    )
    first_far = gather_far(first_near)
    for stride in high[-1:]:
        ff_part = place([ff_part, swap_dp(ff_part, stride)], stride, at)

    first_part, first_near, first_far, ff_part = stage(first_part, first_near, first_far, ff_part)
    ff_near = gather_near(ff_part)
    cotangent_other = swap_core(after(cotangent, first_part))
    first_full = all_rows([first_part, *first_near, *first_far], 0, first_part.shape[2], at)
    out_full = first_full[:, 3 * wide : 4 * wide]
    normed_all, qkv, vectors = project(inputs_all, first_full, qkv_bias, 3 * wide)
    attended, log_sums = attend(qkv, 0, pairs)
    branch = mm("fe,de->fd", attended, out_full).astype(BF)
    branch_other = swap_pieces(branch, PIECES)
    hidden_all, normed_two_all = mid_norm(inputs_all, branch, branch_other, vectors)

    ff_part, ff_near, normed_two_all, cotangent_other = stage(
        ff_part, ff_near, normed_two_all, cotangent_other
    )
    mid_far = gather_far([x[:, :, :hidden_n] for x in ff_near])
    d_out_all = join(cotangent, cotangent_other)

    ff_part, ff_near, mid_far, d_out_all = stage(ff_part, ff_near, mid_far, d_out_all)
    end_far = gather_far([x[:, :, hidden_n:] for x in ff_near])
    mid_full = all_rows([ff_part, *ff_near, *mid_far], 0, hidden_n, at)
    hidden_pre = mm("fd,dh->fh", normed_two_all, mid_full) + fc1_bias.astype(F32)
    cdf = 0.5 * (1.0 + lax.erf(hidden_pre * 0.5**0.5))
    hidden_act = (hidden_pre * cdf).astype(BF)
    slope = cdf + hidden_pre * jnp.exp(-0.5 * hidden_pre * hidden_pre) * 0.3989422804014327
    hidden_act, slope, d_out_all, end_far = stage(hidden_act, slope.astype(BF), d_out_all, end_far)
    fc2_grad = mm("fd,fh->dh", d_out_all, hidden_act).astype(BF)
    fc2_parts, fc2_ops = scatter_operands(fc2_grad, at)

    ff_part, ff_near, end_far, d_out_all, fc2_ops = stage(
        ff_part, ff_near, end_far, d_out_all, fc2_ops
    )
    fc2_far = scatter_low_across(fc2_ops)
    end_full = all_rows([ff_part, *ff_near, *end_far], hidden_n, hidden_n, at)
    d_pre, fc1_bias_grad = act_back(d_out_all, end_full, slope)
    d_two = mm("fh,dh->fd", d_pre, mid_full).astype(BF)

    d_two, fc2_far, d_pre = stage(d_two, fc2_far, d_pre)
    fc2_near = scatter_low_near(near_operands(fc2_parts, fc2_far))
    d_two_other = swap_pieces(d_two, PIECES)
    fc1_grad = mm("fd,fh->dh", normed_two_all, d_pre).astype(BF)
    d_branch_all, d_hidden, mid_sums = mid_norm_back(
        d_two, d_two_other, hidden_all, d_out_all, vectors
    )
    d_attended = mm("fd,de->fe", d_branch_all, out_full).astype(BF)
    out_grad = mm("fd,fe->de", d_branch_all, attended).astype(BF)
    mid_parts, mid_ops = scatter_operands(jnp.concatenate([fc1_grad, out_grad], axis=1), at)

    d_attended, mid_ops = stage(d_attended, mid_ops)
    mid_far = scatter_low_across(mid_ops)
    d_proj = attend_back(qkv, log_sums, d_attended, 0, pairs - 1)

    d_proj, mid_far, fc2_near = stage(d_proj, mid_far, fc2_near)
    mid_near = scatter_low_near(near_operands(mid_parts, mid_far))
    fc2_sum = scatter_high_step(high_operands(total_of(fc2_near), 0, at), 0)
    d_qkv, d_sums = attend_back(qkv, log_sums, d_attended, pairs - 1, 1, d_proj)
    qkv_grad = mm("fd,fe->de", normed_all, d_qkv).astype(BF)
    qkv_parts, qkv_ops = scatter_operands(qkv_grad, at)

    qkv_ops, d_qkv, fc2_sum, hidden_act = stage(qkv_ops, d_qkv, fc2_sum, hidden_act)
    qkv_far = scatter_low_across(qkv_ops)
    d_other = mm("fe,de->fd", d_qkv[half:], first_full[:, : 3 * wide]).astype(BF)
    mlp_other = mm("fh,dh->fd", hidden_act[half:], end_full).astype(BF)
    mlp_mine = mm("fh,dh->fd", hidden_act[:half], end_full)

    fc2_last = scatter_high_last(fc2_sum, 1, at)

    qkv_far, mid_near, d_other, mlp_other, mlp_mine, fc2_last = stage(
        qkv_far, mid_near, d_other, mlp_other, mlp_mine, fc2_last
    )
    qkv_near = scatter_low_near(near_operands(qkv_parts, qkv_far))
    mid_sum = scatter_high_step(high_operands(total_of(mid_near), 0, at), 0)
    d_other_got = swap_pieces(d_other, 2)
    input_grad, first_sums = first_norm_back(
        d_qkv, first_full, d_other_got, inputs, d_hidden, vectors
    )
    rows = jnp.concatenate([first_sums, mid_sums], axis=0)
    rows = rows + swap_core(rows)

    mid_sum, qkv_near, rows = stage(mid_sum, qkv_near, rows)
    width = rows.shape[1]
    flat = [rows, jnp.pad(d_sums[:, 0], ((0, 0), (0, width - 3 * PAIR)))]
    flat += [fc1_bias_grad[:, i : i + width] for i in range(0, fc1_bias_grad.shape[1], width)]
    flat = sum_over(jnp.concatenate(flat, axis=0), [1, 2])
    qkv_sum = scatter_high_step(high_operands(total_of(qkv_near), 0, at), 0)
    mlp_got = swap_core(mlp_other)
    mid_last = scatter_high_last(mid_sum, 1, at)

    qkv_sum, flat, mlp_got = stage(qkv_sum, flat, mlp_got)
    outputs = hidden_all[:half] + ((mlp_mine + mlp_got.astype(F32)) + vectors[5:6])
    flat = sum_over(flat, high[:0:-1])
    gains_out, shifts_out, qv_out, bias_out = finish_sums(
        flat,
        swap_dp(flat, high[0]),
        at["start"],
        [norm_gains.shape, shifts.shape, qv_bias.shape, (flat.shape[0] - 6 - pairs, width)],
    )
    (qkv_out,) = finish(
        finish_qkv_kernel, *scatter_high_last(qkv_sum, 1, at), [qkv_weight.shape], "finish_qkv"
    )
    (fc2_out,) = finish(finish_ff_kernel, *fc2_last, [(own, hidden_n)], "finish_fc2")
    fc1_out, out_out = finish(
        finish_ff_kernel, *mid_last, [(own, n) for n in (hidden_n, wide)], "finish_mid"
    )
    return (
        outputs[None],
        input_grad[None],
        qkv_out,
        out_out.T,
        fc1_out,
        fc2_out.T,
        gains_out,
        shifts_out,
        qv_out,
        bias_out.reshape(-1),
    )


def solution(mesh):
    specs = (
        P("dp", "tensor", None),
        P("dp", "tensor", None),
        P(None, "dp", "tensor"),
        P("tensor", "dp"),
        P("dp", "tensor"),
        P("tensor", "dp"),
        P(None, "dp"),
        P(None, "dp"),
        P(None, "tensor"),
        P("tensor"),
    )
    return jax.shard_map(body, mesh=mesh, in_specs=specs, out_specs=specs, check_vma=False)
```

profile of v0, /device:TPU:0, one launch (start us, length us, event | category | flops | bytes accessed | tf_op | source)
XLA Modules:
  0.0 205.7 jit_solution(15003076628468293819)
XLA Ops:
  0.7 0.8 fusion.38
  1.6 0.9 copy-done.2
  2.5 0.8 copy-done.3
  4.7 5.1 %collective-permute-start = (bf16[1,48,1664]{2,1,0:T(8,128)(2,1)S(1)}, bf16[1,48,1664]{2,1,0:T(8,128)(2,1)S(1)}, u32[]{:S(2)}, u32[]{:S(2)}) collective-permute-start(bf16[1,48,1664]{2,1,0:T(8,128)(2,1)S(1)} %bitcast.187), channel_id=1, source_target_pairs={{0,24},{2,26},{4,28},{6,30},{8,16},{10,18},{12,20},{14,22},{16,8},... | collective-permute-start | bytes 479240 | tf_op jit(solution)/shard_map/ppermute | solution.py:43
  10.5 1.0 maximum_bitcast_fusion.2
  11.5 3.4 %collective-permute-done = bf16[1,48,1664]{2,1,0:T(8,128)(2,1)S(1)} collective-permute-done((bf16[1,48,1664]{2,1,0:T(8,128)(2,1)S(1)}, bf16[1,48,1664]{2,1,0:T(8,128)(2,1)S(1)}, u32[]{:S(2)}, u32[]{:S(2)}) %collective-permute-start) | collective-permute-done | bytes 159776 | tf_op jit(solution)/shard_map/ppermute | solution.py:43
  14.9 8.5 %collective-permute-done.1 = bf16[1,48,1664]{2,1,0:T(8,128)(2,1)S(1)} collective-permute-done((bf16[1,48,1664]{2,1,0:T(8,128)(2,1)S(1)}, bf16[1,48,1664]{2,1,0:T(8,128)(2,1)S(1)}, u32[]{:S(2)}, u32[]{:S(2)}) %collective-permute-start.1) | collective-permute-done | bytes 159776 | tf_op jit(solution)/shard_map/ppermute | solution.py:43
  23.6 1.6 collective-permute-start.4
  25.2 1.5 collective-permute-start.5
  26.8 11.7 %collective-permute-done.6 = bf16[1,48,3072]{2,1,0:T(8,128)(2,1)S(1)} collective-permute-done((bf16[1,48,3072]{2,1,0:T(8,128)(2,1)S(1)}, bf16[1,48,3072]{2,1,0:T(8,128)(2,1)S(1)}, u32[]{:S(2)}, u32[]{:S(2)}) %collective-permute-start.6) | collective-permute-done | bytes 294944 | tf_op jit(solution)/shard_map/ppermute | solution.py:43
  39.1 1.2 collective-permute-done.5.refs_2_
  40.4 2.5 %collective-permute-start.9 = (bf16[2,48,3072]{2,1,0:T(8,128)(2,1)S(1)}, bf16[2,48,3072]{2,1,0:T(8,128)(2,1)S(1)}, u32[]{:S(2)}, u32[]{:S(2)}) collective-permute-start(bf16[2,48,3072]{2,1,0:T(8,128)(2,1)S(1)} %maximum_bitcast_fusion.1), channel_id=1, source_target_pairs={{0,8},{2,10},{4,12},{6,14},{8,0},{10,2},{12,4},{14,6},{16,24},{18,... | collective-permute-start | bytes 1769480 | tf_op jit(solution)/shard_map/ppermute | solution.py:43
  42.9 1.6 collective-permute-start.7
  45.1 8.9 %collective-permute-done.9 = bf16[2,48,3072]{2,1,0:T(8,128)(2,1)S(1)} collective-permute-done((bf16[2,48,3072]{2,1,0:T(8,128)(2,1)S(1)}, bf16[2,48,3072]{2,1,0:T(8,128)(2,1)S(1)}, u32[]{:S(2)}, u32[]{:S(2)}) %collective-permute-start.9) | collective-permute-done | bytes 589856 | tf_op jit(solution)/shard_map/ppermute | solution.py:43
  54.3 1.6 collective-permute-start.12
  55.9 1.5 collective-permute-start.13
  57.6 2.8 %project.1 = (bf16[1024,768]{1,0:T(8,128)(2,1)S(1)}, bf16[1024,1152]{1,0:T(8,128)(2,1)S(1)}, f32[8,768]{1,0:T(8,128)S(1)}) custom-call(bf16[1024,768]{1,0:T(8,128)(2,1)S(1)} %join.2.x_ref, bf16[768,1664]{1,0:T(8,128)(2,1)S(1)} %bitcast.168, f32[1,1152]{1,0:T(1,128)S(1)} %reshape.219.bias_ref), custom_call_target="tpu_custom_call" | custom-call | tf_op jit(solution)/shard_map/project/pallas_call | solution.py:445
  60.4 10.7 %attend.1 = (bf16[1024,384]{1,0:T(8,128)(2,1)S(1)}, f32[3,2,1024]{2,1,0:T(2,128)S(1)}) custom-call(bf16[1024,1152]{1,0:T(8,128)(2,1)S(1)} %get-tuple-element.142.qkv_ref), custom_call_target="tpu_custom_call" | custom-call | tf_op jit(solution)/shard_map/attend/pallas_call | solution.py:227
  71.1 1.0 convolution_convert_fusion.3.mine_ref
  72.9 1.7 collective-permute-done.10.refs_0_
  74.6 1.1 collective-permute-done.11.refs_1_
  75.7 1.6 mid_norm.1
  77.4 2.6 %collective-permute-done.12.refs_1_ = bf16[4,48,3072]{2,1,0:T(8,128)(2,1)S(1)} collective-permute-done((bf16[4,48,3072]{2,1,0:T(8,128)(2,1)S(1)}, bf16[4,48,3072]{2,1,0:T(8,128)(2,1)S(1)}, u32[]{:S(2)}, u32[]{:S(2)}) %collective-permute-start.12) | collective-permute-done | bytes 1179680 | tf_op jit(solution)/shard_map/ppermute | solution.py:43
  80.0 1.9 collective-permute-done.13.refs_2_
  82.0 1.6 collective-permute-start.15
  83.9 5.6 %collective-permute-done.15.refs_3_ = bf16[2,48,1536]{2,1,0:T(8,128)(2,1)S(1)} collective-permute-done((bf16[2,48,1536]{2,1,0:T(8,128)(2,1)S(1)}, bf16[2,48,1536]{2,1,0:T(8,128)(2,1)S(1)}, u32[]{:S(2)}, u32[]{:S(2)}) %collective-permute-start.15) | collective-permute-done | bytes 294944 | tf_op jit(solution)/shard_map/ppermute | solution.py:43
  89.5 2.7 %collective-permute-done.16.refs_4_ = bf16[2,48,1536]{2,1,0:T(8,128)(2,1)S(1)} collective-permute-done((bf16[2,48,1536]{2,1,0:T(8,128)(2,1)S(1)}, bf16[2,48,1536]{2,1,0:T(8,128)(2,1)S(1)}, u32[]{:S(2)}, u32[]{:S(2)}) %collective-permute-start.16) | collective-permute-done | bytes 294944 | tf_op jit(solution)/shard_map/ppermute | solution.py:43
  92.6 6.0 %fusion.4 = (bf16[1024,1536]{1,0:T(8,128)(2,1)S(1)}, bf16[1024,1536]{1,0:T(8,128)(2,1)S(1)}) fusion(f32[1536]{0:T(1024)S(1)} %convert_element_type.207, bf16[1024,768]{1,0:T(8,128)(2,1)S(1)} %get-tuple-element.158, bf16[768,1536]{1,0:T(8,128)(2,1)S(1)} %bitcast.183), kind=kOutput, calls=%fused_computation.5 | convolution fusion | flops 2434793472 | bytes 10229760 | tf_op jit(solution)/shard_map/fd,dh->fh/dot_general | solution.py:563
  99.1 2.9 %convolution_convert_fusion.1 = bf16[768,1536]{1,0:T(8,128)(2,1)S(1)} fusion(bf16[1024,768]{1,0:T(8,128)(2,1)S(1)} %join.3.d_out_ref, bf16[1024,1536]{1,0:T(8,128)(2,1)S(1)} %get-tuple-element.203), kind=kOutput, calls=%fused_computation.9 | convolution fusion | flops 2417098752 | bytes 7077888 | tf_op jit(solution)/shard_map/fd,fh->dh/dot_general | solution.py:563
  102.2 1.6 collective-permute-start.19
  103.8 2.0 collective-permute-start.20
  105.9 4.0 %act_back.1 = (bf16[1024,1536]{1,0:T(8,128)(2,1)S(1)}, f32[1,1536]{1,0:T(1,128)S(1)}) custom-call(bf16[1024,768]{1,0:T(8,128)(2,1)S(1)} %join.3.d_out_ref, bf16[768,1536]{1,0:T(8,128)(2,1)S(1)} %bitcast.177, bf16[1024,1536]{1,0:T(8,128)(2,1)S(1)} %get-tuple-element.173.slope_ref), custom_call_target="tpu_custom_call" | custom-call | tf_op jit(solution)/shard_map/act_back/pallas_call | solution.py:487
  110.0 2.6 %convolution_convert_fusion.4.mine_ref = bf16[1024,768]{1,0:T(8,128)(2,1)S(1)} fusion(bf16[1024,1536]{1,0:T(8,128)(2,1)S(1)} %get-tuple-element.179, bf16[768,1536]{1,0:T(8,128)(2,1)S(1)} %bitcast.184), kind=kOutput, calls=%fused_computation.15 | convolution fusion | flops 2416705536 | bytes 7077888 | tf_op jit(solution)/shard_map/fh,dh->fd/dot_general | solution.py:563
  113.6 2.0 collective-permute-start.25
  115.7 3.2 %convolution_convert_fusion = bf16[768,1536]{1,0:T(8,128)(2,1)S(1)} fusion(bf16[1024,768]{1,0:T(8,128)(2,1)S(1)} %get-tuple-element.158, bf16[1024,1536]{1,0:T(8,128)(2,1)S(1)} %get-tuple-element.179), kind=kOutput, calls=%fused_computation.8 | convolution fusion | flops 2417098752 | bytes 7077888 | tf_op jit(solution)/shard_map/fd,fh->dh/dot_general | solution.py:563
  118.9 2.7 %mid_norm_back.1 = (bf16[1024,768]{1,0:T(8,128)(2,1)S(1)}, f32[512,768]{1,0:T(8,128)S(1)}, f32[4,768]{1,0:T(4,128)S(1)}) custom-call(bf16[1024,768]{1,0:T(8,128)(2,1)S(1)} %convolution_convert_fusion.4.mine_ref, f32[1024,768]{1,0:T(8,128)S(1)} %get-tuple-element.145.hidden_ref, bf16[1024,768]{1,0:T(8,128)(2,1)S(1)} %join.3.d_out_ref, ...), custom_call_target="tpu_custom_call" | custom-call | tf_op jit(solution)/shard_map/mid_norm_back/pallas_call | solution.py:532
  121.5 1.0 convolution_convert_fusion.5.grad_ref
  122.5 1.0 convolution_convert_fusion.6
  124.0 2.0 collective-permute-start.24
  126.0 12.7 %attend_back.2 = (bf16[1024,1152]{1,0:T(8,128)(2,1)S(1)}, f32[3,1,384]{2,1,0:T(1,128)S(1)}) custom-call(bf16[1024,1152]{1,0:T(8,128)(2,1)S(1)} %get-tuple-element.142.qkv_ref, f32[3,2,1024]{2,1,0:T(2,128)S(1)} %get-tuple-element.147.lse_ref, bf16[1024,384]{1,0:T(8,128)(2,1)S(1)} %convolution_convert_fusion.5.grad_ref), custom_call_target="tpu_custom_call" | custom-call | tf_op jit(solution)/shard_map/attend_back/pallas_call | solution.py:281
  139.2 2.3 %collective-permute-start.27 = (bf16[2,48,1536]{2,1,0:T(8,128)(2,1)S(1)}, bf16[2,48,1536]{2,1,0:T(8,128)(2,1)S(1)}, u32[]{:S(2)}, u32[]{:S(2)}) collective-permute-start(bf16[2,48,1536]{2,1,0:T(8,128)(2,1)S(1)} %fusion.27), channel_id=1, source_target_pairs={{0,8},{2,10},{4,12},{6,14},{8,0},{10,2},{12,4},{14,6},{16,24},{18,... | collective-permute-start | bytes 884744 | tf_op jit(solution)/shard_map/ppermute | solution.py:43
  141.7 2.0 collective-permute-start.30
  143.9 6.1 %attend_back.3 = (bf16[1024,1152]{1,0:T(8,128)(2,1)S(1)}, f32[3,1,384]{2,1,0:T(1,128)S(1)}) custom-call(bf16[1024,1152]{1,0:T(8,128)(2,1)S(1)} %get-tuple-element.142.qkv_ref, f32[3,2,1024]{2,1,0:T(2,128)S(1)} %get-tuple-element.147.lse_ref, bf16[1024,384]{1,0:T(8,128)(2,1)S(1)} %convolution_convert_fusion.5.grad_ref, ...), custom_call_target="tpu_custom_call", output_to_operand_aliasing={{0}: (3, {}), {1}: (4, {})} | custom-call | tf_op jit(solution)/shard_map/attend_back/pallas_call | solution.py:281
  150.0 2.2 %convolution_convert_fusion.2 = bf16[768,1152]{1,0:T(8,128)(2,1)S(1)} fusion(bf16[1024,768]{1,0:T(8,128)(2,1)S(1)} %get-tuple-element.146, bf16[1024,1152]{1,0:T(8,128)(2,1)S(1)} %get-tuple-element.202.qkv_ref), kind=kOutput, calls=%fused_computation.10 | convolution fusion | flops 1812824064 | bytes 5701632 | tf_op jit(solution)/shard_map/fd,fe->de/dot_general | solution.py:563
  152.7 2.0 collective-permute-start.29
  154.7 1.2 fusion.14
  155.9 1.4 fusion.11
  158.1 1.4 fusion.7
  159.5 5.3 %collective-permute-done.32 = bf16[1,48,1536]{2,1,0:T(8,128)(2,1)S(1)} collective-permute-done((bf16[1,48,1536]{2,1,0:T(8,128)(2,1)S(1)}, bf16[1,48,1536]{2,1,0:T(8,128)(2,1)S(1)}, u32[]{:S(2)}, u32[]{:S(2)}) %collective-permute-start.32) | collective-permute-done | bytes 147488 | tf_op jit(solution)/shard_map/ppermute | solution.py:43
  166.9 1.1 collective-permute-start.34
  169.1 3.1 %first_norm_back.1 = (f32[512,768]{1,0:T(8,128)}, f32[2,768]{1,0:T(2,128)S(1)}) custom-call(bf16[1024,1152]{1,0:T(8,128)(2,1)S(1)} %get-tuple-element.202.qkv_ref, bf16[768,1664]{1,0:T(8,128)(2,1)S(1)} %bitcast.172, bf16[512,768]{1,0:T(8,128)(2,1)S(1)} %bitcast.182, f32[512,768]{1,0:T(8,128)S(1)} %get-tuple-element.213.d_hidden_ref, ...), custom_call_target="tpu_custom_call" | custom-call | tf_op jit(solution)/shard_map/first_norm_back/pallas_call | solution.py:557
  172.8 1.6 collective-permute-done.33
  174.5 4.8 %collective-permute-done.34 = bf16[4,48,1152]{2,1,0:T(8,128)(2,1)S(1)} collective-permute-done((bf16[4,48,1152]{2,1,0:T(8,128)(2,1)S(1)}, bf16[4,48,1152]{2,1,0:T(8,128)(2,1)S(1)}, u32[]{:S(2)}, u32[]{:S(2)}) %collective-permute-start.34) | collective-permute-done | bytes 442400 | tf_op jit(solution)/shard_map/ppermute | solution.py:43
  180.1 2.1 %collective-permute-start.39 = (bf16[2,48,1152]{2,1,0:T(8,128)(2,1)S(1)}, bf16[2,48,1152]{2,1,0:T(8,128)(2,1)S(1)}, u32[]{:S(2)}, u32[]{:S(2)}) collective-permute-start(bf16[2,48,1152]{2,1,0:T(8,128)(2,1)S(1)} %fusion.28), channel_id=1, source_target_pairs={{0,8},{2,10},{4,12},{6,14},{8,0},{10,2},{12,4},{14,6},{16,24},{18,... | collective-permute-start | bytes 663560 | tf_op jit(solution)/shard_map/ppermute | solution.py:43
  182.2 1.0 collective-permute-start.40
  184.0 2.4 %collective-permute-done.40 = f32[11,768]{1,0:T(8,128)S(1)} collective-permute-done((f32[11,768]{1,0:T(8,128)S(1)}, f32[11,768]{1,0:T(8,128)S(1)}, u32[]{:S(2)}, u32[]{:S(2)}) %collective-permute-start.40) | collective-permute-done | bytes 33824 | tf_op jit(solution)/shard_map/ppermute | solution.py:43
  186.8 3.7 %collective-permute-done.41 = f32[11,768]{1,0:T(8,128)S(1)} collective-permute-done((f32[11,768]{1,0:T(8,128)S(1)}, f32[11,768]{1,0:T(8,128)S(1)}, u32[]{:S(2)}, u32[]{:S(2)}) %collective-permute-start.41) | collective-permute-done | bytes 33824 | tf_op jit(solution)/shard_map/ppermute | solution.py:43
  190.6 2.5 %collective-permute-done.44 = bf16[1,48,1920]{2,1,0:T(8,128)(2,1)S(1)} collective-permute-done((bf16[1,48,1920]{2,1,0:T(8,128)(2,1)S(1)}, bf16[1,48,1920]{2,1,0:T(8,128)(2,1)S(1)}, u32[]{:S(2)}, u32[]{:S(2)}) %collective-permute-start.44) | collective-permute-done | bytes 184352 | tf_op jit(solution)/shard_map/ppermute | solution.py:43
  193.1 0.8 finish_mid.1
  194.3 1.8 collective-permute-start.45
  196.1 1.4 add_bitcast_fusion
  197.6 0.9 collective-permute-done.45
  198.4 2.6 %collective-permute-start.46 = (f32[11,768]{1,0:T(8,128)S(1)}, f32[11,768]{1,0:T(8,128)S(1)}, u32[]{:S(2)}, u32[]{:S(2)}) collective-permute-start(f32[11,768]{1,0:T(8,128)S(1)} %add.120.kept_ref), channel_id=1, source_target_pairs={{0,16},{2,18},{4,20},{6,22},{8,24},{10,26},{12,28},{14,30},{16,0},... | collective-permute-start | bytes 101384 | tf_op jit(solution)/shard_map/ppermute | solution.py:43
  201.1 2.4 %collective-permute-done.46.got_ref = f32[11,768]{1,0:T(8,128)S(1)} collective-permute-done((f32[11,768]{1,0:T(8,128)S(1)}, f32[11,768]{1,0:T(8,128)S(1)}, u32[]{:S(2)}, u32[]{:S(2)}) %collective-permute-start.46) | collective-permute-done | bytes 33824 | tf_op jit(solution)/shard_map/ppermute | solution.py:43
  (141 shorter events, 18.5 us)
Async XLA Ops:
  0.6 26.1 %copy-start = (bf16[1,512,768]{2,1,0:T(8,128)(2,1)S(1)}, bf16[1,512,768]{2,1,0:T(8,128)(2,1)}, u32[]{:S(2)}) copy-start(bf16[1,512,768]{2,1,0:T(8,128)(2,1)} %param.10) | copy-start | bytes 2359300
  1.6 0.9 copy-start.2
  2.5 0.8 copy-start.3
  3.3 0.7 copy-start.4
  4.0 0.7 copy-start.5
  4.7 10.1 %collective-permute-start = (bf16[1,48,1664]{2,1,0:T(8,128)(2,1)S(1)}, bf16[1,48,1664]{2,1,0:T(8,128)(2,1)S(1)}, u32[]{:S(2)}, u32[]{:S(2)}) collective-permute-start(bf16[1,48,1664]{2,1,0:T(8,128)(2,1)S(1)} %bitcast.187), channel_id=1, source_target_pairs={{0,24},{2,26},{4,28},{6,30},{8,16},{10,18},{12,20},{14,22},{16,8},... | collective-permute-start | bytes 479240 | tf_op jit(solution)/shard_map/ppermute | solution.py:43
  9.8 13.5 %collective-permute-start.1 = (bf16[1,48,1664]{2,1,0:T(8,128)(2,1)S(1)}, bf16[1,48,1664]{2,1,0:T(8,128)(2,1)S(1)}, u32[]{:S(2)}, u32[]{:S(2)}) collective-permute-start(bf16[1,48,1664]{2,1,0:T(8,128)(2,1)S(1)} %bitcast.188), channel_id=1, source_target_pairs={{0,16},{2,18},{4,20},{6,22},{8,24},{10,26},{12,28},{14,30},{16,0},... | collective-permute-start | bytes 479240 | tf_op jit(solution)/shard_map/ppermute | solution.py:43
  9.8 13.5 %collective-permute-start.2 = (bf16[1,48,1664]{2,1,0:T(8,128)(2,1)S(1)}, bf16[1,48,1664]{2,1,0:T(8,128)(2,1)S(1)}, u32[]{:S(2)}, u32[]{:S(2)}) collective-permute-start(bf16[1,48,1664]{2,1,0:T(8,128)(2,1)S(1)} %bitcast.189), channel_id=1, source_target_pairs={{0,8},{2,10},{4,12},{6,14},{8,0},{10,2},{12,4},{14,6},{16,24},{18,... | collective-permute-start | bytes 479240 | tf_op jit(solution)/shard_map/ppermute | solution.py:43
  10.5 13.1 %collective-permute-start.3 = (bf16[512,768]{1,0:T(8,128)(2,1)}, bf16[512,768]{1,0:T(8,128)(2,1)S(1)}, u32[]{:S(2)}, u32[]{:S(2)}) collective-permute-start(bf16[512,768]{1,0:T(8,128)(2,1)} %bitcast.180), channel_id=1, source_target_pairs={{0,1},{1,0},{2,3},{3,2},{4,5},{5,4},{6,7},{7,6},{8,9},{9,8},{10,11... | collective-permute-start | bytes 2359304 | tf_op jit(solution)/shard_map/ppermute | solution.py:47
  23.6 15.0 %collective-permute-start.6 = (bf16[1,48,3072]{2,1,0:T(8,128)(2,1)S(1)}, bf16[1,48,3072]{2,1,0:T(8,128)(2,1)S(1)}, u32[]{:S(2)}, u32[]{:S(2)}) collective-permute-start(bf16[1,48,3072]{2,1,0:T(8,128)(2,1)S(1)} %maximum_bitcast_fusion.2), channel_id=1, source_target_pairs={{0,16},{2,18},{4,20},{6,22},{8,24},{10,26},{12,28},{14,30},{16,0},... | collective-permute-start | bytes 884744 | tf_op jit(solution)/shard_map/ppermute | solution.py:43
  23.6 15.5 %collective-permute-start.4 = (bf16[4,48,1664]{2,1,0:T(8,128)(2,1)S(1)}, bf16[4,48,1664]{2,1,0:T(8,128)(2,1)S(1)}, u32[]{:S(2)}, u32[]{:S(2)}) collective-permute-start(bf16[4,48,1664]{2,1,0:T(8,128)(2,1)S(1)} %maximum_bitcast_fusion.refs_0_), channel_id=1, source_target_pairs={{0,2},{2,0},{4,6},{6,4},{8,10},{10,8},{12,14},{14,12},{16,18},{18,... | collective-permute-start | bytes 1916936 | tf_op jit(solution)/shard_map/ppermute | solution.py:43
  25.2 15.2 %collective-permute-start.5 = (bf16[4,48,1664]{2,1,0:T(8,128)(2,1)S(1)}, bf16[4,48,1664]{2,1,0:T(8,128)(2,1)S(1)}, u32[]{:S(2)}, u32[]{:S(2)}) collective-permute-start(bf16[4,48,1664]{2,1,0:T(8,128)(2,1)S(1)} %maximum_bitcast_fusion.refs_0_), channel_id=1, source_target_pairs={{0,4},{2,6},{4,0},{6,2},{8,12},{10,14},{12,8},{14,10},{16,20},{18,... | collective-permute-start | bytes 1916936 | tf_op jit(solution)/shard_map/ppermute | solution.py:43
  40.4 13.7 %collective-permute-start.9 = (bf16[2,48,3072]{2,1,0:T(8,128)(2,1)S(1)}, bf16[2,48,3072]{2,1,0:T(8,128)(2,1)S(1)}, u32[]{:S(2)}, u32[]{:S(2)}) collective-permute-start(bf16[2,48,3072]{2,1,0:T(8,128)(2,1)S(1)} %maximum_bitcast_fusion.1), channel_id=1, source_target_pairs={{0,8},{2,10},{4,12},{6,14},{8,0},{10,2},{12,4},{14,6},{16,24},{18,... | collective-permute-start | bytes 1769480 | tf_op jit(solution)/shard_map/ppermute | solution.py:43
  42.9 11.4 %collective-permute-start.7 = (bf16[2,48,1664]{2,1,0:T(8,128)(2,1)S(1)}, bf16[2,48,1664]{2,1,0:T(8,128)(2,1)S(1)}, u32[]{:S(2)}, u32[]{:S(2)}) collective-permute-start(bf16[2,48,1664]{2,1,0:T(8,128)(2,1)S(1)} %slice.79), channel_id=1, source_target_pairs={{0,4},{2,6},{4,0},{6,2},{8,12},{10,14},{12,8},{14,10},{16,20},{18,... | collective-permute-start | bytes 958472 | tf_op jit(solution)/shard_map/ppermute | solution.py:43
  44.5 9.8 %collective-permute-start.8 = (bf16[2,48,1664]{2,1,0:T(8,128)(2,1)S(1)}, bf16[2,48,1664]{2,1,0:T(8,128)(2,1)S(1)}, u32[]{:S(2)}, u32[]{:S(2)}) collective-permute-start(bf16[2,48,1664]{2,1,0:T(8,128)(2,1)S(1)} %slice.80), channel_id=1, source_target_pairs={{0,2},{2,0},{4,6},{6,4},{8,10},{10,8},{12,14},{14,12},{16,18},{18,... | collective-permute-start | bytes 958472 | tf_op jit(solution)/shard_map/ppermute | solution.py:43
  54.3 25.7 %collective-permute-start.12 = (bf16[4,48,3072]{2,1,0:T(8,128)(2,1)S(1)}, bf16[4,48,3072]{2,1,0:T(8,128)(2,1)S(1)}, u32[]{:S(2)}, u32[]{:S(2)}) collective-permute-start(bf16[4,48,3072]{2,1,0:T(8,128)(2,1)S(1)} %bitcast.173), channel_id=1, source_target_pairs={{0,2},{2,0},{4,6},{6,4},{8,10},{10,8},{12,14},{14,12},{16,18},{18,... | collective-permute-start | bytes 3538952 | tf_op jit(solution)/shard_map/ppermute | solution.py:43
  55.9 26.0 %collective-permute-start.13 = (bf16[4,48,3072]{2,1,0:T(8,128)(2,1)S(1)}, bf16[4,48,3072]{2,1,0:T(8,128)(2,1)S(1)}, u32[]{:S(2)}, u32[]{:S(2)}) collective-permute-start(bf16[4,48,3072]{2,1,0:T(8,128)(2,1)S(1)} %bitcast.174), channel_id=1, source_target_pairs={{0,4},{2,6},{4,0},{6,2},{8,12},{10,14},{12,8},{14,10},{16,20},{18,... | collective-permute-start | bytes 3538952 | tf_op jit(solution)/shard_map/ppermute | solution.py:43
  71.1 1.7 copy-start.1
  72.3 2.4 %collective-permute-start.10 = (bf16[512,768]{1,0:T(8,128)(2,1)S(1)}, bf16[512,768]{1,0:T(8,128)(2,1)S(1)}, u32[]{:S(2)}, u32[]{:S(2)}) collective-permute-start(bf16[512,768]{1,0:T(8,128)(2,1)S(1)} %get-tuple-element.261), channel_id=1, source_target_pairs={{0,1},{1,0},{2,3},{3,2},{4,5},{5,4},{6,7},{7,6},{8,9},{9,8},{10,11... | collective-permute-start | bytes 2359304 | tf_op jit(solution)/shard_map/ppermute | solution.py:47
  72.3 3.4 %collective-permute-start.11 = (bf16[512,768]{1,0:T(8,128)(2,1)S(1)}, bf16[512,768]{1,0:T(8,128)(2,1)S(1)}, u32[]{:S(2)}, u32[]{:S(2)}) collective-permute-start(bf16[512,768]{1,0:T(8,128)(2,1)S(1)} %get-tuple-element.260), channel_id=1, source_target_pairs={{0,1},{1,0},{2,3},{3,2},{4,5},{5,4},{6,7},{7,6},{8,9},{9,8},{10,11... | collective-permute-start | bytes 2359304 | tf_op jit(solution)/shard_map/ppermute | solution.py:47
  72.8 4.5 %collective-permute-start.14 = (bf16[512,768]{1,0:T(8,128)(2,1)S(1)}, bf16[512,768]{1,0:T(8,128)(2,1)S(1)}, u32[]{:S(2)}, u32[]{:S(2)}) collective-permute-start(bf16[512,768]{1,0:T(8,128)(2,1)S(1)} %bitcast.185), channel_id=1, source_target_pairs={{0,1},{1,0},{2,3},{3,2},{4,5},{5,4},{6,7},{7,6},{8,9},{9,8},{10,11... | collective-permute-start | bytes 2359304 | tf_op jit(solution)/shard_map/ppermute | solution.py:47
  75.7 8.1 %copy-start.6 = (bf16[1536]{0:T(1024)(128)(2,1)S(1)}, bf16[1536]{0:T(1024)(128)(2,1)}, u32[]{:S(2)}) copy-start(bf16[1536]{0:T(1024)(128)(2,1)} %param.19) | copy-start | bytes 9220
  82.0 7.5 %collective-permute-start.15 = (bf16[2,48,1536]{2,1,0:T(8,128)(2,1)S(1)}, bf16[2,48,1536]{2,1,0:T(8,128)(2,1)S(1)}, u32[]{:S(2)}, u32[]{:S(2)}) collective-permute-start(bf16[2,48,1536]{2,1,0:T(8,128)(2,1)S(1)} %slice.85), channel_id=1, source_target_pairs={{0,4},{2,6},{4,0},{6,2},{8,12},{10,14},{12,8},{14,10},{16,20},{18,... | collective-permute-start | bytes 884744 | tf_op jit(solution)/shard_map/ppermute | solution.py:43
  83.6 8.6 %collective-permute-start.16 = (bf16[2,48,1536]{2,1,0:T(8,128)(2,1)S(1)}, bf16[2,48,1536]{2,1,0:T(8,128)(2,1)S(1)}, u32[]{:S(2)}, u32[]{:S(2)}) collective-permute-start(bf16[2,48,1536]{2,1,0:T(8,128)(2,1)S(1)} %slice.86), channel_id=1, source_target_pairs={{0,2},{2,0},{4,6},{6,4},{8,10},{10,8},{12,14},{14,12},{16,18},{18,... | collective-permute-start | bytes 884744 | tf_op jit(solution)/shard_map/ppermute | solution.py:43
  92.2 6.8 %collective-permute-start.17 = (bf16[2,48,1536]{2,1,0:T(8,128)(2,1)S(1)}, bf16[2,48,1536]{2,1,0:T(8,128)(2,1)S(1)}, u32[]{:S(2)}, u32[]{:S(2)}) collective-permute-start(bf16[2,48,1536]{2,1,0:T(8,128)(2,1)S(1)} %slice.87), channel_id=1, source_target_pairs={{0,4},{2,6},{4,0},{6,2},{8,12},{10,14},{12,8},{14,10},{16,20},{18,... | collective-permute-start | bytes 884744 | tf_op jit(solution)/shard_map/ppermute | solution.py:43
  92.3 6.8 %collective-permute-start.18 = (bf16[2,48,1536]{2,1,0:T(8,128)(2,1)S(1)}, bf16[2,48,1536]{2,1,0:T(8,128)(2,1)S(1)}, u32[]{:S(2)}, u32[]{:S(2)}) collective-permute-start(bf16[2,48,1536]{2,1,0:T(8,128)(2,1)S(1)} %slice.88), channel_id=1, source_target_pairs={{0,2},{2,0},{4,6},{6,4},{8,10},{10,8},{12,14},{14,12},{16,18},{18,... | collective-permute-start | bytes 884744 | tf_op jit(solution)/shard_map/ppermute | solution.py:43
  98.6 3.5 %copy-start.7 = (bf16[1024,1536]{1,0:T(8,128)(2,1)}, bf16[1024,1536]{1,0:T(8,128)(2,1)S(1)}, u32[]{:S(2)}) copy-start(bf16[1024,1536]{1,0:T(8,128)(2,1)S(1)} %get-tuple-element.203) | copy-start | bytes 9437188
  102.2 10.4 %collective-permute-start.19 = (bf16[2,48,1536]{2,1,0:T(8,128)(2,1)S(1)}, bf16[2,48,1536]{2,1,0:T(8,128)(2,1)S(1)}, u32[]{:S(2)}, u32[]{:S(2)}) collective-permute-start(bf16[2,48,1536]{2,1,0:T(8,128)(2,1)S(1)} %get-tuple-element.175), channel_id=1, source_target_pairs={{0,2},{2,0},{4,6},{6,4},{8,10},{10,8},{12,14},{14,12},{16,18},{18,... | collective-permute-start | bytes 884744 | tf_op jit(solution)/shard_map/ppermute | solution.py:43
  103.8 8.9 %collective-permute-start.20 = (bf16[2,48,1536]{2,1,0:T(8,128)(2,1)S(1)}, bf16[2,48,1536]{2,1,0:T(8,128)(2,1)S(1)}, u32[]{:S(2)}, u32[]{:S(2)}) collective-permute-start(bf16[2,48,1536]{2,1,0:T(8,128)(2,1)S(1)} %get-tuple-element.176), channel_id=1, source_target_pairs={{0,4},{2,6},{4,0},{6,2},{8,12},{10,14},{12,8},{14,10},{16,20},{18,... | collective-permute-start | bytes 884744 | tf_op jit(solution)/shard_map/ppermute | solution.py:43
  112.8 6.1 %collective-permute-start.21 = (bf16[512,768]{1,0:T(8,128)(2,1)S(1)}, bf16[512,768]{1,0:T(8,128)(2,1)S(1)}, u32[]{:S(2)}, u32[]{:S(2)}) collective-permute-start(bf16[512,768]{1,0:T(8,128)(2,1)S(1)} %get-tuple-element.259), channel_id=1, source_target_pairs={{0,1},{1,0},{2,3},{3,2},{4,5},{5,4},{6,7},{7,6},{8,9},{9,8},{10,11... | collective-permute-start | bytes 2359304 | tf_op jit(solution)/shard_map/ppermute | solution.py:47
  112.8 6.0 %collective-permute-start.22 = (bf16[512,768]{1,0:T(8,128)(2,1)S(1)}, bf16[512,768]{1,0:T(8,128)(2,1)S(1)}, u32[]{:S(2)}, u32[]{:S(2)}) collective-permute-start(bf16[512,768]{1,0:T(8,128)(2,1)S(1)} %get-tuple-element.258), channel_id=1, source_target_pairs={{0,1},{1,0},{2,3},{3,2},{4,5},{5,4},{6,7},{7,6},{8,9},{9,8},{10,11... | collective-permute-start | bytes 2359304 | tf_op jit(solution)/shard_map/ppermute | solution.py:47
  113.6 25.3 %collective-permute-start.25 = (bf16[4,48,1536]{2,1,0:T(8,128)(2,1)S(1)}, bf16[4,48,1536]{2,1,0:T(8,128)(2,1)S(1)}, u32[]{:S(2)}, u32[]{:S(2)}) collective-permute-start(bf16[4,48,1536]{2,1,0:T(8,128)(2,1)S(1)} %pad_maximum_fusion.4), channel_id=1, source_target_pairs={{0,2},{2,0},{4,6},{6,4},{8,10},{10,8},{12,14},{14,12},{16,18},{18,... | collective-permute-start | bytes 1769480 | tf_op jit(solution)/shard_map/ppermute | solution.py:43
  115.6 23.2 %collective-permute-start.26 = (bf16[4,48,1536]{2,1,0:T(8,128)(2,1)S(1)}, bf16[4,48,1536]{2,1,0:T(8,128)(2,1)S(1)}, u32[]{:S(2)}, u32[]{:S(2)}) collective-permute-start(bf16[4,48,1536]{2,1,0:T(8,128)(2,1)S(1)} %pad_maximum_fusion.5), channel_id=1, source_target_pairs={{0,4},{2,6},{4,0},{6,2},{8,12},{10,14},{12,8},{14,10},{16,20},{18,... | collective-permute-start | bytes 1769480 | tf_op jit(solution)/shard_map/ppermute | solution.py:43
  123.9 15.0 %collective-permute-start.23 = (bf16[2,48,1920]{2,1,0:T(8,128)(2,1)S(1)}, bf16[2,48,1920]{2,1,0:T(8,128)(2,1)S(1)}, u32[]{:S(2)}, u32[]{:S(2)}) collective-permute-start(bf16[2,48,1920]{2,1,0:T(8,128)(2,1)S(1)} %get-tuple-element.183), channel_id=1, source_target_pairs={{0,2},{2,0},{4,6},{6,4},{8,10},{10,8},{12,14},{14,12},{16,18},{18,... | collective-permute-start | bytes 1105928 | tf_op jit(solution)/shard_map/ppermute | solution.py:43
  124.0 14.8 %collective-permute-start.24 = (bf16[2,48,1920]{2,1,0:T(8,128)(2,1)S(1)}, bf16[2,48,1920]{2,1,0:T(8,128)(2,1)S(1)}, u32[]{:S(2)}, u32[]{:S(2)}) collective-permute-start(bf16[2,48,1920]{2,1,0:T(8,128)(2,1)S(1)} %get-tuple-element.184), channel_id=1, source_target_pairs={{0,4},{2,6},{4,0},{6,2},{8,12},{10,14},{12,8},{14,10},{16,20},{18,... | collective-permute-start | bytes 1105928 | tf_op jit(solution)/shard_map/ppermute | solution.py:43
  139.2 13.3 %collective-permute-start.27 = (bf16[2,48,1536]{2,1,0:T(8,128)(2,1)S(1)}, bf16[2,48,1536]{2,1,0:T(8,128)(2,1)S(1)}, u32[]{:S(2)}, u32[]{:S(2)}) collective-permute-start(bf16[2,48,1536]{2,1,0:T(8,128)(2,1)S(1)} %fusion.27), channel_id=1, source_target_pairs={{0,8},{2,10},{4,12},{6,14},{8,0},{10,2},{12,4},{14,6},{16,24},{18,... | collective-permute-start | bytes 884744 | tf_op jit(solution)/shard_map/ppermute | solution.py:43
  141.7 23.7 %collective-permute-start.30 = (bf16[4,48,1920]{2,1,0:T(8,128)(2,1)S(1)}, bf16[4,48,1920]{2,1,0:T(8,128)(2,1)S(1)}, u32[]{:S(2)}, u32[]{:S(2)}) collective-permute-start(bf16[4,48,1920]{2,1,0:T(8,128)(2,1)S(1)} %pad_maximum_fusion.2), channel_id=1, source_target_pairs={{0,2},{2,0},{4,6},{6,4},{8,10},{10,8},{12,14},{14,12},{16,18},{18,... | collective-permute-start | bytes 2211848 | tf_op jit(solution)/shard_map/ppermute | solution.py:43
  143.8 21.6 %collective-permute-start.31 = (bf16[4,48,1920]{2,1,0:T(8,128)(2,1)S(1)}, bf16[4,48,1920]{2,1,0:T(8,128)(2,1)S(1)}, u32[]{:S(2)}, u32[]{:S(2)}) collective-permute-start(bf16[4,48,1920]{2,1,0:T(8,128)(2,1)S(1)} %pad_maximum_fusion.3), channel_id=1, source_target_pairs={{0,4},{2,6},{4,0},{6,2},{8,12},{10,14},{12,8},{14,10},{16,20},{18,... | collective-permute-start | bytes 2211848 | tf_op jit(solution)/shard_map/ppermute | solution.py:43
  152.5 3.4 %copy-start.8 = (bf16[1024,1536]{1,0:T(8,128)(2,1)S(1)}, bf16[1024,1536]{1,0:T(8,128)(2,1)}, u32[]{:S(2)}) copy-start(bf16[1024,1536]{1,0:T(8,128)(2,1)} %copy-done.7) | copy-start | bytes 9437188
  152.5 12.3 %collective-permute-start.28 = (bf16[2,48,1152]{2,1,0:T(8,128)(2,1)S(1)}, bf16[2,48,1152]{2,1,0:T(8,128)(2,1)S(1)}, u32[]{:S(2)}, u32[]{:S(2)}) collective-permute-start(bf16[2,48,1152]{2,1,0:T(8,128)(2,1)S(1)} %get-tuple-element.198), channel_id=1, source_target_pairs={{0,2},{2,0},{4,6},{6,4},{8,10},{10,8},{12,14},{14,12},{16,18},{18,... | collective-permute-start | bytes 663560 | tf_op jit(solution)/shard_map/ppermute | solution.py:43
  152.7 12.7 %collective-permute-start.29 = (bf16[2,48,1152]{2,1,0:T(8,128)(2,1)S(1)}, bf16[2,48,1152]{2,1,0:T(8,128)(2,1)S(1)}, u32[]{:S(2)}, u32[]{:S(2)}) collective-permute-start(bf16[2,48,1152]{2,1,0:T(8,128)(2,1)S(1)} %get-tuple-element.199), channel_id=1, source_target_pairs={{0,4},{2,6},{4,0},{6,2},{8,12},{10,14},{12,8},{14,10},{16,20},{18,... | collective-permute-start | bytes 663560 | tf_op jit(solution)/shard_map/ppermute | solution.py:43
  157.4 7.5 %collective-permute-start.32 = (bf16[1,48,1536]{2,1,0:T(8,128)(2,1)S(1)}, bf16[1,48,1536]{2,1,0:T(8,128)(2,1)S(1)}, u32[]{:S(2)}, u32[]{:S(2)}) collective-permute-start(bf16[1,48,1536]{2,1,0:T(8,128)(2,1)S(1)} %dynamic-slice_convert_fusion.1), channel_id=1, source_target_pairs={{0,16},{2,18},{4,20},{6,22},{8,24},{10,26},{12,28},{14,30},{16,0},... | collective-permute-start | bytes 442376 | tf_op jit(solution)/shard_map/ppermute | solution.py:43
  165.7 8.7 %collective-permute-start.33 = (bf16[2,48,1920]{2,1,0:T(8,128)(2,1)S(1)}, bf16[2,48,1920]{2,1,0:T(8,128)(2,1)S(1)}, u32[]{:S(2)}, u32[]{:S(2)}) collective-permute-start(bf16[2,48,1920]{2,1,0:T(8,128)(2,1)S(1)} %fusion.26), channel_id=1, source_target_pairs={{0,8},{2,10},{4,12},{6,14},{8,0},{10,2},{12,4},{14,6},{16,24},{18,... | collective-permute-start | bytes 1105928 | tf_op jit(solution)/shard_map/ppermute | solution.py:43
  166.1 3.0 %collective-permute-start.36 = (bf16[256,768]{1,0:T(8,128)(2,1)S(1)}, bf16[256,768]{1,0:T(8,128)(2,1)S(1)}, u32[]{:S(2)}, u32[]{:S(2)}) collective-permute-start(bf16[256,768]{1,0:T(8,128)(2,1)S(1)} %get-tuple-element.265), channel_id=1, source_target_pairs={{0,1},{1,0},{2,3},{3,2},{4,5},{5,4},{6,7},{7,6},{8,9},{9,8},{10,11... | collective-permute-start | bytes 1179656 | tf_op jit(solution)/shard_map/ppermute | solution.py:47
  166.2 2.9 %collective-permute-start.37 = (bf16[256,768]{1,0:T(8,128)(2,1)S(1)}, bf16[256,768]{1,0:T(8,128)(2,1)S(1)}, u32[]{:S(2)}, u32[]{:S(2)}) collective-permute-start(bf16[256,768]{1,0:T(8,128)(2,1)S(1)} %get-tuple-element.264), channel_id=1, source_target_pairs={{0,1},{1,0},{2,3},{3,2},{4,5},{5,4},{6,7},{7,6},{8,9},{9,8},{10,11... | collective-permute-start | bytes 1179656 | tf_op jit(solution)/shard_map/ppermute | solution.py:47
  166.9 12.4 %collective-permute-start.34 = (bf16[4,48,1152]{2,1,0:T(8,128)(2,1)S(1)}, bf16[4,48,1152]{2,1,0:T(8,128)(2,1)S(1)}, u32[]{:S(2)}, u32[]{:S(2)}) collective-permute-start(bf16[4,48,1152]{2,1,0:T(8,128)(2,1)S(1)} %pad_maximum_fusion.6), channel_id=1, source_target_pairs={{0,2},{2,0},{4,6},{6,4},{8,10},{10,8},{12,14},{14,12},{16,18},{18,... | collective-permute-start | bytes 1327112 | tf_op jit(solution)/shard_map/ppermute | solution.py:43
  168.0 11.9 %collective-permute-start.35 = (bf16[4,48,1152]{2,1,0:T(8,128)(2,1)S(1)}, bf16[4,48,1152]{2,1,0:T(8,128)(2,1)S(1)}, u32[]{:S(2)}, u32[]{:S(2)}) collective-permute-start(bf16[4,48,1152]{2,1,0:T(8,128)(2,1)S(1)} %pad_maximum_fusion.7), channel_id=1, source_target_pairs={{0,4},{2,6},{4,0},{6,2},{8,12},{10,14},{12,8},{14,10},{16,20},{18,... | collective-permute-start | bytes 1327112 | tf_op jit(solution)/shard_map/ppermute | solution.py:43
  169.1 24.7 %collective-permute-start.42 = (bf16[512,768]{1,0:T(8,128)(2,1)S(1)}, bf16[512,768]{1,0:T(8,128)(2,1)S(1)}, u32[]{:S(2)}, u32[]{:S(2)}) collective-permute-start(bf16[512,768]{1,0:T(8,128)(2,1)S(1)} %fusion.11), channel_id=1, source_target_pairs={{0,1},{1,0},{2,3},{3,2},{4,5},{5,4},{6,7},{7,6},{8,9},{9,8},{10,11... | collective-permute-start | bytes 2359304 | tf_op jit(solution)/shard_map/ppermute | solution.py:47
  172.2 2.3 %collective-permute-start.38 = (f32[6,768]{1,0:T(8,128)S(1)}, f32[6,768]{1,0:T(8,128)S(1)}, u32[]{:S(2)}, u32[]{:S(2)}) collective-permute-start(f32[6,768]{1,0:T(8,128)S(1)} %pad_maximum_fusion.8), channel_id=1, source_target_pairs={{0,1},{1,0},{2,3},{3,2},{4,5},{5,4},{6,7},{7,6},{8,9},{9,8},{10,11... | collective-permute-start | bytes 55304 | tf_op jit(solution)/shard_map/ppermute | solution.py:47
  180.1 13.7 %collective-permute-start.39 = (bf16[2,48,1152]{2,1,0:T(8,128)(2,1)S(1)}, bf16[2,48,1152]{2,1,0:T(8,128)(2,1)S(1)}, u32[]{:S(2)}, u32[]{:S(2)}) collective-permute-start(bf16[2,48,1152]{2,1,0:T(8,128)(2,1)S(1)} %fusion.28), channel_id=1, source_target_pairs={{0,8},{2,10},{4,12},{6,14},{8,0},{10,2},{12,4},{14,6},{16,24},{18,... | collective-permute-start | bytes 663560 | tf_op jit(solution)/shard_map/ppermute | solution.py:43
  182.2 4.2 %collective-permute-start.40 = (f32[11,768]{1,0:T(8,128)S(1)}, f32[11,768]{1,0:T(8,128)S(1)}, u32[]{:S(2)}, u32[]{:S(2)}) collective-permute-start(f32[11,768]{1,0:T(8,128)S(1)} %fusion.30), channel_id=1, source_target_pairs={{0,2},{2,0},{4,6},{6,4},{8,10},{10,8},{12,14},{14,12},{16,18},{18,... | collective-permute-start | bytes 101384 | tf_op jit(solution)/shard_map/ppermute | solution.py:43
  183.2 9.8 %collective-permute-start.44 = (bf16[1,48,1920]{2,1,0:T(8,128)(2,1)S(1)}, bf16[1,48,1920]{2,1,0:T(8,128)(2,1)S(1)}, u32[]{:S(2)}, u32[]{:S(2)}) collective-permute-start(bf16[1,48,1920]{2,1,0:T(8,128)(2,1)S(1)} %dynamic-slice_convert_fusion), channel_id=1, source_target_pairs={{0,16},{2,18},{4,20},{6,22},{8,24},{10,26},{12,28},{14,30},{16,0},... | collective-permute-start | bytes 552968 | tf_op jit(solution)/shard_map/ppermute | solution.py:43
  186.4 4.2 %collective-permute-start.41 = (f32[11,768]{1,0:T(8,128)S(1)}, f32[11,768]{1,0:T(8,128)S(1)}, u32[]{:S(2)}, u32[]{:S(2)}) collective-permute-start(f32[11,768]{1,0:T(8,128)S(1)} %fusion.33), channel_id=1, source_target_pairs={{0,4},{2,6},{4,0},{6,2},{8,12},{10,14},{12,8},{14,10},{16,20},{18,... | collective-permute-start | bytes 101384 | tf_op jit(solution)/shard_map/ppermute | solution.py:43
  193.9 10.9 %collective-permute-start.43 = (bf16[1,48,1152]{2,1,0:T(8,128)(2,1)S(1)}, bf16[1,48,1152]{2,1,0:T(8,128)(2,1)S(1)}, u32[]{:S(2)}, u32[]{:S(2)}) collective-permute-start(bf16[1,48,1152]{2,1,0:T(8,128)(2,1)S(1)} %dynamic-slice_convert_fusion.2), channel_id=1, source_target_pairs={{0,16},{2,18},{4,20},{6,22},{8,24},{10,26},{12,28},{14,30},{16,0},... | collective-permute-start | bytes 331784 | tf_op jit(solution)/shard_map/ppermute | solution.py:43
  194.3 4.1 %collective-permute-start.45 = (f32[11,768]{1,0:T(8,128)S(1)}, f32[11,768]{1,0:T(8,128)S(1)}, u32[]{:S(2)}, u32[]{:S(2)}) collective-permute-start(f32[11,768]{1,0:T(8,128)S(1)} %add.114), channel_id=1, source_target_pairs={{0,8},{2,10},{4,12},{6,14},{8,0},{10,2},{12,4},{14,6},{16,24},{18,... | collective-permute-start | bytes 101384 | tf_op jit(solution)/shard_map/ppermute | solution.py:43
  198.4 5.0 %collective-permute-start.46 = (f32[11,768]{1,0:T(8,128)S(1)}, f32[11,768]{1,0:T(8,128)S(1)}, u32[]{:S(2)}, u32[]{:S(2)}) collective-permute-start(f32[11,768]{1,0:T(8,128)S(1)} %add.120.kept_ref), channel_id=1, source_target_pairs={{0,16},{2,18},{4,20},{6,22},{8,24},{10,26},{12,28},{14,30},{16,0},... | collective-permute-start | bytes 101384 | tf_op jit(solution)/shard_map/ppermute | solution.py:43
where the time goes:
time: 209 us; the launch traced here: 206 us
  waiting for transfers between devices  75.3 us (36%)
  Pallas kernels  47.4 us (23%)
  starting transfers between devices  46.8 us (22%)
  matrix products  23.9 us (11%)
  local copies, waits for them, and re-layouts  5.72 us (3%)
  other arithmetic  4.9 us (2%)
    ppermute x37, waiting for transfers between devices, swap_dp(): return lax.ppermute(x, 'dp', [(i, i ^ step) for i in range(n)])  72.5 us
    ppermute x37, starting transfers between devices, swap_dp(): return lax.ppermute(x, 'dp', [(i, i ^ step) for i in range(n)])  44.5 us
    dot_general x11, matrix products, mm(): return jnp.einsum(spec, a, b, preferred_element_type=F32)  23.9 us
    pallas_call x2, Pallas kernels, attend_back(): pl.pallas_call(attend_back_kernel, grid=(count,), in_specs=[pl.BlockSpec(...  18.9 us
    pallas_call x1, Pallas kernels, attend(): pl.pallas_call(attend_kernel, grid=(count,), in_specs=[pl.BlockSpec((n, 3...  10.7 us
  transfers between devices with their start and end apart: 47, of which 24 were waited for; matrix products, arithmetic and copies ran while one was open for 13% of the time, Pallas kernels for 23%

commit v1 on v0

--- a/solution.py
+++ b/solution.py
@@ -346,14 +346,6 @@
     )(*args)
 
 
-def finish_qkv_kernel(kept_ref, got_ref, out_ref):
-    total = kept_ref[...] + got_ref[...].astype(F32)
-    for pair in range(out_ref.shape[2] // PAIR):
-        for i in range(3):
-            start = (3 * pair + i) * PAIR
-            out_ref[i, :, pair * PAIR : (pair + 1) * PAIR] = total[:, start : start + PAIR]
-
-
 def finish_ff_kernel(kept_ref, got_ref, *out_refs):
     total = kept_ref[...] + got_ref[...].astype(F32)
     start = 0
@@ -363,32 +355,41 @@
         start += columns
 
 
-def finish_sums_kernel(kept_ref, got_ref, start_ref, gains_ref, shifts_ref, qv_ref, bias_ref):
+def finish_last_kernel(
+    qkv_ref, qkv_got_ref, sums_ref, sums_got_ref, start_ref, *out_refs
+):
+    grad_ref, gains_ref, shifts_ref, qv_ref, bias_ref = out_refs
+    pairs = qv_ref.shape[1] // PAIR
+    grad = qkv_ref[...] + qkv_got_ref[...].astype(F32)
+    for pair in range(pairs):
+        for i in range(3):
+            start = (3 * pair + i) * PAIR
+            grad_ref[i, :, pair * PAIR : (pair + 1) * PAIR] = grad[:, start : start + PAIR]
     own = gains_ref.shape[1]
-    total = kept_ref[...] + got_ref[...]
+    total = sums_ref[...] + sums_got_ref[...]
     columns = total.shape[1]
     rows = pltpu.roll(total[:8], columns - start_ref[0], 1)[:, :own]
     gains_ref[...] = jnp.concatenate([rows[0:1], rows[2:3]], axis=0)
     shifts_ref[...] = jnp.concatenate([rows[1:2], rows[3:6]], axis=0)
-    pairs = qv_ref.shape[1] // PAIR
     for pair in range(pairs):
         for i in range(2):
             here = slice(2 * i * PAIR, (2 * i + 1) * PAIR)
             qv_ref[i : i + 1, pair * PAIR : (pair + 1) * PAIR] = total[6 + pair : 7 + pair, here]
-    bias_ref[...] = total[6 + pairs :]
-
-
-def finish_sums(kept, got, start, shapes):
+    for i in range(total.shape[0] - 6 - pairs):
+        bias_ref[pl.ds(i * columns, columns)] = total[6 + pairs + i]
+
+
+def finish_last(args, start, shapes):
     return pl.pallas_call(
-        finish_sums_kernel,
-        in_specs=[pl.BlockSpec(memory_space=pltpu.VMEM)] * 2
+        finish_last_kernel,
+        in_specs=[pl.BlockSpec(memory_space=pltpu.VMEM)] * 4
         + [pl.BlockSpec(memory_space=pltpu.SMEM)],
-        out_specs=[pl.BlockSpec(memory_space=pltpu.VMEM)] * 4,
+        out_specs=[pl.BlockSpec(memory_space=pltpu.VMEM)] * 5,
         out_shape=[jax.ShapeDtypeStruct(x, F32) for x in shapes],
         cost_estimate=FREE,
         compiler_params=pltpu.CompilerParams(vmem_limit_bytes=4 * 2**20),
-        name="finish_sums",
-    )(kept, got, start)
+        name="finish_last",
+    )(*args, start)
 
 
 def finish(kernel, kept, got, shapes, name):
@@ -424,12 +425,18 @@
     small = weight_ref.shape[1] - PAIR
     vectors = weight_ref[:, small:].astype(F32).T[:8]
     vectors_ref[...] = vectors
+    qv = bias_ref[...].astype(F32)
+    none = jnp.zeros((1, PAIR), F32)
+    bias = []
+    for start in range(0, qv.shape[1], PAIR):
+        bias += [qv[0:1, start : start + PAIR], none, qv[1:2, start : start + PAIR]]
+    bias = jnp.concatenate(bias, axis=1)
 
     def step(here):
         unit, _ = standardized(x_ref[here].astype(F32))
         normed = (unit * vectors_ref[0:1] + vectors_ref[2:3]).astype(BF)
         normed_ref[here] = normed
-        qkv_ref[here] = (dot(normed, weight_ref[:, :width], 1, 0) + bias_ref[...]).astype(BF)
+        qkv_ref[here] = (dot(normed, weight_ref[:, :width], 1, 0) + bias).astype(BF)
 
     for i in range(0, x_ref.shape[0], ROW_BLOCK):
         step(pl.ds(i, ROW_BLOCK))
@@ -583,13 +590,10 @@
 
     first_own = pack(qkv_weight, out_weight.T, norm_gains, shifts)
     at = position(own)
-    zeros = jnp.zeros((wide,), BF)
-    qkv_bias = jnp.stack([qv_bias[0], zeros, qv_bias[1]]).reshape(3, pairs, PAIR)
-    qkv_bias = qkv_bias.transpose(1, 0, 2).reshape(1, 3 * wide).astype(F32)
     half = inputs.shape[0]
     hidden_n = fc1_weight.shape[1]
     high = [stride for stride, _ in reversed(digits_of(lax.axis_size("dp"))[1:])]
-    first_own, at, qkv_bias = stage(first_own, at, qkv_bias)
+    first_own, at = stage(first_own, at)
     first_part = gather_high_at_once(first_own, at)
     inputs_other = swap_core(inputs)
 
@@ -598,22 +602,18 @@
     first_part, inputs_other, ff_part = stage(first_part, inputs_other, ff_own[None])
     first_near = gather_near(first_part)
     inputs_all = join(inputs, inputs_other)
-    for stride in high[:-1]:
+    for stride in high:
         ff_part = place([ff_part, swap_dp(ff_part, stride)], stride, at)
 
-    first_part, first_near, ff_part, inputs_all = stage(
-        first_part, first_near, ff_part, inputs_all
-    )
+    first_part, first_near, inputs_all = stage(first_part, first_near, inputs_all)
     first_far = gather_far(first_near)
-    for stride in high[-1:]:
-        ff_part = place([ff_part, swap_dp(ff_part, stride)], stride, at)
 
     first_part, first_near, first_far, ff_part = stage(first_part, first_near, first_far, ff_part)
     ff_near = gather_near(ff_part)
     cotangent_other = swap_core(after(cotangent, first_part))
     first_full = all_rows([first_part, *first_near, *first_far], 0, first_part.shape[2], at)
     out_full = first_full[:, 3 * wide : 4 * wide]
-    normed_all, qkv, vectors = project(inputs_all, first_full, qkv_bias, 3 * wide)
+    normed_all, qkv, vectors = project(inputs_all, first_full, qv_bias, 3 * wide)
     attended, log_sums = attend(qkv, 0, pairs)
     branch = mm("fe,de->fd", attended, out_full).astype(BF)
     branch_other = swap_pieces(branch, PIECES)
@@ -690,22 +690,17 @@
     width = rows.shape[1]
     flat = [rows, jnp.pad(d_sums[:, 0], ((0, 0), (0, width - 3 * PAIR)))]
     flat += [fc1_bias_grad[:, i : i + width] for i in range(0, fc1_bias_grad.shape[1], width)]
-    flat = sum_over(jnp.concatenate(flat, axis=0), [1, 2])
+    flat = sum_over(jnp.concatenate(flat, axis=0), [1, 2] + high[:0:-1])
     qkv_sum = scatter_high_step(high_operands(total_of(qkv_near), 0, at), 0)
     mlp_got = swap_core(mlp_other)
     mid_last = scatter_high_last(mid_sum, 1, at)
 
     qkv_sum, flat, mlp_got = stage(qkv_sum, flat, mlp_got)
     outputs = hidden_all[:half] + ((mlp_mine + mlp_got.astype(F32)) + vectors[5:6])
-    flat = sum_over(flat, high[:0:-1])
-    gains_out, shifts_out, qv_out, bias_out = finish_sums(
-        flat,
-        swap_dp(flat, high[0]),
+    qkv_out, gains_out, shifts_out, qv_out, bias_out = finish_last(
+        (*scatter_high_last(qkv_sum, 1, at), flat, swap_dp(flat, high[0])),
         at["start"],
-        [norm_gains.shape, shifts.shape, qv_bias.shape, (flat.shape[0] - 6 - pairs, width)],
-    )
-    (qkv_out,) = finish(
-        finish_qkv_kernel, *scatter_high_last(qkv_sum, 1, at), [qkv_weight.shape], "finish_qkv"
+        [qkv_weight.shape, norm_gains.shape, shifts.shape, qv_bias.shape, fc1_bias.shape],
     )
     (fc2_out,) = finish(finish_ff_kernel, *fc2_last, [(own, hidden_n)], "finish_fc2")
     fc1_out, out_out = finish(
@@ -721,7 +716,7 @@
         gains_out,
         shifts_out,
         qv_out,
-        bias_out.reshape(-1),
+        bias_out,
     )
 
 

time: 209 us -> 204 us (0.976)
  starting transfers between devices: 46.8 us -> 44.2 us
    ppermute x37, starting transfers between devices: 44.5 us -> 41.9 us  [swap_dp(): return lax.ppermute(x, 'dp', [(i, i ^ step) for i in range(n)])]
  transfers between devices with their start and end apart: 47 -> 47, of which waited for: 24 -> 21; matrix products, arithmetic and copies ran while one was open for 13% -> 13% of each run, Pallas kernels for 23% -> 23%
where the time goes in v1:
time: 204 us; the launch traced here: 200 us
  waiting for transfers between devices  74.1 us (36%)
  Pallas kernels  46.7 us (23%)
  starting transfers between devices  44.2 us (22%)
  matrix products  24 us (12%)
  other arithmetic  4.86 us (2%)
  local copies, waits for them, and re-layouts  4.24 us (2%)
    ppermute x37, waiting for transfers between devices, swap_dp(): return lax.ppermute(x, 'dp', [(i, i ^ step) for i in range(n)])  70.5 us
    ppermute x37, starting transfers between devices, swap_dp(): return lax.ppermute(x, 'dp', [(i, i ^ step) for i in range(n)])  41.9 us
    dot_general x11, matrix products, mm(): return jnp.einsum(spec, a, b, preferred_element_type=F32)  24 us
    pallas_call x2, Pallas kernels, attend_back(): pl.pallas_call(attend_back_kernel, grid=(count,), in_specs=[pl.BlockSpec(...  18.9 us
    pallas_call x1, Pallas kernels, attend(): pl.pallas_call(attend_kernel, grid=(count,), in_specs=[pl.BlockSpec((n, 3...  10.7 us
  transfers between devices with their start and end apart: 47, of which 21 were waited for; matrix products, arithmetic and copies ran while one was open for 13% of the time, Pallas kernels for 23%

profile of v1, /device:TPU:0, one launch (start us, length us, event | category | flops | bytes accessed | tf_op | source)
XLA Modules:
  0.0 199.7 jit_solution(8691506084155885556)
XLA Ops:
  0.7 0.9 copy-done.2
  1.6 0.8 copy-done.3
  3.8 5.1 %collective-permute-start = (bf16[1,48,1664]{2,1,0:T(8,128)(2,1)S(1)}, bf16[1,48,1664]{2,1,0:T(8,128)(2,1)S(1)}, u32[]{:S(2)}, u32[]{:S(2)}) collective-permute-start(bf16[1,48,1664]{2,1,0:T(8,128)(2,1)S(1)} %bitcast.183), channel_id=1, source_target_pairs={{0,24},{2,26},{4,28},{6,30},{8,16},{10,18},{12,20},{14,22},{16,8},... | collective-permute-start | bytes 479240 | tf_op jit(solution)/shard_map/ppermute | solution.py:43
  9.5 1.0 maximum_bitcast_fusion.2
  10.5 3.4 %collective-permute-done = bf16[1,48,1664]{2,1,0:T(8,128)(2,1)S(1)} collective-permute-done((bf16[1,48,1664]{2,1,0:T(8,128)(2,1)S(1)}, bf16[1,48,1664]{2,1,0:T(8,128)(2,1)S(1)}, u32[]{:S(2)}, u32[]{:S(2)}) %collective-permute-start) | collective-permute-done | bytes 159776 | tf_op jit(solution)/shard_map/ppermute | solution.py:43
  13.9 8.5 %collective-permute-done.1 = bf16[1,48,1664]{2,1,0:T(8,128)(2,1)S(1)} collective-permute-done((bf16[1,48,1664]{2,1,0:T(8,128)(2,1)S(1)}, bf16[1,48,1664]{2,1,0:T(8,128)(2,1)S(1)}, u32[]{:S(2)}, u32[]{:S(2)}) %collective-permute-start.1) | collective-permute-done | bytes 159776 | tf_op jit(solution)/shard_map/ppermute | solution.py:43
  22.7 1.6 collective-permute-start.4
  24.2 1.5 collective-permute-start.5
  25.8 11.8 %collective-permute-done.8 = bf16[1,48,3072]{2,1,0:T(8,128)(2,1)S(1)} collective-permute-done((bf16[1,48,3072]{2,1,0:T(8,128)(2,1)S(1)}, bf16[1,48,3072]{2,1,0:T(8,128)(2,1)S(1)}, u32[]{:S(2)}, u32[]{:S(2)}) %collective-permute-start.8) | collective-permute-done | bytes 294944 | tf_op jit(solution)/shard_map/ppermute | solution.py:43
  38.2 1.2 collective-permute-done.5.refs_2_
  39.4 1.6 collective-permute-start.6
  41.6 11.4 %collective-permute-done.9 = bf16[2,48,3072]{2,1,0:T(8,128)(2,1)S(1)} collective-permute-done((bf16[2,48,3072]{2,1,0:T(8,128)(2,1)S(1)}, bf16[2,48,3072]{2,1,0:T(8,128)(2,1)S(1)}, u32[]{:S(2)}, u32[]{:S(2)}) %collective-permute-start.9) | collective-permute-done | bytes 589856 | tf_op jit(solution)/shard_map/ppermute | solution.py:43
  53.4 1.6 collective-permute-start.12
  54.9 1.5 collective-permute-start.13
  56.6 2.8 %project.1 = (bf16[1024,768]{1,0:T(8,128)(2,1)S(1)}, bf16[1024,1152]{1,0:T(8,128)(2,1)S(1)}, f32[8,768]{1,0:T(8,128)S(1)}) custom-call(bf16[1024,768]{1,0:T(8,128)(2,1)S(1)} %join.2.x_ref, bf16[768,1664]{1,0:T(8,128)(2,1)S(1)} %bitcast.164, bf16[2,384]{1,0:T(2,128)(2,1)S(1)} %copy-done.4), custom_call_target="tpu_custom_call" | custom-call | tf_op jit(solution)/shard_map/project/pallas_call | solution.py:452
  59.5 10.7 %attend.1 = (bf16[1024,384]{1,0:T(8,128)(2,1)S(1)}, f32[3,2,1024]{2,1,0:T(2,128)S(1)}) custom-call(bf16[1024,1152]{1,0:T(8,128)(2,1)S(1)} %get-tuple-element.139.qkv_ref), custom_call_target="tpu_custom_call" | custom-call | tf_op jit(solution)/shard_map/attend/pallas_call | solution.py:227
  70.2 1.0 convolution_convert_fusion.3.mine_ref
  71.9 1.7 collective-permute-done.10.refs_0_
  73.6 1.1 collective-permute-done.11.refs_1_
  74.8 1.6 mid_norm.1
  76.4 4.1 %collective-permute-done.12.refs_1_ = bf16[4,48,3072]{2,1,0:T(8,128)(2,1)S(1)} collective-permute-done((bf16[4,48,3072]{2,1,0:T(8,128)(2,1)S(1)}, bf16[4,48,3072]{2,1,0:T(8,128)(2,1)S(1)}, u32[]{:S(2)}, u32[]{:S(2)}) %collective-permute-start.12) | collective-permute-done | bytes 1179680 | tf_op jit(solution)/shard_map/ppermute | solution.py:43
  80.5 1.2 collective-permute-done.13.refs_2_
  81.7 1.6 collective-permute-start.15
  84.1 4.6 %collective-permute-done.15.refs_3_ = bf16[2,48,1536]{2,1,0:T(8,128)(2,1)S(1)} collective-permute-done((bf16[2,48,1536]{2,1,0:T(8,128)(2,1)S(1)}, bf16[2,48,1536]{2,1,0:T(8,128)(2,1)S(1)}, u32[]{:S(2)}, u32[]{:S(2)}) %collective-permute-start.15) | collective-permute-done | bytes 294944 | tf_op jit(solution)/shard_map/ppermute | solution.py:43
  88.7 1.5 collective-permute-done.16.refs_4_
  91.5 6.0 %fusion.4 = (bf16[1024,1536]{1,0:T(8,128)(2,1)S(1)}, bf16[1024,1536]{1,0:T(8,128)(2,1)S(1)}) fusion(f32[1536]{0:T(1024)S(1)} %convert_element_type.183, bf16[1024,768]{1,0:T(8,128)(2,1)S(1)} %get-tuple-element.155, bf16[768,1536]{1,0:T(8,128)(2,1)S(1)} %bitcast.179), kind=kOutput, calls=%fused_computation.5 | convolution fusion | flops 2434793472 | bytes 10229760 | tf_op jit(solution)/shard_map/fd,dh->fh/dot_general | solution.py:570
  97.5 3.0 %convolution_convert_fusion.1 = bf16[768,1536]{1,0:T(8,128)(2,1)S(1)} fusion(bf16[1024,768]{1,0:T(8,128)(2,1)S(1)} %join.3.d_out_ref, bf16[1024,1536]{1,0:T(8,128)(2,1)S(1)} %get-tuple-element.200), kind=kOutput, calls=%fused_computation.9 | convolution fusion | flops 2417098752 | bytes 7077888 | tf_op jit(solution)/shard_map/fd,fh->dh/dot_general | solution.py:570
  100.6 1.6 collective-permute-start.19
  102.1 1.6 collective-permute-start.20
  103.9 4.0 %act_back.1 = (bf16[1024,1536]{1,0:T(8,128)(2,1)S(1)}, f32[1,1536]{1,0:T(1,128)S(1)}) custom-call(bf16[1024,768]{1,0:T(8,128)(2,1)S(1)} %join.3.d_out_ref, bf16[768,1536]{1,0:T(8,128)(2,1)S(1)} %bitcast.173, bf16[1024,1536]{1,0:T(8,128)(2,1)S(1)} %get-tuple-element.170.slope_ref), custom_call_target="tpu_custom_call" | custom-call | tf_op jit(solution)/shard_map/act_back/pallas_call | solution.py:494
  107.9 2.6 %convolution_convert_fusion.4.mine_ref = bf16[1024,768]{1,0:T(8,128)(2,1)S(1)} fusion(bf16[1024,1536]{1,0:T(8,128)(2,1)S(1)} %get-tuple-element.176, bf16[768,1536]{1,0:T(8,128)(2,1)S(1)} %bitcast.180), kind=kOutput, calls=%fused_computation.15 | convolution fusion | flops 2416705536 | bytes 7077888 | tf_op jit(solution)/shard_map/fh,dh->fd/dot_general | solution.py:570
  112.7 3.1 %convolution_convert_fusion = bf16[768,1536]{1,0:T(8,128)(2,1)S(1)} fusion(bf16[1024,768]{1,0:T(8,128)(2,1)S(1)} %get-tuple-element.155, bf16[1024,1536]{1,0:T(8,128)(2,1)S(1)} %get-tuple-element.176), kind=kOutput, calls=%fused_computation.8 | convolution fusion | flops 2417098752 | bytes 7077888 | tf_op jit(solution)/shard_map/fd,fh->dh/dot_general | solution.py:570
  115.8 2.7 %mid_norm_back.1 = (bf16[1024,768]{1,0:T(8,128)(2,1)S(1)}, f32[512,768]{1,0:T(8,128)S(1)}, f32[4,768]{1,0:T(4,128)S(1)}) custom-call(bf16[1024,768]{1,0:T(8,128)(2,1)S(1)} %convolution_convert_fusion.4.mine_ref, f32[1024,768]{1,0:T(8,128)S(1)} %get-tuple-element.142.hidden_ref, bf16[1024,768]{1,0:T(8,128)(2,1)S(1)} %join.3.d_out_ref, ...), custom_call_target="tpu_custom_call" | custom-call | tf_op jit(solution)/shard_map/mid_norm_back/pallas_call | solution.py:539
  118.5 1.0 convolution_convert_fusion.5.grad_ref
  119.5 1.0 convolution_convert_fusion.6
  120.9 1.5 collective-permute-start.23
  122.4 1.6 collective-permute-start.24
  124.0 12.7 %attend_back.2 = (bf16[1024,1152]{1,0:T(8,128)(2,1)S(1)}, f32[3,1,384]{2,1,0:T(1,128)S(1)}) custom-call(bf16[1024,1152]{1,0:T(8,128)(2,1)S(1)} %get-tuple-element.139.qkv_ref, f32[3,2,1024]{2,1,0:T(2,128)S(1)} %get-tuple-element.144.lse_ref, bf16[1024,384]{1,0:T(8,128)(2,1)S(1)} %convolution_convert_fusion.5.grad_ref), custom_call_target="tpu_custom_call" | custom-call | tf_op jit(solution)/shard_map/attend_back/pallas_call | solution.py:281
  137.1 0.8 collective-permute-start.27
  139.5 6.1 %attend_back.3 = (bf16[1024,1152]{1,0:T(8,128)(2,1)S(1)}, f32[3,1,384]{2,1,0:T(1,128)S(1)}) custom-call(bf16[1024,1152]{1,0:T(8,128)(2,1)S(1)} %get-tuple-element.139.qkv_ref, f32[3,2,1024]{2,1,0:T(2,128)S(1)} %get-tuple-element.144.lse_ref, bf16[1024,384]{1,0:T(8,128)(2,1)S(1)} %convolution_convert_fusion.5.grad_ref, ...), custom_call_target="tpu_custom_call", output_to_operand_aliasing={{0}: (3, {}), {1}: (4, {})} | custom-call | tf_op jit(solution)/shard_map/attend_back/pallas_call | solution.py:281
  145.6 2.2 %convolution_convert_fusion.2 = bf16[768,1152]{1,0:T(8,128)(2,1)S(1)} fusion(bf16[1024,768]{1,0:T(8,128)(2,1)S(1)} %get-tuple-element.143, bf16[1024,1152]{1,0:T(8,128)(2,1)S(1)} %get-tuple-element.199.qkv_ref), kind=kOutput, calls=%fused_computation.10 | convolution fusion | flops 1812824064 | bytes 5701632 | tf_op jit(solution)/shard_map/fd,fe->de/dot_general | solution.py:570
  148.1 1.5 collective-permute-start.28
  149.6 1.5 collective-permute-start.29
  151.2 1.2 fusion.14
  152.4 1.4 fusion.11
  153.8 1.5 collective-permute-start.32
  155.3 1.4 fusion.7
  156.8 4.8 %collective-permute-done.32 = bf16[1,48,1536]{2,1,0:T(8,128)(2,1)S(1)} collective-permute-done((bf16[1,48,1536]{2,1,0:T(8,128)(2,1)S(1)}, bf16[1,48,1536]{2,1,0:T(8,128)(2,1)S(1)}, u32[]{:S(2)}, u32[]{:S(2)}) %collective-permute-start.32) | collective-permute-done | bytes 147488 | tf_op jit(solution)/shard_map/ppermute | solution.py:43
  163.0 1.7 collective-permute-start.34
  166.0 3.0 %first_norm_back.1 = (f32[512,768]{1,0:T(8,128)}, f32[2,768]{1,0:T(2,128)S(1)}) custom-call(bf16[1024,1152]{1,0:T(8,128)(2,1)S(1)} %get-tuple-element.199.qkv_ref, bf16[768,1664]{1,0:T(8,128)(2,1)S(1)} %bitcast.168, bf16[512,768]{1,0:T(8,128)(2,1)S(1)} %bitcast.178, f32[512,768]{1,0:T(8,128)S(1)} %get-tuple-element.210.d_hidden_ref, ...), custom_call_target="tpu_custom_call" | custom-call | tf_op jit(solution)/shard_map/first_norm_back/pallas_call | solution.py:564
  169.7 0.8 collective-permute-done.38
  170.5 4.9 %collective-permute-done.34 = bf16[4,48,1152]{2,1,0:T(8,128)(2,1)S(1)} collective-permute-done((bf16[4,48,1152]{2,1,0:T(8,128)(2,1)S(1)}, bf16[4,48,1152]{2,1,0:T(8,128)(2,1)S(1)}, u32[]{:S(2)}, u32[]{:S(2)}) %collective-permute-start.34) | collective-permute-done | bytes 442400 | tf_op jit(solution)/shard_map/ppermute | solution.py:43
  175.4 1.3 collective-permute-done.35
  177.6 1.9 collective-permute-start.39
  179.5 1.4 collective-permute-done.40
  181.4 1.1 collective-permute-start.46
  182.6 2.5 %collective-permute-done.41 = f32[11,768]{1,0:T(8,128)S(1)} collective-permute-done((f32[11,768]{1,0:T(8,128)S(1)}, f32[11,768]{1,0:T(8,128)S(1)}, u32[]{:S(2)}, u32[]{:S(2)}) %collective-permute-start.41) | collective-permute-done | bytes 33824 | tf_op jit(solution)/shard_map/ppermute | solution.py:43
  185.1 0.9 collective-permute-start.42
  186.1 3.2 %collective-permute-done.42 = f32[11,768]{1,0:T(8,128)S(1)} collective-permute-done((f32[11,768]{1,0:T(8,128)S(1)}, f32[11,768]{1,0:T(8,128)S(1)}, u32[]{:S(2)}, u32[]{:S(2)}) %collective-permute-start.42) | collective-permute-done | bytes 33824 | tf_op jit(solution)/shard_map/ppermute | solution.py:43
  189.3 1.1 collective-permute-done.46
  190.4 0.8 finish_mid.1
  191.8 2.4 %collective-permute-start.45 = (f32[11,768]{1,0:T(8,128)S(1)}, f32[11,768]{1,0:T(8,128)S(1)}, u32[]{:S(2)}, u32[]{:S(2)}) collective-permute-start(f32[11,768]{1,0:T(8,128)S(1)} %add.115.sums_ref), channel_id=1, source_target_pairs={{0,16},{2,18},{4,20},{6,22},{8,24},{10,26},{12,28},{14,30},{16,0},... | collective-permute-start | bytes 101384 | tf_op jit(solution)/shard_map/ppermute | solution.py:43
  194.2 1.4 add_bitcast_fusion
  195.7 3.1 %collective-permute-done.45.sums_got_ref = f32[11,768]{1,0:T(8,128)S(1)} collective-permute-done((f32[11,768]{1,0:T(8,128)S(1)}, f32[11,768]{1,0:T(8,128)S(1)}, u32[]{:S(2)}, u32[]{:S(2)}) %collective-permute-start.45) | collective-permute-done | bytes 33824 | tf_op jit(solution)/shard_map/ppermute | solution.py:43
  (133 shorter events, 17.8 us)
Async XLA Ops:
  0.7 0.9 copy-start.2
  1.6 0.8 copy-start.3
  2.3 0.7 copy-start.5
  3.0 0.7 copy-start.6
  3.8 10.1 %collective-permute-start = (bf16[1,48,1664]{2,1,0:T(8,128)(2,1)S(1)}, bf16[1,48,1664]{2,1,0:T(8,128)(2,1)S(1)}, u32[]{:S(2)}, u32[]{:S(2)}) collective-permute-start(bf16[1,48,1664]{2,1,0:T(8,128)(2,1)S(1)} %bitcast.183), channel_id=1, source_target_pairs={{0,24},{2,26},{4,28},{6,30},{8,16},{10,18},{12,20},{14,22},{16,8},... | collective-permute-start | bytes 479240 | tf_op jit(solution)/shard_map/ppermute | solution.py:43
  8.9 13.5 %collective-permute-start.1 = (bf16[1,48,1664]{2,1,0:T(8,128)(2,1)S(1)}, bf16[1,48,1664]{2,1,0:T(8,128)(2,1)S(1)}, u32[]{:S(2)}, u32[]{:S(2)}) collective-permute-start(bf16[1,48,1664]{2,1,0:T(8,128)(2,1)S(1)} %bitcast.184), channel_id=1, source_target_pairs={{0,16},{2,18},{4,20},{6,22},{8,24},{10,26},{12,28},{14,30},{16,0},... | collective-permute-start | bytes 479240 | tf_op jit(solution)/shard_map/ppermute | solution.py:43
  8.9 13.5 %collective-permute-start.2 = (bf16[1,48,1664]{2,1,0:T(8,128)(2,1)S(1)}, bf16[1,48,1664]{2,1,0:T(8,128)(2,1)S(1)}, u32[]{:S(2)}, u32[]{:S(2)}) collective-permute-start(bf16[1,48,1664]{2,1,0:T(8,128)(2,1)S(1)} %bitcast.185), channel_id=1, source_target_pairs={{0,8},{2,10},{4,12},{6,14},{8,0},{10,2},{12,4},{14,6},{16,24},{18,... | collective-permute-start | bytes 479240 | tf_op jit(solution)/shard_map/ppermute | solution.py:43
  9.5 13.1 %collective-permute-start.3 = (bf16[512,768]{1,0:T(8,128)(2,1)}, bf16[512,768]{1,0:T(8,128)(2,1)S(1)}, u32[]{:S(2)}, u32[]{:S(2)}) collective-permute-start(bf16[512,768]{1,0:T(8,128)(2,1)} %bitcast.176), channel_id=1, source_target_pairs={{0,1},{1,0},{2,3},{3,2},{4,5},{5,4},{6,7},{7,6},{8,9},{9,8},{10,11... | collective-permute-start | bytes 2359304 | tf_op jit(solution)/shard_map/ppermute | solution.py:47
  10.5 27.3 %copy-start = (bf16[1,512,768]{2,1,0:T(8,128)(2,1)S(1)}, bf16[1,512,768]{2,1,0:T(8,128)(2,1)}, u32[]{:S(2)}) copy-start(bf16[1,512,768]{2,1,0:T(8,128)(2,1)} %param.10) | copy-start | bytes 2359300
  22.6 15.0 %collective-permute-start.8 = (bf16[1,48,3072]{2,1,0:T(8,128)(2,1)S(1)}, bf16[1,48,3072]{2,1,0:T(8,128)(2,1)S(1)}, u32[]{:S(2)}, u32[]{:S(2)}) collective-permute-start(bf16[1,48,3072]{2,1,0:T(8,128)(2,1)S(1)} %maximum_bitcast_fusion.2), channel_id=1, source_target_pairs={{0,16},{2,18},{4,20},{6,22},{8,24},{10,26},{12,28},{14,30},{16,0},... | collective-permute-start | bytes 884744 | tf_op jit(solution)/shard_map/ppermute | solution.py:43
  22.7 15.5 %collective-permute-start.4 = (bf16[4,48,1664]{2,1,0:T(8,128)(2,1)S(1)}, bf16[4,48,1664]{2,1,0:T(8,128)(2,1)S(1)}, u32[]{:S(2)}, u32[]{:S(2)}) collective-permute-start(bf16[4,48,1664]{2,1,0:T(8,128)(2,1)S(1)} %maximum_bitcast_fusion.refs_0_), channel_id=1, source_target_pairs={{0,2},{2,0},{4,6},{6,4},{8,10},{10,8},{12,14},{14,12},{16,18},{18,... | collective-permute-start | bytes 1916936 | tf_op jit(solution)/shard_map/ppermute | solution.py:43
  24.2 15.2 %collective-permute-start.5 = (bf16[4,48,1664]{2,1,0:T(8,128)(2,1)S(1)}, bf16[4,48,1664]{2,1,0:T(8,128)(2,1)S(1)}, u32[]{:S(2)}, u32[]{:S(2)}) collective-permute-start(bf16[4,48,1664]{2,1,0:T(8,128)(2,1)S(1)} %maximum_bitcast_fusion.refs_0_), channel_id=1, source_target_pairs={{0,4},{2,6},{4,0},{6,2},{8,12},{10,14},{12,8},{14,10},{16,20},{18,... | collective-permute-start | bytes 1916936 | tf_op jit(solution)/shard_map/ppermute | solution.py:43
  37.7 15.3 %collective-permute-start.9 = (bf16[2,48,3072]{2,1,0:T(8,128)(2,1)S(1)}, bf16[2,48,3072]{2,1,0:T(8,128)(2,1)S(1)}, u32[]{:S(2)}, u32[]{:S(2)}) collective-permute-start(bf16[2,48,3072]{2,1,0:T(8,128)(2,1)S(1)} %maximum_bitcast_fusion.1), channel_id=1, source_target_pairs={{0,8},{2,10},{4,12},{6,14},{8,0},{10,2},{12,4},{14,6},{16,24},{18,... | collective-permute-start | bytes 1769480 | tf_op jit(solution)/shard_map/ppermute | solution.py:43
  39.4 13.9 %collective-permute-start.6 = (bf16[2,48,1664]{2,1,0:T(8,128)(2,1)S(1)}, bf16[2,48,1664]{2,1,0:T(8,128)(2,1)S(1)}, u32[]{:S(2)}, u32[]{:S(2)}) collective-permute-start(bf16[2,48,1664]{2,1,0:T(8,128)(2,1)S(1)} %slice.71), channel_id=1, source_target_pairs={{0,4},{2,6},{4,0},{6,2},{8,12},{10,14},{12,8},{14,10},{16,20},{18,... | collective-permute-start | bytes 958472 | tf_op jit(solution)/shard_map/ppermute | solution.py:43
  41.0 12.3 %collective-permute-start.7 = (bf16[2,48,1664]{2,1,0:T(8,128)(2,1)S(1)}, bf16[2,48,1664]{2,1,0:T(8,128)(2,1)S(1)}, u32[]{:S(2)}, u32[]{:S(2)}) collective-permute-start(bf16[2,48,1664]{2,1,0:T(8,128)(2,1)S(1)} %slice.72), channel_id=1, source_target_pairs={{0,2},{2,0},{4,6},{6,4},{8,10},{10,8},{12,14},{14,12},{16,18},{18,... | collective-permute-start | bytes 958472 | tf_op jit(solution)/shard_map/ppermute | solution.py:43
  53.4 3.3 %copy-start.4 = (bf16[2,384]{1,0:T(2,128)(2,1)S(1)}, bf16[2,384]{1,0:T(2,128)(2,1)}, u32[]{:S(2)}) copy-start(bf16[2,384]{1,0:T(2,128)(2,1)} %bias_ref.1) | copy-start | bytes 4612
  53.4 27.1 %collective-permute-start.12 = (bf16[4,48,3072]{2,1,0:T(8,128)(2,1)S(1)}, bf16[4,48,3072]{2,1,0:T(8,128)(2,1)S(1)}, u32[]{:S(2)}, u32[]{:S(2)}) collective-permute-start(bf16[4,48,3072]{2,1,0:T(8,128)(2,1)S(1)} %bitcast.169), channel_id=1, source_target_pairs={{0,2},{2,0},{4,6},{6,4},{8,10},{10,8},{12,14},{14,12},{16,18},{18,... | collective-permute-start | bytes 3538952 | tf_op jit(solution)/shard_map/ppermute | solution.py:43
  54.9 26.8 %collective-permute-start.13 = (bf16[4,48,3072]{2,1,0:T(8,128)(2,1)S(1)}, bf16[4,48,3072]{2,1,0:T(8,128)(2,1)S(1)}, u32[]{:S(2)}, u32[]{:S(2)}) collective-permute-start(bf16[4,48,3072]{2,1,0:T(8,128)(2,1)S(1)} %bitcast.170), channel_id=1, source_target_pairs={{0,4},{2,6},{4,0},{6,2},{8,12},{10,14},{12,8},{14,10},{16,20},{18,... | collective-permute-start | bytes 3538952 | tf_op jit(solution)/shard_map/ppermute | solution.py:43
  70.1 1.7 copy-start.1
  71.3 2.4 %collective-permute-start.10 = (bf16[512,768]{1,0:T(8,128)(2,1)S(1)}, bf16[512,768]{1,0:T(8,128)(2,1)S(1)}, u32[]{:S(2)}, u32[]{:S(2)}) collective-permute-start(bf16[512,768]{1,0:T(8,128)(2,1)S(1)} %get-tuple-element.259), channel_id=1, source_target_pairs={{0,1},{1,0},{2,3},{3,2},{4,5},{5,4},{6,7},{7,6},{8,9},{9,8},{10,11... | collective-permute-start | bytes 2359304 | tf_op jit(solution)/shard_map/ppermute | solution.py:47
  71.4 3.4 %collective-permute-start.11 = (bf16[512,768]{1,0:T(8,128)(2,1)S(1)}, bf16[512,768]{1,0:T(8,128)(2,1)S(1)}, u32[]{:S(2)}, u32[]{:S(2)}) collective-permute-start(bf16[512,768]{1,0:T(8,128)(2,1)S(1)} %get-tuple-element.258), channel_id=1, source_target_pairs={{0,1},{1,0},{2,3},{3,2},{4,5},{5,4},{6,7},{7,6},{8,9},{9,8},{10,11... | collective-permute-start | bytes 2359304 | tf_op jit(solution)/shard_map/ppermute | solution.py:47
  71.9 4.5 %collective-permute-start.14 = (bf16[512,768]{1,0:T(8,128)(2,1)S(1)}, bf16[512,768]{1,0:T(8,128)(2,1)S(1)}, u32[]{:S(2)}, u32[]{:S(2)}) collective-permute-start(bf16[512,768]{1,0:T(8,128)(2,1)S(1)} %bitcast.181), channel_id=1, source_target_pairs={{0,1},{1,0},{2,3},{3,2},{4,5},{5,4},{6,7},{7,6},{8,9},{9,8},{10,11... | collective-permute-start | bytes 2359304 | tf_op jit(solution)/shard_map/ppermute | solution.py:47
  74.8 9.2 %copy-start.7 = (bf16[1536]{0:T(1024)(128)(2,1)S(1)}, bf16[1536]{0:T(1024)(128)(2,1)}, u32[]{:S(2)}) copy-start(bf16[1536]{0:T(1024)(128)(2,1)} %param.19) | copy-start | bytes 9220
  81.7 6.9 %collective-permute-start.15 = (bf16[2,48,1536]{2,1,0:T(8,128)(2,1)S(1)}, bf16[2,48,1536]{2,1,0:T(8,128)(2,1)S(1)}, u32[]{:S(2)}, u32[]{:S(2)}) collective-permute-start(bf16[2,48,1536]{2,1,0:T(8,128)(2,1)S(1)} %slice.77), channel_id=1, source_target_pairs={{0,4},{2,6},{4,0},{6,2},{8,12},{10,14},{12,8},{14,10},{16,20},{18,... | collective-permute-start | bytes 884744 | tf_op jit(solution)/shard_map/ppermute | solution.py:43
  83.3 6.9 %collective-permute-start.16 = (bf16[2,48,1536]{2,1,0:T(8,128)(2,1)S(1)}, bf16[2,48,1536]{2,1,0:T(8,128)(2,1)S(1)}, u32[]{:S(2)}, u32[]{:S(2)}) collective-permute-start(bf16[2,48,1536]{2,1,0:T(8,128)(2,1)S(1)} %slice.78), channel_id=1, source_target_pairs={{0,2},{2,0},{4,6},{6,4},{8,10},{10,8},{12,14},{14,12},{16,18},{18,... | collective-permute-start | bytes 884744 | tf_op jit(solution)/shard_map/ppermute | solution.py:43
  90.2 7.2 %collective-permute-start.17 = (bf16[2,48,1536]{2,1,0:T(8,128)(2,1)S(1)}, bf16[2,48,1536]{2,1,0:T(8,128)(2,1)S(1)}, u32[]{:S(2)}, u32[]{:S(2)}) collective-permute-start(bf16[2,48,1536]{2,1,0:T(8,128)(2,1)S(1)} %slice.79), channel_id=1, source_target_pairs={{0,4},{2,6},{4,0},{6,2},{8,12},{10,14},{12,8},{14,10},{16,20},{18,... | collective-permute-start | bytes 884744 | tf_op jit(solution)/shard_map/ppermute | solution.py:43
  90.7 6.8 %collective-permute-start.18 = (bf16[2,48,1536]{2,1,0:T(8,128)(2,1)S(1)}, bf16[2,48,1536]{2,1,0:T(8,128)(2,1)S(1)}, u32[]{:S(2)}, u32[]{:S(2)}) collective-permute-start(bf16[2,48,1536]{2,1,0:T(8,128)(2,1)S(1)} %slice.80), channel_id=1, source_target_pairs={{0,2},{2,0},{4,6},{6,4},{8,10},{10,8},{12,14},{14,12},{16,18},{18,... | collective-permute-start | bytes 884744 | tf_op jit(solution)/shard_map/ppermute | solution.py:43
  100.6 10.1 %collective-permute-start.19 = (bf16[2,48,1536]{2,1,0:T(8,128)(2,1)S(1)}, bf16[2,48,1536]{2,1,0:T(8,128)(2,1)S(1)}, u32[]{:S(2)}, u32[]{:S(2)}) collective-permute-start(bf16[2,48,1536]{2,1,0:T(8,128)(2,1)S(1)} %get-tuple-element.172), channel_id=1, source_target_pairs={{0,2},{2,0},{4,6},{6,4},{8,10},{10,8},{12,14},{14,12},{16,18},{18,... | collective-permute-start | bytes 884744 | tf_op jit(solution)/shard_map/ppermute | solution.py:43
  102.1 8.5 %collective-permute-start.20 = (bf16[2,48,1536]{2,1,0:T(8,128)(2,1)S(1)}, bf16[2,48,1536]{2,1,0:T(8,128)(2,1)S(1)}, u32[]{:S(2)}, u32[]{:S(2)}) collective-permute-start(bf16[2,48,1536]{2,1,0:T(8,128)(2,1)S(1)} %get-tuple-element.173), channel_id=1, source_target_pairs={{0,4},{2,6},{4,0},{6,2},{8,12},{10,14},{12,8},{14,10},{16,20},{18,... | collective-permute-start | bytes 884744 | tf_op jit(solution)/shard_map/ppermute | solution.py:43
  110.8 5.1 %collective-permute-start.21 = (bf16[512,768]{1,0:T(8,128)(2,1)S(1)}, bf16[512,768]{1,0:T(8,128)(2,1)S(1)}, u32[]{:S(2)}, u32[]{:S(2)}) collective-permute-start(bf16[512,768]{1,0:T(8,128)(2,1)S(1)} %get-tuple-element.257), channel_id=1, source_target_pairs={{0,1},{1,0},{2,3},{3,2},{4,5},{5,4},{6,7},{7,6},{8,9},{9,8},{10,11... | collective-permute-start | bytes 2359304 | tf_op jit(solution)/shard_map/ppermute | solution.py:47
  110.8 5.0 %collective-permute-start.22 = (bf16[512,768]{1,0:T(8,128)(2,1)S(1)}, bf16[512,768]{1,0:T(8,128)(2,1)S(1)}, u32[]{:S(2)}, u32[]{:S(2)}) collective-permute-start(bf16[512,768]{1,0:T(8,128)(2,1)S(1)} %get-tuple-element.256), channel_id=1, source_target_pairs={{0,1},{1,0},{2,3},{3,2},{4,5},{5,4},{6,7},{7,6},{8,9},{9,8},{10,11... | collective-permute-start | bytes 2359304 | tf_op jit(solution)/shard_map/ppermute | solution.py:47
  111.5 25.3 %collective-permute-start.25 = (bf16[4,48,1536]{2,1,0:T(8,128)(2,1)S(1)}, bf16[4,48,1536]{2,1,0:T(8,128)(2,1)S(1)}, u32[]{:S(2)}, u32[]{:S(2)}) collective-permute-start(bf16[4,48,1536]{2,1,0:T(8,128)(2,1)S(1)} %pad_maximum_fusion.4), channel_id=1, source_target_pairs={{0,2},{2,0},{4,6},{6,4},{8,10},{10,8},{12,14},{14,12},{16,18},{18,... | collective-permute-start | bytes 1769480 | tf_op jit(solution)/shard_map/ppermute | solution.py:43
  112.2 24.6 %collective-permute-start.26 = (bf16[4,48,1536]{2,1,0:T(8,128)(2,1)S(1)}, bf16[4,48,1536]{2,1,0:T(8,128)(2,1)S(1)}, u32[]{:S(2)}, u32[]{:S(2)}) collective-permute-start(bf16[4,48,1536]{2,1,0:T(8,128)(2,1)S(1)} %pad_maximum_fusion.5), channel_id=1, source_target_pairs={{0,4},{2,6},{4,0},{6,2},{8,12},{10,14},{12,8},{14,10},{16,20},{18,... | collective-permute-start | bytes 1769480 | tf_op jit(solution)/shard_map/ppermute | solution.py:43
  120.9 16.0 %collective-permute-start.23 = (bf16[2,48,1920]{2,1,0:T(8,128)(2,1)S(1)}, bf16[2,48,1920]{2,1,0:T(8,128)(2,1)S(1)}, u32[]{:S(2)}, u32[]{:S(2)}) collective-permute-start(bf16[2,48,1920]{2,1,0:T(8,128)(2,1)S(1)} %get-tuple-element.180), channel_id=1, source_target_pairs={{0,2},{2,0},{4,6},{6,4},{8,10},{10,8},{12,14},{14,12},{16,18},{18,... | collective-permute-start | bytes 1105928 | tf_op jit(solution)/shard_map/ppermute | solution.py:43
  122.4 14.5 %collective-permute-start.24 = (bf16[2,48,1920]{2,1,0:T(8,128)(2,1)S(1)}, bf16[2,48,1920]{2,1,0:T(8,128)(2,1)S(1)}, u32[]{:S(2)}, u32[]{:S(2)}) collective-permute-start(bf16[2,48,1920]{2,1,0:T(8,128)(2,1)S(1)} %get-tuple-element.181), channel_id=1, source_target_pairs={{0,4},{2,6},{4,0},{6,2},{8,12},{10,14},{12,8},{14,10},{16,20},{18,... | collective-permute-start | bytes 1105928 | tf_op jit(solution)/shard_map/ppermute | solution.py:43
  137.1 10.9 %collective-permute-start.27 = (bf16[2,48,1536]{2,1,0:T(8,128)(2,1)S(1)}, bf16[2,48,1536]{2,1,0:T(8,128)(2,1)S(1)}, u32[]{:S(2)}, u32[]{:S(2)}) collective-permute-start(bf16[2,48,1536]{2,1,0:T(8,128)(2,1)S(1)} %fusion.27), channel_id=1, source_target_pairs={{0,8},{2,10},{4,12},{6,14},{8,0},{10,2},{12,4},{14,6},{16,24},{18,... | collective-permute-start | bytes 884744 | tf_op jit(solution)/shard_map/ppermute | solution.py:43
  138.2 23.4 %collective-permute-start.30 = (bf16[4,48,1920]{2,1,0:T(8,128)(2,1)S(1)}, bf16[4,48,1920]{2,1,0:T(8,128)(2,1)S(1)}, u32[]{:S(2)}, u32[]{:S(2)}) collective-permute-start(bf16[4,48,1920]{2,1,0:T(8,128)(2,1)S(1)} %pad_maximum_fusion.2), channel_id=1, source_target_pairs={{0,2},{2,0},{4,6},{6,4},{8,10},{10,8},{12,14},{14,12},{16,18},{18,... | collective-permute-start | bytes 2211848 | tf_op jit(solution)/shard_map/ppermute | solution.py:43
  138.9 22.7 %collective-permute-start.31 = (bf16[4,48,1920]{2,1,0:T(8,128)(2,1)S(1)}, bf16[4,48,1920]{2,1,0:T(8,128)(2,1)S(1)}, u32[]{:S(2)}, u32[]{:S(2)}) collective-permute-start(bf16[4,48,1920]{2,1,0:T(8,128)(2,1)S(1)} %pad_maximum_fusion.3), channel_id=1, source_target_pairs={{0,4},{2,6},{4,0},{6,2},{8,12},{10,14},{12,8},{14,10},{16,20},{18,... | collective-permute-start | bytes 2211848 | tf_op jit(solution)/shard_map/ppermute | solution.py:43
  148.1 13.5 %collective-permute-start.28 = (bf16[2,48,1152]{2,1,0:T(8,128)(2,1)S(1)}, bf16[2,48,1152]{2,1,0:T(8,128)(2,1)S(1)}, u32[]{:S(2)}, u32[]{:S(2)}) collective-permute-start(bf16[2,48,1152]{2,1,0:T(8,128)(2,1)S(1)} %get-tuple-element.195), channel_id=1, source_target_pairs={{0,2},{2,0},{4,6},{6,4},{8,10},{10,8},{12,14},{14,12},{16,18},{18,... | collective-permute-start | bytes 663560 | tf_op jit(solution)/shard_map/ppermute | solution.py:43
  149.6 11.9 %collective-permute-start.29 = (bf16[2,48,1152]{2,1,0:T(8,128)(2,1)S(1)}, bf16[2,48,1152]{2,1,0:T(8,128)(2,1)S(1)}, u32[]{:S(2)}, u32[]{:S(2)}) collective-permute-start(bf16[2,48,1152]{2,1,0:T(8,128)(2,1)S(1)} %get-tuple-element.196), channel_id=1, source_target_pairs={{0,4},{2,6},{4,0},{6,2},{8,12},{10,14},{12,8},{14,10},{16,20},{18,... | collective-permute-start | bytes 663560 | tf_op jit(solution)/shard_map/ppermute | solution.py:43
  153.8 7.7 %collective-permute-start.32 = (bf16[1,48,1536]{2,1,0:T(8,128)(2,1)S(1)}, bf16[1,48,1536]{2,1,0:T(8,128)(2,1)S(1)}, u32[]{:S(2)}, u32[]{:S(2)}) collective-permute-start(bf16[1,48,1536]{2,1,0:T(8,128)(2,1)S(1)} %dynamic-slice_convert_fusion.1), channel_id=1, source_target_pairs={{0,16},{2,18},{4,20},{6,22},{8,24},{10,26},{12,28},{14,30},{16,0},... | collective-permute-start | bytes 442376 | tf_op jit(solution)/shard_map/ppermute | solution.py:43
  162.0 7.7 %collective-permute-start.33 = (bf16[2,48,1920]{2,1,0:T(8,128)(2,1)S(1)}, bf16[2,48,1920]{2,1,0:T(8,128)(2,1)S(1)}, u32[]{:S(2)}, u32[]{:S(2)}) collective-permute-start(bf16[2,48,1920]{2,1,0:T(8,128)(2,1)S(1)} %fusion.26), channel_id=1, source_target_pairs={{0,8},{2,10},{4,12},{6,14},{8,0},{10,2},{12,4},{14,6},{16,24},{18,... | collective-permute-start | bytes 1105928 | tf_op jit(solution)/shard_map/ppermute | solution.py:43
  162.3 3.8 %collective-permute-start.36 = (bf16[256,768]{1,0:T(8,128)(2,1)S(1)}, bf16[256,768]{1,0:T(8,128)(2,1)S(1)}, u32[]{:S(2)}, u32[]{:S(2)}) collective-permute-start(bf16[256,768]{1,0:T(8,128)(2,1)S(1)} %get-tuple-element.263), channel_id=1, source_target_pairs={{0,1},{1,0},{2,3},{3,2},{4,5},{5,4},{6,7},{7,6},{8,9},{9,8},{10,11... | collective-permute-start | bytes 1179656 | tf_op jit(solution)/shard_map/ppermute | solution.py:47
  162.3 3.7 %collective-permute-start.37 = (bf16[256,768]{1,0:T(8,128)(2,1)S(1)}, bf16[256,768]{1,0:T(8,128)(2,1)S(1)}, u32[]{:S(2)}, u32[]{:S(2)}) collective-permute-start(bf16[256,768]{1,0:T(8,128)(2,1)S(1)} %get-tuple-element.262), channel_id=1, source_target_pairs={{0,1},{1,0},{2,3},{3,2},{4,5},{5,4},{6,7},{7,6},{8,9},{9,8},{10,11... | collective-permute-start | bytes 1179656 | tf_op jit(solution)/shard_map/ppermute | solution.py:47
  163.0 12.4 %collective-permute-start.34 = (bf16[4,48,1152]{2,1,0:T(8,128)(2,1)S(1)}, bf16[4,48,1152]{2,1,0:T(8,128)(2,1)S(1)}, u32[]{:S(2)}, u32[]{:S(2)}) collective-permute-start(bf16[4,48,1152]{2,1,0:T(8,128)(2,1)S(1)} %pad_maximum_fusion.6), channel_id=1, source_target_pairs={{0,2},{2,0},{4,6},{6,4},{8,10},{10,8},{12,14},{14,12},{16,18},{18,... | collective-permute-start | bytes 1327112 | tf_op jit(solution)/shard_map/ppermute | solution.py:43
  164.8 11.9 %collective-permute-start.35 = (bf16[4,48,1152]{2,1,0:T(8,128)(2,1)S(1)}, bf16[4,48,1152]{2,1,0:T(8,128)(2,1)S(1)}, u32[]{:S(2)}, u32[]{:S(2)}) collective-permute-start(bf16[4,48,1152]{2,1,0:T(8,128)(2,1)S(1)} %pad_maximum_fusion.7), channel_id=1, source_target_pairs={{0,4},{2,6},{4,0},{6,2},{8,12},{10,14},{12,8},{14,10},{16,20},{18,... | collective-permute-start | bytes 1327112 | tf_op jit(solution)/shard_map/ppermute | solution.py:43
  166.0 25.2 %collective-permute-start.43 = (bf16[512,768]{1,0:T(8,128)(2,1)S(1)}, bf16[512,768]{1,0:T(8,128)(2,1)S(1)}, u32[]{:S(2)}, u32[]{:S(2)}) collective-permute-start(bf16[512,768]{1,0:T(8,128)(2,1)S(1)} %fusion.11), channel_id=1, source_target_pairs={{0,1},{1,0},{2,3},{3,2},{4,5},{5,4},{6,7},{7,6},{8,9},{9,8},{10,11... | collective-permute-start | bytes 2359304 | tf_op jit(solution)/shard_map/ppermute | solution.py:47
  169.1 1.4 collective-permute-start.38
  176.8 4.2 %collective-permute-start.40 = (f32[11,768]{1,0:T(8,128)S(1)}, f32[11,768]{1,0:T(8,128)S(1)}, u32[]{:S(2)}, u32[]{:S(2)}) collective-permute-start(f32[11,768]{1,0:T(8,128)S(1)} %fusion.30), channel_id=1, source_target_pairs={{0,2},{2,0},{4,6},{6,4},{8,10},{10,8},{12,14},{14,12},{16,18},{18,... | collective-permute-start | bytes 101384 | tf_op jit(solution)/shard_map/ppermute | solution.py:43
  177.6 13.6 %collective-permute-start.39 = (bf16[2,48,1152]{2,1,0:T(8,128)(2,1)S(1)}, bf16[2,48,1152]{2,1,0:T(8,128)(2,1)S(1)}, u32[]{:S(2)}, u32[]{:S(2)}) collective-permute-start(bf16[2,48,1152]{2,1,0:T(8,128)(2,1)S(1)} %fusion.28), channel_id=1, source_target_pairs={{0,8},{2,10},{4,12},{6,14},{8,0},{10,2},{12,4},{14,6},{16,24},{18,... | collective-permute-start | bytes 663560 | tf_op jit(solution)/shard_map/ppermute | solution.py:43
  180.9 4.2 %collective-permute-start.41 = (f32[11,768]{1,0:T(8,128)S(1)}, f32[11,768]{1,0:T(8,128)S(1)}, u32[]{:S(2)}, u32[]{:S(2)}) collective-permute-start(f32[11,768]{1,0:T(8,128)S(1)} %fusion.33), channel_id=1, source_target_pairs={{0,4},{2,6},{4,0},{6,2},{8,12},{10,14},{12,8},{14,10},{16,20},{18,... | collective-permute-start | bytes 101384 | tf_op jit(solution)/shard_map/ppermute | solution.py:43
  181.4 8.9 %collective-permute-start.46 = (bf16[1,48,1920]{2,1,0:T(8,128)(2,1)S(1)}, bf16[1,48,1920]{2,1,0:T(8,128)(2,1)S(1)}, u32[]{:S(2)}, u32[]{:S(2)}) collective-permute-start(bf16[1,48,1920]{2,1,0:T(8,128)(2,1)S(1)} %dynamic-slice_convert_fusion), channel_id=1, source_target_pairs={{0,16},{2,18},{4,20},{6,22},{8,24},{10,26},{12,28},{14,30},{16,0},... | collective-permute-start | bytes 552968 | tf_op jit(solution)/shard_map/ppermute | solution.py:43
  185.1 4.2 %collective-permute-start.42 = (f32[11,768]{1,0:T(8,128)S(1)}, f32[11,768]{1,0:T(8,128)S(1)}, u32[]{:S(2)}, u32[]{:S(2)}) collective-permute-start(f32[11,768]{1,0:T(8,128)S(1)} %add.114), channel_id=1, source_target_pairs={{0,8},{2,10},{4,12},{6,14},{8,0},{10,2},{12,4},{14,6},{16,24},{18,... | collective-permute-start | bytes 101384 | tf_op jit(solution)/shard_map/ppermute | solution.py:43
  191.3 7.5 %collective-permute-start.44 = (bf16[1,48,1152]{2,1,0:T(8,128)(2,1)S(1)}, bf16[1,48,1152]{2,1,0:T(8,128)(2,1)S(1)}, u32[]{:S(2)}, u32[]{:S(2)}) collective-permute-start(bf16[1,48,1152]{2,1,0:T(8,128)(2,1)S(1)} %dynamic-slice_convert_fusion.2), channel_id=1, source_target_pairs={{0,16},{2,18},{4,20},{6,22},{8,24},{10,26},{12,28},{14,30},{16,0},... | collective-permute-start | bytes 331784 | tf_op jit(solution)/shard_map/ppermute | solution.py:43
  191.8 6.9 %collective-permute-start.45 = (f32[11,768]{1,0:T(8,128)S(1)}, f32[11,768]{1,0:T(8,128)S(1)}, u32[]{:S(2)}, u32[]{:S(2)}) collective-permute-start(f32[11,768]{1,0:T(8,128)S(1)} %add.115.sums_ref), channel_id=1, source_target_pairs={{0,16},{2,18},{4,20},{6,22},{8,24},{10,26},{12,28},{14,30},{16,0},... | collective-permute-start | bytes 101384 | tf_op jit(solution)/shard_map/ppermute | solution.py:43

commit v2 on v1

--- a/solution.py
+++ b/solution.py
@@ -14,7 +14,8 @@
 ROWS_VMEM = 16 * 2**20
 PIECES = 2
 ROW_BLOCK = 256
-COLUMN_BLOCK = 384
+COLUMN_BLOCK = 512
+ACT_BLOCK = 256
 FREE = pl.CostEstimate(flops=0, bytes_accessed=0, transcendentals=0)
 EPS = 1e-05
 BF = jnp.bfloat16
@@ -479,6 +480,22 @@
     return rows_call(mid_norm_kernel, shapes, "mid_norm")(x, mine, vectors, *others)
 
 
+def act_kernel(x_ref, weight_ref, bias_ref, act_ref, slope_ref):
+    bias = bias_ref[...].astype(F32).reshape(1, bias_ref.shape[0])
+    for start in range(0, act_ref.shape[1], ACT_BLOCK):
+        here = slice(start, start + ACT_BLOCK)
+        pre = dot(x_ref[...], weight_ref[:, here], 1, 0) + bias[:, here]
+        cdf = 0.5 * (1.0 + lax.erf(pre * 0.5**0.5))
+        act_ref[:, here] = (pre * cdf).astype(BF)
+        slope = cdf + pre * jnp.exp(-0.5 * pre * pre) * 0.3989422804014327
+        slope_ref[:, here] = slope.astype(BF)
+
+
+def act(x, weight, bias):
+    shape = jax.ShapeDtypeStruct((x.shape[0], weight.shape[1]), BF)
+    return rows_call(act_kernel, [shape, shape], "act")(x, weight, bias)
+
+
 def act_back_kernel(d_out_ref, weight_ref, slope_ref, d_pre_ref, sums_ref):
     @pl.loop(0, d_pre_ref.shape[1] // COLUMN_BLOCK)
     def _(i):
@@ -563,6 +580,24 @@
     shapes = [jax.ShapeDtypeStruct((n, columns), F32) for n in (rows, 2)]
     return rows_call(first_norm_back_kernel, shapes, "first_norm_back")(
         d_qkv, first_full, x, d_hidden, vectors, *others
+    )
+
+
+def last_terms_kernel(d_qkv_ref, first_ref, act_ref, end_ref, d_other_ref, other_ref, mine_ref):
+    half, columns = mine_ref.shape
+    width = d_qkv_ref.shape[1]
+    there = pl.ds(half, half)
+    d_other = dot(d_qkv_ref[there], first_ref[:, :width], 1, 1)
+    d_other_ref[...] = d_other.astype(BF)
+    other_ref[...] = dot(act_ref[there], end_ref[...], 1, 1).astype(BF)
+    mine_ref[...] = dot(act_ref[pl.ds(0, half)], end_ref[...], 1, 1)
+
+
+def last_terms(d_qkv, first_full, hidden_act, end_full):
+    shape = (d_qkv.shape[0] // 2, end_full.shape[0])
+    shapes = [jax.ShapeDtypeStruct(shape, t) for t in (BF, BF, F32)]
+    return rows_call(last_terms_kernel, shapes, "last_terms")(
+        d_qkv, first_full, hidden_act, end_full
     )
 
 
@@ -628,11 +663,8 @@
     ff_part, ff_near, mid_far, d_out_all = stage(ff_part, ff_near, mid_far, d_out_all)
     end_far = gather_far([x[:, :, hidden_n:] for x in ff_near])
     mid_full = all_rows([ff_part, *ff_near, *mid_far], 0, hidden_n, at)
-    hidden_pre = mm("fd,dh->fh", normed_two_all, mid_full) + fc1_bias.astype(F32)
-    cdf = 0.5 * (1.0 + lax.erf(hidden_pre * 0.5**0.5))
-    hidden_act = (hidden_pre * cdf).astype(BF)
-    slope = cdf + hidden_pre * jnp.exp(-0.5 * hidden_pre * hidden_pre) * 0.3989422804014327
-    hidden_act, slope, d_out_all, end_far = stage(hidden_act, slope.astype(BF), d_out_all, end_far)
+    hidden_act, slope = act(normed_two_all, mid_full, fc1_bias)
+    hidden_act, slope, d_out_all = stage(hidden_act, slope, d_out_all)
     fc2_grad = mm("fd,fh->dh", d_out_all, hidden_act).astype(BF)
     fc2_parts, fc2_ops = scatter_operands(fc2_grad, at)
 
@@ -668,16 +700,15 @@
 
     qkv_ops, d_qkv, fc2_sum, hidden_act = stage(qkv_ops, d_qkv, fc2_sum, hidden_act)
     qkv_far = scatter_low_across(qkv_ops)
-    d_other = mm("fe,de->fd", d_qkv[half:], first_full[:, : 3 * wide]).astype(BF)
-    mlp_other = mm("fh,dh->fd", hidden_act[half:], end_full).astype(BF)
-    mlp_mine = mm("fh,dh->fd", hidden_act[:half], end_full)
-
+    d_other, mlp_other, mlp_mine = last_terms(d_qkv, first_full, hidden_act, end_full)
     fc2_last = scatter_high_last(fc2_sum, 1, at)
 
     qkv_far, mid_near, d_other, mlp_other, mlp_mine, fc2_last = stage(
         qkv_far, mid_near, d_other, mlp_other, mlp_mine, fc2_last
     )
-    qkv_near = scatter_low_near(near_operands(qkv_parts, qkv_far))
+    qkv_ops = near_operands(qkv_parts, qkv_far)
+    mid_near = after(mid_near, qkv_ops)
+    qkv_near = scatter_low_near(qkv_ops)
     mid_sum = scatter_high_step(high_operands(total_of(mid_near), 0, at), 0)
     d_other_got = swap_pieces(d_other, 2)
     input_grad, first_sums = first_norm_back(
@@ -690,18 +721,20 @@
     width = rows.shape[1]
     flat = [rows, jnp.pad(d_sums[:, 0], ((0, 0), (0, width - 3 * PAIR)))]
     flat += [fc1_bias_grad[:, i : i + width] for i in range(0, fc1_bias_grad.shape[1], width)]
-    flat = sum_over(jnp.concatenate(flat, axis=0), [1, 2] + high[:0:-1])
+    flat = sum_over(jnp.concatenate(flat, axis=0), [1, 2])
     qkv_sum = scatter_high_step(high_operands(total_of(qkv_near), 0, at), 0)
     mlp_got = swap_core(mlp_other)
     mid_last = scatter_high_last(mid_sum, 1, at)
 
     qkv_sum, flat, mlp_got = stage(qkv_sum, flat, mlp_got)
     outputs = hidden_all[:half] + ((mlp_mine + mlp_got.astype(F32)) + vectors[5:6])
+    flat = sum_over(flat, high[:0:-1])
     qkv_out, gains_out, shifts_out, qv_out, bias_out = finish_last(
         (*scatter_high_last(qkv_sum, 1, at), flat, swap_dp(flat, high[0])),
         at["start"],
         [qkv_weight.shape, norm_gains.shape, shifts.shape, qv_bias.shape, fc1_bias.shape],
     )
+    mid_last = after(mid_last[0], qkv_sum), mid_last[1]
     (fc2_out,) = finish(finish_ff_kernel, *fc2_last, [(own, hidden_n)], "finish_fc2")
     fc1_out, out_out = finish(
         finish_ff_kernel, *mid_last, [(own, n) for n in (hidden_n, wide)], "finish_mid"

time: 204 us -> 200 us (0.980)
  matrix products: 24 us -> 13.8 us
  Pallas kernels: 46.7 us -> 54.3 us
  waiting for transfers between devices: 74.1 us -> 72 us
    dot_general x11 -> x7, matrix products: 24 us -> 13.8 us  [mm(): return jnp.einsum(spec, a, b, preferred_element_type=F32)]
    pallas_call x0 -> x2, Pallas kernels: none -> 8.21 us  [the longest x1 4.55 us: act(): return rows_call(act_kernel, [shape, shape], 'act')(x, weight, bias)]
  transfers between devices with their start and end apart: 47 -> 47, of which waited for: 21 -> 23; matrix products, arithmetic and copies ran while one was open for 13% -> 10% of each run, Pallas kernels for 23% -> 27%
where the time goes in v2:
time: 200 us; the launch traced here: 196 us
  waiting for transfers between devices  72 us (36%)
  Pallas kernels  54.3 us (27%)
  starting transfers between devices  45 us (22%)
  matrix products  13.8 us (7%)
  other arithmetic  4.83 us (2%)
  local copies, waits for them, and re-layouts  4.64 us (2%)
    ppermute x37, waiting for transfers between devices, swap_dp(): return lax.ppermute(x, 'dp', [(i, i ^ step) for i in range(n)])  69.6 us
    ppermute x37, starting transfers between devices, swap_dp(): return lax.ppermute(x, 'dp', [(i, i ^ step) for i in range(n)])  42.7 us
    pallas_call x2, Pallas kernels, attend_back(): pl.pallas_call(attend_back_kernel, grid=(count,), in_specs=[pl.BlockSpec(...  18.7 us
    dot_general x7, matrix products, mm(): return jnp.einsum(spec, a, b, preferred_element_type=F32)  13.8 us
    pallas_call x1, Pallas kernels, attend(): pl.pallas_call(attend_kernel, grid=(count,), in_specs=[pl.BlockSpec((n, 3...  10.7 us
    pallas_call x1, Pallas kernels, act(): return rows_call(act_kernel, [shape, shape], 'act')(x, weight, bias)  4.55 us
  transfers between devices with their start and end apart: 47, of which 23 were waited for; matrix products, arithmetic and copies ran while one was open for 10% of the time, Pallas kernels for 27%

profile of v2, /device:TPU:0, one launch (start us, length us, event | category | flops | bytes accessed | tf_op | source)
XLA Modules:
  0.0 196.2 jit_solution(6578746456380042631)
XLA Ops:
  0.7 0.9 copy-done.2
  1.6 0.8 copy-done.3
  3.8 5.1 %collective-permute-start = (bf16[1,48,1664]{2,1,0:T(8,128)(2,1)S(1)}, bf16[1,48,1664]{2,1,0:T(8,128)(2,1)S(1)}, u32[]{:S(2)}, u32[]{:S(2)}) collective-permute-start(bf16[1,48,1664]{2,1,0:T(8,128)(2,1)S(1)} %bitcast.178), channel_id=1, source_target_pairs={{0,24},{2,26},{4,28},{6,30},{8,16},{10,18},{12,20},{14,22},{16,8},... | collective-permute-start | bytes 479240 | tf_op jit(solution)/shard_map/ppermute | solution.py:44
  9.5 1.0 maximum_bitcast_fusion.2
  10.5 3.4 %collective-permute-done = bf16[1,48,1664]{2,1,0:T(8,128)(2,1)S(1)} collective-permute-done((bf16[1,48,1664]{2,1,0:T(8,128)(2,1)S(1)}, bf16[1,48,1664]{2,1,0:T(8,128)(2,1)S(1)}, u32[]{:S(2)}, u32[]{:S(2)}) %collective-permute-start) | collective-permute-done | bytes 159776 | tf_op jit(solution)/shard_map/ppermute | solution.py:44
  13.9 8.5 %collective-permute-done.1 = bf16[1,48,1664]{2,1,0:T(8,128)(2,1)S(1)} collective-permute-done((bf16[1,48,1664]{2,1,0:T(8,128)(2,1)S(1)}, bf16[1,48,1664]{2,1,0:T(8,128)(2,1)S(1)}, u32[]{:S(2)}, u32[]{:S(2)}) %collective-permute-start.1) | collective-permute-done | bytes 159776 | tf_op jit(solution)/shard_map/ppermute | solution.py:44
  22.7 1.6 collective-permute-start.4
  24.3 1.5 collective-permute-start.5
  25.8 11.8 %collective-permute-done.8 = bf16[1,48,3072]{2,1,0:T(8,128)(2,1)S(1)} collective-permute-done((bf16[1,48,3072]{2,1,0:T(8,128)(2,1)S(1)}, bf16[1,48,3072]{2,1,0:T(8,128)(2,1)S(1)}, u32[]{:S(2)}, u32[]{:S(2)}) %collective-permute-start.8) | collective-permute-done | bytes 294944 | tf_op jit(solution)/shard_map/ppermute | solution.py:44
  38.2 1.2 collective-permute-done.5.refs_2_
  39.4 1.6 collective-permute-start.6
  41.7 11.4 %collective-permute-done.9 = bf16[2,48,3072]{2,1,0:T(8,128)(2,1)S(1)} collective-permute-done((bf16[2,48,3072]{2,1,0:T(8,128)(2,1)S(1)}, bf16[2,48,3072]{2,1,0:T(8,128)(2,1)S(1)}, u32[]{:S(2)}, u32[]{:S(2)}) %collective-permute-start.9) | collective-permute-done | bytes 589856 | tf_op jit(solution)/shard_map/ppermute | solution.py:44
  53.4 1.6 collective-permute-start.12
  54.9 1.5 collective-permute-start.13
  56.6 2.8 %project.1 = (bf16[1024,768]{1,0:T(8,128)(2,1)S(1)}, bf16[1024,1152]{1,0:T(8,128)(2,1)S(1)}, f32[8,768]{1,0:T(8,128)S(1)}) custom-call(bf16[1024,768]{1,0:T(8,128)(2,1)S(1)} %join.2.x_ref, bf16[768,1664]{1,0:T(8,128)(2,1)S(1)} %bitcast.160, bf16[2,384]{1,0:T(2,128)(2,1)S(1)} %copy-done.5), custom_call_target="tpu_custom_call" | custom-call | tf_op jit(solution)/shard_map/project/pallas_call | solution.py:453
  59.5 10.7 %attend.1 = (bf16[1024,384]{1,0:T(8,128)(2,1)S(1)}, f32[3,2,1024]{2,1,0:T(2,128)S(1)}) custom-call(bf16[1024,1152]{1,0:T(8,128)(2,1)S(1)} %get-tuple-element.146.qkv_ref), custom_call_target="tpu_custom_call" | custom-call | tf_op jit(solution)/shard_map/attend/pallas_call | solution.py:228
  70.2 1.0 convolution_convert_fusion.3.mine_ref
  72.3 1.3 collective-permute-done.10.refs_0_
  73.6 1.1 collective-permute-done.11.refs_1_
  74.8 1.6 mid_norm.1
  76.4 4.1 %collective-permute-done.12.refs_1_ = bf16[4,48,3072]{2,1,0:T(8,128)(2,1)S(1)} collective-permute-done((bf16[4,48,3072]{2,1,0:T(8,128)(2,1)S(1)}, bf16[4,48,3072]{2,1,0:T(8,128)(2,1)S(1)}, u32[]{:S(2)}, u32[]{:S(2)}) %collective-permute-start.12) | collective-permute-done | bytes 1179680 | tf_op jit(solution)/shard_map/ppermute | solution.py:44
  80.5 1.2 collective-permute-done.13.refs_2_
  81.7 1.6 collective-permute-start.15
  84.0 4.6 %collective-permute-done.15.refs_3_ = bf16[2,48,1536]{2,1,0:T(8,128)(2,1)S(1)} collective-permute-done((bf16[2,48,1536]{2,1,0:T(8,128)(2,1)S(1)}, bf16[2,48,1536]{2,1,0:T(8,128)(2,1)S(1)}, u32[]{:S(2)}, u32[]{:S(2)}) %collective-permute-start.15) | collective-permute-done | bytes 294944 | tf_op jit(solution)/shard_map/ppermute | solution.py:44
  88.7 1.5 collective-permute-done.16.refs_4_
  91.5 4.5 %act.1 = (bf16[1024,1536]{1,0:T(8,128)(2,1)S(1)}, bf16[1024,1536]{1,0:T(8,128)(2,1)S(1)}) custom-call(bf16[1024,768]{1,0:T(8,128)(2,1)S(1)} %get-tuple-element.162.x_ref, bf16[768,1536]{1,0:T(8,128)(2,1)S(1)} %bitcast.171, bf16[1536]{0:T(1024)(128)(2,1)S(1)} %copy-done.4), custom_call_target="tpu_custom_call" | custom-call | tf_op jit(solution)/shard_map/act/pallas_call | solution.py:496
  96.1 3.0 %convolution_convert_fusion.1 = bf16[768,1536]{1,0:T(8,128)(2,1)S(1)} fusion(bf16[1024,768]{1,0:T(8,128)(2,1)S(1)} %join.3.d_out_ref, bf16[1024,1536]{1,0:T(8,128)(2,1)S(1)} %get-tuple-element.207.act_ref), kind=kOutput, calls=%fused_computation.1 | convolution fusion | flops 2417098752 | bytes 7077888 | tf_op jit(solution)/shard_map/fd,fh->dh/dot_general | solution.py:605
  99.2 1.5 collective-permute-start.19
  100.7 1.6 collective-permute-start.20
  102.5 3.6 %act_back.1 = (bf16[1024,1536]{1,0:T(8,128)(2,1)S(1)}, f32[1,1536]{1,0:T(1,128)S(1)}) custom-call(bf16[1024,768]{1,0:T(8,128)(2,1)S(1)} %join.3.d_out_ref, bf16[768,1536]{1,0:T(8,128)(2,1)S(1)} %bitcast.165, bf16[1024,1536]{1,0:T(8,128)(2,1)S(1)} %get-tuple-element.177.slope_ref), custom_call_target="tpu_custom_call" | custom-call | tf_op jit(solution)/shard_map/act_back/pallas_call | solution.py:511
  106.1 2.6 %convolution_convert_fusion.4.mine_ref = bf16[1024,768]{1,0:T(8,128)(2,1)S(1)} fusion(bf16[1024,1536]{1,0:T(8,128)(2,1)S(1)} %get-tuple-element.183, bf16[768,1536]{1,0:T(8,128)(2,1)S(1)} %bitcast.172), kind=kOutput, calls=%fused_computation.5 | convolution fusion | flops 2416705536 | bytes 7077888 | tf_op jit(solution)/shard_map/fh,dh->fd/dot_general | solution.py:605
  110.8 3.0 %convolution_convert_fusion = bf16[768,1536]{1,0:T(8,128)(2,1)S(1)} fusion(bf16[1024,768]{1,0:T(8,128)(2,1)S(1)} %get-tuple-element.162.x_ref, bf16[1024,1536]{1,0:T(8,128)(2,1)S(1)} %get-tuple-element.183), kind=kOutput, calls=%fused_computation | convolution fusion | flops 2417098752 | bytes 7077888 | tf_op jit(solution)/shard_map/fd,fh->dh/dot_general | solution.py:605
  113.8 2.7 %mid_norm_back.1 = (bf16[1024,768]{1,0:T(8,128)(2,1)S(1)}, f32[512,768]{1,0:T(8,128)S(1)}, f32[4,768]{1,0:T(4,128)S(1)}) custom-call(bf16[1024,768]{1,0:T(8,128)(2,1)S(1)} %convolution_convert_fusion.4.mine_ref, f32[1024,768]{1,0:T(8,128)S(1)} %get-tuple-element.149.hidden_ref, bf16[1024,768]{1,0:T(8,128)(2,1)S(1)} %join.3.d_out_ref, ...), custom_call_target="tpu_custom_call" | custom-call | tf_op jit(solution)/shard_map/mid_norm_back/pallas_call | solution.py:556
  116.4 1.0 convolution_convert_fusion.5.grad_ref
  117.4 1.0 convolution_convert_fusion.6
  118.8 1.5 collective-permute-start.23
  120.3 1.6 collective-permute-start.24
  122.0 12.5 %attend_back.2 = (bf16[1024,1152]{1,0:T(8,128)(2,1)S(1)}, f32[3,1,384]{2,1,0:T(1,128)S(1)}) custom-call(bf16[1024,1152]{1,0:T(8,128)(2,1)S(1)} %get-tuple-element.146.qkv_ref, f32[3,2,1024]{2,1,0:T(2,128)S(1)} %get-tuple-element.151.lse_ref, bf16[1024,384]{1,0:T(8,128)(2,1)S(1)} %convolution_convert_fusion.5.grad_ref), custom_call_target="tpu_custom_call" | custom-call | tf_op jit(solution)/shard_map/attend_back/pallas_call | solution.py:282
  134.9 0.8 collective-permute-start.27
  137.3 6.1 %attend_back.3 = (bf16[1024,1152]{1,0:T(8,128)(2,1)S(1)}, f32[3,1,384]{2,1,0:T(1,128)S(1)}) custom-call(bf16[1024,1152]{1,0:T(8,128)(2,1)S(1)} %get-tuple-element.146.qkv_ref, f32[3,2,1024]{2,1,0:T(2,128)S(1)} %get-tuple-element.151.lse_ref, bf16[1024,384]{1,0:T(8,128)(2,1)S(1)} %convolution_convert_fusion.5.grad_ref, ...), custom_call_target="tpu_custom_call", output_to_operand_aliasing={{0}: (3, {}), {1}: (4, {})} | custom-call | tf_op jit(solution)/shard_map/attend_back/pallas_call | solution.py:282
  143.4 2.2 %convolution_convert_fusion.2 = bf16[768,1152]{1,0:T(8,128)(2,1)S(1)} fusion(bf16[1024,768]{1,0:T(8,128)(2,1)S(1)} %get-tuple-element.150, bf16[1024,1152]{1,0:T(8,128)(2,1)S(1)} %get-tuple-element.206.d_qkv_ref.qkv_ref), kind=kOutput, calls=%fused_computation.2 | convolution fusion | flops 1812824064 | bytes 5701632 | tf_op jit(solution)/shard_map/fd,fe->de/dot_general | solution.py:605
  145.9 1.5 collective-permute-start.28
  147.4 1.5 collective-permute-start.29
  148.9 1.5 collective-permute-start.32
  150.4 3.7 %last_terms.1 = (bf16[512,768]{1,0:T(8,128)(2,1)S(1)}, bf16[512,768]{1,0:T(8,128)(2,1)S(1)}, f32[512,768]{1,0:T(8,128)S(1)}) custom-call(bf16[1024,1152]{1,0:T(8,128)(2,1)S(1)} %get-tuple-element.206.d_qkv_ref.qkv_ref, bf16[768,1664]{1,0:T(8,128)(2,1)S(1)} %bitcast.163, bf16[1024,1536]{1,0:T(8,128)(2,1)S(1)} %get-tuple-element.207.act_ref, ...), custom_call_target="tpu_custom_call" | custom-call | tf_op jit(solution)/shard_map/last_terms/pallas_call | solution.py:599
  154.1 2.5 %collective-permute-done.32 = bf16[1,48,1536]{2,1,0:T(8,128)(2,1)S(1)} collective-permute-done((bf16[1,48,1536]{2,1,0:T(8,128)(2,1)S(1)}, bf16[1,48,1536]{2,1,0:T(8,128)(2,1)S(1)}, u32[]{:S(2)}, u32[]{:S(2)}) %collective-permute-start.32) | collective-permute-done | bytes 147488 | tf_op jit(solution)/shard_map/ppermute | solution.py:44
  156.6 1.2 collective-permute-done.28
  159.5 1.3 collective-permute-start.33
  160.9 1.6 collective-permute-start.34
  163.8 3.1 %first_norm_back.1 = (f32[512,768]{1,0:T(8,128)}, f32[2,768]{1,0:T(2,128)S(1)}) custom-call(bf16[1024,1152]{1,0:T(8,128)(2,1)S(1)} %get-tuple-element.206.d_qkv_ref.qkv_ref, bf16[768,1664]{1,0:T(8,128)(2,1)S(1)} %bitcast.164, bf16[512,768]{1,0:T(8,128)(2,1)S(1)} %bitcast.175, f32[512,768]{1,0:T(8,128)S(1)} %get-tuple-element.223.d_hidden_ref, ...), custom_call_target="tpu_custom_call" | custom-call | tf_op jit(solution)/shard_map/first_norm_back/pallas_call | solution.py:581
  167.5 2.6 %collective-permute-done.33 = bf16[2,48,1920]{2,1,0:T(8,128)(2,1)S(1)} collective-permute-done((bf16[2,48,1920]{2,1,0:T(8,128)(2,1)S(1)}, bf16[2,48,1920]{2,1,0:T(8,128)(2,1)S(1)}, u32[]{:S(2)}, u32[]{:S(2)}) %collective-permute-start.33) | collective-permute-done | bytes 368672 | tf_op jit(solution)/shard_map/ppermute | solution.py:44
  170.2 2.5 %collective-permute-done.34 = bf16[4,48,1152]{2,1,0:T(8,128)(2,1)S(1)} collective-permute-done((bf16[4,48,1152]{2,1,0:T(8,128)(2,1)S(1)}, bf16[4,48,1152]{2,1,0:T(8,128)(2,1)S(1)}, u32[]{:S(2)}, u32[]{:S(2)}) %collective-permute-start.34) | collective-permute-done | bytes 442400 | tf_op jit(solution)/shard_map/ppermute | solution.py:44
  172.8 1.4 collective-permute-done.35
  174.4 0.8 collective-permute-start.39
  175.9 3.5 %collective-permute-done.40 = f32[11,768]{1,0:T(8,128)S(1)} collective-permute-done((f32[11,768]{1,0:T(8,128)S(1)}, f32[11,768]{1,0:T(8,128)S(1)}, u32[]{:S(2)}, u32[]{:S(2)}) %collective-permute-start.40) | collective-permute-done | bytes 33824 | tf_op jit(solution)/shard_map/ppermute | solution.py:44
  180.0 1.4 collective-permute-start.46
  181.4 2.2 %collective-permute-done.41 = f32[11,768]{1,0:T(8,128)S(1)} collective-permute-done((f32[11,768]{1,0:T(8,128)S(1)}, f32[11,768]{1,0:T(8,128)S(1)}, u32[]{:S(2)}, u32[]{:S(2)}) %collective-permute-start.41) | collective-permute-done | bytes 33824 | tf_op jit(solution)/shard_map/ppermute | solution.py:44
  183.7 1.5 collective-permute-start.43
  185.8 1.4 add_bitcast_fusion
  187.2 2.4 %collective-permute-done.44 = f32[11,768]{1,0:T(8,128)S(1)} collective-permute-done((f32[11,768]{1,0:T(8,128)S(1)}, f32[11,768]{1,0:T(8,128)S(1)}, u32[]{:S(2)}, u32[]{:S(2)}) %collective-permute-start.44) | collective-permute-done | bytes 33824 | tf_op jit(solution)/shard_map/ppermute | solution.py:44
  189.6 2.3 %collective-permute-start.45 = (f32[11,768]{1,0:T(8,128)S(1)}, f32[11,768]{1,0:T(8,128)S(1)}, u32[]{:S(2)}, u32[]{:S(2)}) collective-permute-start(f32[11,768]{1,0:T(8,128)S(1)} %add.98.sums_ref), channel_id=1, source_target_pairs={{0,16},{2,18},{4,20},{6,22},{8,24},{10,26},{12,28},{14,30},{16,0},... | collective-permute-start | bytes 101384 | tf_op jit(solution)/shard_map/ppermute | solution.py:44
  191.9 1.1 collective-permute-done.46
  193.0 0.8 finish_mid.1
  193.8 1.5 collective-permute-done.45.sums_got_ref
  (130 shorter events, 18.7 us)
Async XLA Ops:
  0.7 0.9 copy-start.2
  1.6 0.8 copy-start.3
  2.3 0.7 copy-start.6
  3.0 0.7 copy-start.7
  3.8 10.1 %collective-permute-start = (bf16[1,48,1664]{2,1,0:T(8,128)(2,1)S(1)}, bf16[1,48,1664]{2,1,0:T(8,128)(2,1)S(1)}, u32[]{:S(2)}, u32[]{:S(2)}) collective-permute-start(bf16[1,48,1664]{2,1,0:T(8,128)(2,1)S(1)} %bitcast.178), channel_id=1, source_target_pairs={{0,24},{2,26},{4,28},{6,30},{8,16},{10,18},{12,20},{14,22},{16,8},... | collective-permute-start | bytes 479240 | tf_op jit(solution)/shard_map/ppermute | solution.py:44
  8.9 13.5 %collective-permute-start.1 = (bf16[1,48,1664]{2,1,0:T(8,128)(2,1)S(1)}, bf16[1,48,1664]{2,1,0:T(8,128)(2,1)S(1)}, u32[]{:S(2)}, u32[]{:S(2)}) collective-permute-start(bf16[1,48,1664]{2,1,0:T(8,128)(2,1)S(1)} %bitcast.179), channel_id=1, source_target_pairs={{0,16},{2,18},{4,20},{6,22},{8,24},{10,26},{12,28},{14,30},{16,0},... | collective-permute-start | bytes 479240 | tf_op jit(solution)/shard_map/ppermute | solution.py:44
  8.9 13.5 %collective-permute-start.2 = (bf16[1,48,1664]{2,1,0:T(8,128)(2,1)S(1)}, bf16[1,48,1664]{2,1,0:T(8,128)(2,1)S(1)}, u32[]{:S(2)}, u32[]{:S(2)}) collective-permute-start(bf16[1,48,1664]{2,1,0:T(8,128)(2,1)S(1)} %bitcast.180), channel_id=1, source_target_pairs={{0,8},{2,10},{4,12},{6,14},{8,0},{10,2},{12,4},{14,6},{16,24},{18,... | collective-permute-start | bytes 479240 | tf_op jit(solution)/shard_map/ppermute | solution.py:44
  9.5 13.1 %collective-permute-start.3 = (bf16[512,768]{1,0:T(8,128)(2,1)}, bf16[512,768]{1,0:T(8,128)(2,1)S(1)}, u32[]{:S(2)}, u32[]{:S(2)}) collective-permute-start(bf16[512,768]{1,0:T(8,128)(2,1)} %bitcast.173), channel_id=1, source_target_pairs={{0,1},{1,0},{2,3},{3,2},{4,5},{5,4},{6,7},{7,6},{8,9},{9,8},{10,11... | collective-permute-start | bytes 2359304 | tf_op jit(solution)/shard_map/ppermute | solution.py:48
  22.5 15.3 %copy-start = (bf16[1,512,768]{2,1,0:T(8,128)(2,1)S(1)}, bf16[1,512,768]{2,1,0:T(8,128)(2,1)}, u32[]{:S(2)}) copy-start(bf16[1,512,768]{2,1,0:T(8,128)(2,1)} %param.10) | copy-start | bytes 2359300
  22.6 15.0 %collective-permute-start.8 = (bf16[1,48,3072]{2,1,0:T(8,128)(2,1)S(1)}, bf16[1,48,3072]{2,1,0:T(8,128)(2,1)S(1)}, u32[]{:S(2)}, u32[]{:S(2)}) collective-permute-start(bf16[1,48,3072]{2,1,0:T(8,128)(2,1)S(1)} %maximum_bitcast_fusion.2), channel_id=1, source_target_pairs={{0,16},{2,18},{4,20},{6,22},{8,24},{10,26},{12,28},{14,30},{16,0},... | collective-permute-start | bytes 884744 | tf_op jit(solution)/shard_map/ppermute | solution.py:44
  22.7 15.5 %collective-permute-start.4 = (bf16[4,48,1664]{2,1,0:T(8,128)(2,1)S(1)}, bf16[4,48,1664]{2,1,0:T(8,128)(2,1)S(1)}, u32[]{:S(2)}, u32[]{:S(2)}) collective-permute-start(bf16[4,48,1664]{2,1,0:T(8,128)(2,1)S(1)} %maximum_bitcast_fusion.refs_0_), channel_id=1, source_target_pairs={{0,2},{2,0},{4,6},{6,4},{8,10},{10,8},{12,14},{14,12},{16,18},{18,... | collective-permute-start | bytes 1916936 | tf_op jit(solution)/shard_map/ppermute | solution.py:44
  24.3 15.2 %collective-permute-start.5 = (bf16[4,48,1664]{2,1,0:T(8,128)(2,1)S(1)}, bf16[4,48,1664]{2,1,0:T(8,128)(2,1)S(1)}, u32[]{:S(2)}, u32[]{:S(2)}) collective-permute-start(bf16[4,48,1664]{2,1,0:T(8,128)(2,1)S(1)} %maximum_bitcast_fusion.refs_0_), channel_id=1, source_target_pairs={{0,4},{2,6},{4,0},{6,2},{8,12},{10,14},{12,8},{14,10},{16,20},{18,... | collective-permute-start | bytes 1916936 | tf_op jit(solution)/shard_map/ppermute | solution.py:44
  37.7 15.3 %collective-permute-start.9 = (bf16[2,48,3072]{2,1,0:T(8,128)(2,1)S(1)}, bf16[2,48,3072]{2,1,0:T(8,128)(2,1)S(1)}, u32[]{:S(2)}, u32[]{:S(2)}) collective-permute-start(bf16[2,48,3072]{2,1,0:T(8,128)(2,1)S(1)} %maximum_bitcast_fusion.1), channel_id=1, source_target_pairs={{0,8},{2,10},{4,12},{6,14},{8,0},{10,2},{12,4},{14,6},{16,24},{18,... | collective-permute-start | bytes 1769480 | tf_op jit(solution)/shard_map/ppermute | solution.py:44
  39.4 13.9 %collective-permute-start.6 = (bf16[2,48,1664]{2,1,0:T(8,128)(2,1)S(1)}, bf16[2,48,1664]{2,1,0:T(8,128)(2,1)S(1)}, u32[]{:S(2)}, u32[]{:S(2)}) collective-permute-start(bf16[2,48,1664]{2,1,0:T(8,128)(2,1)S(1)} %slice.59), channel_id=1, source_target_pairs={{0,4},{2,6},{4,0},{6,2},{8,12},{10,14},{12,8},{14,10},{16,20},{18,... | collective-permute-start | bytes 958472 | tf_op jit(solution)/shard_map/ppermute | solution.py:44
  41.1 12.3 %collective-permute-start.7 = (bf16[2,48,1664]{2,1,0:T(8,128)(2,1)S(1)}, bf16[2,48,1664]{2,1,0:T(8,128)(2,1)S(1)}, u32[]{:S(2)}, u32[]{:S(2)}) collective-permute-start(bf16[2,48,1664]{2,1,0:T(8,128)(2,1)S(1)} %slice.60), channel_id=1, source_target_pairs={{0,2},{2,0},{4,6},{6,4},{8,10},{10,8},{12,14},{14,12},{16,18},{18,... | collective-permute-start | bytes 958472 | tf_op jit(solution)/shard_map/ppermute | solution.py:44
  53.4 3.3 %copy-start.5 = (bf16[2,384]{1,0:T(2,128)(2,1)S(1)}, bf16[2,384]{1,0:T(2,128)(2,1)}, u32[]{:S(2)}) copy-start(bf16[2,384]{1,0:T(2,128)(2,1)} %bias_ref.2) | copy-start | bytes 4612
  53.4 27.1 %collective-permute-start.12 = (bf16[4,48,3072]{2,1,0:T(8,128)(2,1)S(1)}, bf16[4,48,3072]{2,1,0:T(8,128)(2,1)S(1)}, u32[]{:S(2)}, u32[]{:S(2)}) collective-permute-start(bf16[4,48,3072]{2,1,0:T(8,128)(2,1)S(1)} %bitcast.167), channel_id=1, source_target_pairs={{0,2},{2,0},{4,6},{6,4},{8,10},{10,8},{12,14},{14,12},{16,18},{18,... | collective-permute-start | bytes 3538952 | tf_op jit(solution)/shard_map/ppermute | solution.py:44
  54.9 26.8 %collective-permute-start.13 = (bf16[4,48,3072]{2,1,0:T(8,128)(2,1)S(1)}, bf16[4,48,3072]{2,1,0:T(8,128)(2,1)S(1)}, u32[]{:S(2)}, u32[]{:S(2)}) collective-permute-start(bf16[4,48,3072]{2,1,0:T(8,128)(2,1)S(1)} %bitcast.168), channel_id=1, source_target_pairs={{0,4},{2,6},{4,0},{6,2},{8,12},{10,14},{12,8},{14,10},{16,20},{18,... | collective-permute-start | bytes 3538952 | tf_op jit(solution)/shard_map/ppermute | solution.py:44
  71.2 1.1 copy-start.1
  71.3 2.4 %collective-permute-start.10 = (bf16[512,768]{1,0:T(8,128)(2,1)S(1)}, bf16[512,768]{1,0:T(8,128)(2,1)S(1)}, u32[]{:S(2)}, u32[]{:S(2)}) collective-permute-start(bf16[512,768]{1,0:T(8,128)(2,1)S(1)} %get-tuple-element.271), channel_id=1, source_target_pairs={{0,1},{1,0},{2,3},{3,2},{4,5},{5,4},{6,7},{7,6},{8,9},{9,8},{10,11... | collective-permute-start | bytes 2359304 | tf_op jit(solution)/shard_map/ppermute | solution.py:48
  71.4 3.4 %collective-permute-start.11 = (bf16[512,768]{1,0:T(8,128)(2,1)S(1)}, bf16[512,768]{1,0:T(8,128)(2,1)S(1)}, u32[]{:S(2)}, u32[]{:S(2)}) collective-permute-start(bf16[512,768]{1,0:T(8,128)(2,1)S(1)} %get-tuple-element.270), channel_id=1, source_target_pairs={{0,1},{1,0},{2,3},{3,2},{4,5},{5,4},{6,7},{7,6},{8,9},{9,8},{10,11... | collective-permute-start | bytes 2359304 | tf_op jit(solution)/shard_map/ppermute | solution.py:48
  72.3 4.1 %collective-permute-start.14 = (bf16[512,768]{1,0:T(8,128)(2,1)S(1)}, bf16[512,768]{1,0:T(8,128)(2,1)S(1)}, u32[]{:S(2)}, u32[]{:S(2)}) collective-permute-start(bf16[512,768]{1,0:T(8,128)(2,1)S(1)} %bitcast.176), channel_id=1, source_target_pairs={{0,1},{1,0},{2,3},{3,2},{4,5},{5,4},{6,7},{7,6},{8,9},{9,8},{10,11... | collective-permute-start | bytes 2359304 | tf_op jit(solution)/shard_map/ppermute | solution.py:48
  81.7 6.9 %collective-permute-start.15 = (bf16[2,48,1536]{2,1,0:T(8,128)(2,1)S(1)}, bf16[2,48,1536]{2,1,0:T(8,128)(2,1)S(1)}, u32[]{:S(2)}, u32[]{:S(2)}) collective-permute-start(bf16[2,48,1536]{2,1,0:T(8,128)(2,1)S(1)} %slice.65), channel_id=1, source_target_pairs={{0,4},{2,6},{4,0},{6,2},{8,12},{10,14},{12,8},{14,10},{16,20},{18,... | collective-permute-start | bytes 884744 | tf_op jit(solution)/shard_map/ppermute | solution.py:44
  83.3 6.9 %collective-permute-start.16 = (bf16[2,48,1536]{2,1,0:T(8,128)(2,1)S(1)}, bf16[2,48,1536]{2,1,0:T(8,128)(2,1)S(1)}, u32[]{:S(2)}, u32[]{:S(2)}) collective-permute-start(bf16[2,48,1536]{2,1,0:T(8,128)(2,1)S(1)} %slice.66), channel_id=1, source_target_pairs={{0,2},{2,0},{4,6},{6,4},{8,10},{10,8},{12,14},{14,12},{16,18},{18,... | collective-permute-start | bytes 884744 | tf_op jit(solution)/shard_map/ppermute | solution.py:44
  90.2 8.9 %collective-permute-start.17 = (bf16[2,48,1536]{2,1,0:T(8,128)(2,1)S(1)}, bf16[2,48,1536]{2,1,0:T(8,128)(2,1)S(1)}, u32[]{:S(2)}, u32[]{:S(2)}) collective-permute-start(bf16[2,48,1536]{2,1,0:T(8,128)(2,1)S(1)} %slice.67), channel_id=1, source_target_pairs={{0,4},{2,6},{4,0},{6,2},{8,12},{10,14},{12,8},{14,10},{16,20},{18,... | collective-permute-start | bytes 884744 | tf_op jit(solution)/shard_map/ppermute | solution.py:44
  90.7 0.8 copy-start.4
  90.7 8.4 %collective-permute-start.18 = (bf16[2,48,1536]{2,1,0:T(8,128)(2,1)S(1)}, bf16[2,48,1536]{2,1,0:T(8,128)(2,1)S(1)}, u32[]{:S(2)}, u32[]{:S(2)}) collective-permute-start(bf16[2,48,1536]{2,1,0:T(8,128)(2,1)S(1)} %slice.68), channel_id=1, source_target_pairs={{0,2},{2,0},{4,6},{6,4},{8,10},{10,8},{12,14},{14,12},{16,18},{18,... | collective-permute-start | bytes 884744 | tf_op jit(solution)/shard_map/ppermute | solution.py:44
  99.2 9.6 %collective-permute-start.19 = (bf16[2,48,1536]{2,1,0:T(8,128)(2,1)S(1)}, bf16[2,48,1536]{2,1,0:T(8,128)(2,1)S(1)}, u32[]{:S(2)}, u32[]{:S(2)}) collective-permute-start(bf16[2,48,1536]{2,1,0:T(8,128)(2,1)S(1)} %get-tuple-element.179), channel_id=1, source_target_pairs={{0,2},{2,0},{4,6},{6,4},{8,10},{10,8},{12,14},{14,12},{16,18},{18,... | collective-permute-start | bytes 884744 | tf_op jit(solution)/shard_map/ppermute | solution.py:44
  100.7 8.0 %collective-permute-start.20 = (bf16[2,48,1536]{2,1,0:T(8,128)(2,1)S(1)}, bf16[2,48,1536]{2,1,0:T(8,128)(2,1)S(1)}, u32[]{:S(2)}, u32[]{:S(2)}) collective-permute-start(bf16[2,48,1536]{2,1,0:T(8,128)(2,1)S(1)} %get-tuple-element.180), channel_id=1, source_target_pairs={{0,4},{2,6},{4,0},{6,2},{8,12},{10,14},{12,8},{14,10},{16,20},{18,... | collective-permute-start | bytes 884744 | tf_op jit(solution)/shard_map/ppermute | solution.py:44
  108.9 4.9 %collective-permute-start.21 = (bf16[512,768]{1,0:T(8,128)(2,1)S(1)}, bf16[512,768]{1,0:T(8,128)(2,1)S(1)}, u32[]{:S(2)}, u32[]{:S(2)}) collective-permute-start(bf16[512,768]{1,0:T(8,128)(2,1)S(1)} %get-tuple-element.269), channel_id=1, source_target_pairs={{0,1},{1,0},{2,3},{3,2},{4,5},{5,4},{6,7},{7,6},{8,9},{9,8},{10,11... | collective-permute-start | bytes 2359304 | tf_op jit(solution)/shard_map/ppermute | solution.py:48
  108.9 4.8 %collective-permute-start.22 = (bf16[512,768]{1,0:T(8,128)(2,1)S(1)}, bf16[512,768]{1,0:T(8,128)(2,1)S(1)}, u32[]{:S(2)}, u32[]{:S(2)}) collective-permute-start(bf16[512,768]{1,0:T(8,128)(2,1)S(1)} %get-tuple-element.268), channel_id=1, source_target_pairs={{0,1},{1,0},{2,3},{3,2},{4,5},{5,4},{6,7},{7,6},{8,9},{9,8},{10,11... | collective-permute-start | bytes 2359304 | tf_op jit(solution)/shard_map/ppermute | solution.py:48
  109.7 24.9 %collective-permute-start.25 = (bf16[4,48,1536]{2,1,0:T(8,128)(2,1)S(1)}, bf16[4,48,1536]{2,1,0:T(8,128)(2,1)S(1)}, u32[]{:S(2)}, u32[]{:S(2)}) collective-permute-start(bf16[4,48,1536]{2,1,0:T(8,128)(2,1)S(1)} %pad_maximum_fusion.4), channel_id=1, source_target_pairs={{0,2},{2,0},{4,6},{6,4},{8,10},{10,8},{12,14},{14,12},{16,18},{18,... | collective-permute-start | bytes 1769480 | tf_op jit(solution)/shard_map/ppermute | solution.py:44
  110.3 24.3 %collective-permute-start.26 = (bf16[4,48,1536]{2,1,0:T(8,128)(2,1)S(1)}, bf16[4,48,1536]{2,1,0:T(8,128)(2,1)S(1)}, u32[]{:S(2)}, u32[]{:S(2)}) collective-permute-start(bf16[4,48,1536]{2,1,0:T(8,128)(2,1)S(1)} %pad_maximum_fusion.5), channel_id=1, source_target_pairs={{0,4},{2,6},{4,0},{6,2},{8,12},{10,14},{12,8},{14,10},{16,20},{18,... | collective-permute-start | bytes 1769480 | tf_op jit(solution)/shard_map/ppermute | solution.py:44
  118.8 15.8 %collective-permute-start.23 = (bf16[2,48,1920]{2,1,0:T(8,128)(2,1)S(1)}, bf16[2,48,1920]{2,1,0:T(8,128)(2,1)S(1)}, u32[]{:S(2)}, u32[]{:S(2)}) collective-permute-start(bf16[2,48,1920]{2,1,0:T(8,128)(2,1)S(1)} %get-tuple-element.187), channel_id=1, source_target_pairs={{0,2},{2,0},{4,6},{6,4},{8,10},{10,8},{12,14},{14,12},{16,18},{18,... | collective-permute-start | bytes 1105928 | tf_op jit(solution)/shard_map/ppermute | solution.py:44
  120.3 14.3 %collective-permute-start.24 = (bf16[2,48,1920]{2,1,0:T(8,128)(2,1)S(1)}, bf16[2,48,1920]{2,1,0:T(8,128)(2,1)S(1)}, u32[]{:S(2)}, u32[]{:S(2)}) collective-permute-start(bf16[2,48,1920]{2,1,0:T(8,128)(2,1)S(1)} %get-tuple-element.188), channel_id=1, source_target_pairs={{0,4},{2,6},{4,0},{6,2},{8,12},{10,14},{12,8},{14,10},{16,20},{18,... | collective-permute-start | bytes 1105928 | tf_op jit(solution)/shard_map/ppermute | solution.py:44
  134.9 10.9 %collective-permute-start.27 = (bf16[2,48,1536]{2,1,0:T(8,128)(2,1)S(1)}, bf16[2,48,1536]{2,1,0:T(8,128)(2,1)S(1)}, u32[]{:S(2)}, u32[]{:S(2)}) collective-permute-start(bf16[2,48,1536]{2,1,0:T(8,128)(2,1)S(1)} %fusion.9), channel_id=1, source_target_pairs={{0,8},{2,10},{4,12},{6,14},{8,0},{10,2},{12,4},{14,6},{16,24},{18,... | collective-permute-start | bytes 884744 | tf_op jit(solution)/shard_map/ppermute | solution.py:44
  136.0 22.3 %collective-permute-start.30 = (bf16[4,48,1920]{2,1,0:T(8,128)(2,1)S(1)}, bf16[4,48,1920]{2,1,0:T(8,128)(2,1)S(1)}, u32[]{:S(2)}, u32[]{:S(2)}) collective-permute-start(bf16[4,48,1920]{2,1,0:T(8,128)(2,1)S(1)} %pad_maximum_fusion.2), channel_id=1, source_target_pairs={{0,2},{2,0},{4,6},{6,4},{8,10},{10,8},{12,14},{14,12},{16,18},{18,... | collective-permute-start | bytes 2211848 | tf_op jit(solution)/shard_map/ppermute | solution.py:44
  136.7 21.6 %collective-permute-start.31 = (bf16[4,48,1920]{2,1,0:T(8,128)(2,1)S(1)}, bf16[4,48,1920]{2,1,0:T(8,128)(2,1)S(1)}, u32[]{:S(2)}, u32[]{:S(2)}) collective-permute-start(bf16[4,48,1920]{2,1,0:T(8,128)(2,1)S(1)} %pad_maximum_fusion.3), channel_id=1, source_target_pairs={{0,4},{2,6},{4,0},{6,2},{8,12},{10,14},{12,8},{14,10},{16,20},{18,... | collective-permute-start | bytes 2211848 | tf_op jit(solution)/shard_map/ppermute | solution.py:44
  145.9 11.9 %collective-permute-start.28 = (bf16[2,48,1152]{2,1,0:T(8,128)(2,1)S(1)}, bf16[2,48,1152]{2,1,0:T(8,128)(2,1)S(1)}, u32[]{:S(2)}, u32[]{:S(2)}) collective-permute-start(bf16[2,48,1152]{2,1,0:T(8,128)(2,1)S(1)} %get-tuple-element.202), channel_id=1, source_target_pairs={{0,2},{2,0},{4,6},{6,4},{8,10},{10,8},{12,14},{14,12},{16,18},{18,... | collective-permute-start | bytes 663560 | tf_op jit(solution)/shard_map/ppermute | solution.py:44
  147.4 10.9 %collective-permute-start.29 = (bf16[2,48,1152]{2,1,0:T(8,128)(2,1)S(1)}, bf16[2,48,1152]{2,1,0:T(8,128)(2,1)S(1)}, u32[]{:S(2)}, u32[]{:S(2)}) collective-permute-start(bf16[2,48,1152]{2,1,0:T(8,128)(2,1)S(1)} %get-tuple-element.203), channel_id=1, source_target_pairs={{0,4},{2,6},{4,0},{6,2},{8,12},{10,14},{12,8},{14,10},{16,20},{18,... | collective-permute-start | bytes 663560 | tf_op jit(solution)/shard_map/ppermute | solution.py:44
  148.9 7.7 %collective-permute-start.32 = (bf16[1,48,1536]{2,1,0:T(8,128)(2,1)S(1)}, bf16[1,48,1536]{2,1,0:T(8,128)(2,1)S(1)}, u32[]{:S(2)}, u32[]{:S(2)}) collective-permute-start(bf16[1,48,1536]{2,1,0:T(8,128)(2,1)S(1)} %dynamic-slice_convert_fusion.1), channel_id=1, source_target_pairs={{0,16},{2,18},{4,20},{6,22},{8,24},{10,26},{12,28},{14,30},{16,0},... | collective-permute-start | bytes 442376 | tf_op jit(solution)/shard_map/ppermute | solution.py:44
  158.6 5.2 %collective-permute-start.36 = (bf16[256,768]{1,0:T(8,128)(2,1)S(1)}, bf16[256,768]{1,0:T(8,128)(2,1)S(1)}, u32[]{:S(2)}, u32[]{:S(2)}) collective-permute-start(bf16[256,768]{1,0:T(8,128)(2,1)S(1)} %get-tuple-element.275), channel_id=1, source_target_pairs={{0,1},{1,0},{2,3},{3,2},{4,5},{5,4},{6,7},{7,6},{8,9},{9,8},{10,11... | collective-permute-start | bytes 1179656 | tf_op jit(solution)/shard_map/ppermute | solution.py:48
  158.7 5.2 %collective-permute-start.37 = (bf16[256,768]{1,0:T(8,128)(2,1)S(1)}, bf16[256,768]{1,0:T(8,128)(2,1)S(1)}, u32[]{:S(2)}, u32[]{:S(2)}) collective-permute-start(bf16[256,768]{1,0:T(8,128)(2,1)S(1)} %get-tuple-element.274), channel_id=1, source_target_pairs={{0,1},{1,0},{2,3},{3,2},{4,5},{5,4},{6,7},{7,6},{8,9},{9,8},{10,11... | collective-permute-start | bytes 1179656 | tf_op jit(solution)/shard_map/ppermute | solution.py:48
  159.5 10.6 %collective-permute-start.33 = (bf16[2,48,1920]{2,1,0:T(8,128)(2,1)S(1)}, bf16[2,48,1920]{2,1,0:T(8,128)(2,1)S(1)}, u32[]{:S(2)}, u32[]{:S(2)}) collective-permute-start(bf16[2,48,1920]{2,1,0:T(8,128)(2,1)S(1)} %fusion.8), channel_id=1, source_target_pairs={{0,8},{2,10},{4,12},{6,14},{8,0},{10,2},{12,4},{14,6},{16,24},{18,... | collective-permute-start | bytes 1105928 | tf_op jit(solution)/shard_map/ppermute | solution.py:44
  160.9 11.9 %collective-permute-start.34 = (bf16[4,48,1152]{2,1,0:T(8,128)(2,1)S(1)}, bf16[4,48,1152]{2,1,0:T(8,128)(2,1)S(1)}, u32[]{:S(2)}, u32[]{:S(2)}) collective-permute-start(bf16[4,48,1152]{2,1,0:T(8,128)(2,1)S(1)} %pad_maximum_fusion.6), channel_id=1, source_target_pairs={{0,2},{2,0},{4,6},{6,4},{8,10},{10,8},{12,14},{14,12},{16,18},{18,... | collective-permute-start | bytes 1327112 | tf_op jit(solution)/shard_map/ppermute | solution.py:44
  162.4 11.8 %collective-permute-start.35 = (bf16[4,48,1152]{2,1,0:T(8,128)(2,1)S(1)}, bf16[4,48,1152]{2,1,0:T(8,128)(2,1)S(1)}, u32[]{:S(2)}, u32[]{:S(2)}) collective-permute-start(bf16[4,48,1152]{2,1,0:T(8,128)(2,1)S(1)} %pad_maximum_fusion.7), channel_id=1, source_target_pairs={{0,4},{2,6},{4,0},{6,2},{8,12},{10,14},{12,8},{14,10},{16,20},{18,... | collective-permute-start | bytes 1327112 | tf_op jit(solution)/shard_map/ppermute | solution.py:44
  163.8 19.8 %collective-permute-start.42 = (bf16[512,768]{1,0:T(8,128)(2,1)S(1)}, bf16[512,768]{1,0:T(8,128)(2,1)S(1)}, u32[]{:S(2)}, u32[]{:S(2)}) collective-permute-start(bf16[512,768]{1,0:T(8,128)(2,1)S(1)} %get-tuple-element.233), channel_id=1, source_target_pairs={{0,1},{1,0},{2,3},{3,2},{4,5},{5,4},{6,7},{7,6},{8,9},{9,8},{10,11... | collective-permute-start | bytes 2359304 | tf_op jit(solution)/shard_map/ppermute | solution.py:48
  166.9 3.3 %collective-permute-start.38 = (f32[6,768]{1,0:T(8,128)S(1)}, f32[6,768]{1,0:T(8,128)S(1)}, u32[]{:S(2)}, u32[]{:S(2)}) collective-permute-start(f32[6,768]{1,0:T(8,128)S(1)} %pad_maximum_fusion.8), channel_id=1, source_target_pairs={{0,1},{1,0},{2,3},{3,2},{4,5},{5,4},{6,7},{7,6},{8,9},{9,8},{10,11... | collective-permute-start | bytes 55304 | tf_op jit(solution)/shard_map/ppermute | solution.py:48
  174.4 9.1 %collective-permute-start.39 = (bf16[2,48,1152]{2,1,0:T(8,128)(2,1)S(1)}, bf16[2,48,1152]{2,1,0:T(8,128)(2,1)S(1)}, u32[]{:S(2)}, u32[]{:S(2)}) collective-permute-start(bf16[2,48,1152]{2,1,0:T(8,128)(2,1)S(1)} %fusion.10), channel_id=1, source_target_pairs={{0,8},{2,10},{4,12},{6,14},{8,0},{10,2},{12,4},{14,6},{16,24},{18,... | collective-permute-start | bytes 663560 | tf_op jit(solution)/shard_map/ppermute | solution.py:44
  175.2 4.2 %collective-permute-start.40 = (f32[11,768]{1,0:T(8,128)S(1)}, f32[11,768]{1,0:T(8,128)S(1)}, u32[]{:S(2)}, u32[]{:S(2)}) collective-permute-start(f32[11,768]{1,0:T(8,128)S(1)} %fusion.12), channel_id=1, source_target_pairs={{0,2},{2,0},{4,6},{6,4},{8,10},{10,8},{12,14},{14,12},{16,18},{18,... | collective-permute-start | bytes 101384 | tf_op jit(solution)/shard_map/ppermute | solution.py:44
  179.4 4.2 %collective-permute-start.41 = (f32[11,768]{1,0:T(8,128)S(1)}, f32[11,768]{1,0:T(8,128)S(1)}, u32[]{:S(2)}, u32[]{:S(2)}) collective-permute-start(f32[11,768]{1,0:T(8,128)S(1)} %fusion.15), channel_id=1, source_target_pairs={{0,4},{2,6},{4,0},{6,2},{8,12},{10,14},{12,8},{14,10},{16,20},{18,... | collective-permute-start | bytes 101384 | tf_op jit(solution)/shard_map/ppermute | solution.py:44
  180.0 13.0 %collective-permute-start.46 = (bf16[1,48,1920]{2,1,0:T(8,128)(2,1)S(1)}, bf16[1,48,1920]{2,1,0:T(8,128)(2,1)S(1)}, u32[]{:S(2)}, u32[]{:S(2)}) collective-permute-start(bf16[1,48,1920]{2,1,0:T(8,128)(2,1)S(1)} %dynamic-slice_convert_fusion), channel_id=1, source_target_pairs={{0,16},{2,18},{4,20},{6,22},{8,24},{10,26},{12,28},{14,30},{16,0},... | collective-permute-start | bytes 552968 | tf_op jit(solution)/shard_map/ppermute | solution.py:44
  183.7 11.5 %collective-permute-start.43 = (bf16[1,48,1152]{2,1,0:T(8,128)(2,1)S(1)}, bf16[1,48,1152]{2,1,0:T(8,128)(2,1)S(1)}, u32[]{:S(2)}, u32[]{:S(2)}) collective-permute-start(bf16[1,48,1152]{2,1,0:T(8,128)(2,1)S(1)} %dynamic-slice_convert_fusion.2), channel_id=1, source_target_pairs={{0,16},{2,18},{4,20},{6,22},{8,24},{10,26},{12,28},{14,30},{16,0},... | collective-permute-start | bytes 331784 | tf_op jit(solution)/shard_map/ppermute | solution.py:44
  185.1 4.5 %collective-permute-start.44 = (f32[11,768]{1,0:T(8,128)S(1)}, f32[11,768]{1,0:T(8,128)S(1)}, u32[]{:S(2)}, u32[]{:S(2)}) collective-permute-start(f32[11,768]{1,0:T(8,128)S(1)} %add.92), channel_id=1, source_target_pairs={{0,8},{2,10},{4,12},{6,14},{8,0},{10,2},{12,4},{14,6},{16,24},{18,... | collective-permute-start | bytes 101384 | tf_op jit(solution)/shard_map/ppermute | solution.py:44
  189.6 5.6 %collective-permute-start.45 = (f32[11,768]{1,0:T(8,128)S(1)}, f32[11,768]{1,0:T(8,128)S(1)}, u32[]{:S(2)}, u32[]{:S(2)}) collective-permute-start(f32[11,768]{1,0:T(8,128)S(1)} %add.98.sums_ref), channel_id=1, source_target_pairs={{0,16},{2,18},{4,20},{6,22},{8,24},{10,26},{12,28},{14,30},{16,0},... | collective-permute-start | bytes 101384 | tf_op jit(solution)/shard_map/ppermute | solution.py:44

commit v3 on v2

--- a/solution.py
+++ b/solution.py
@@ -203,23 +203,28 @@
 
 def attend_kernel(qkv_ref, *refs):
     out_ref, lse_ref = refs[-2:]
-    queries = qkv_ref[:, :PAIR]
     keys_all = qkv_ref[:, PAIR : 2 * PAIR] * jnp.asarray(HEAD**-0.5, BF)
     values = qkv_ref[:, 2 * PAIR :]
     first = lax.broadcasted_iota(jnp.int32, (1, PAIR), 1) < HEAD
-    outs, logs = [], []
-    for own in (first, ~first):
-        here = jnp.where(own, queries, jnp.zeros_like(queries))
-        scores = dot(keys_all, here, 1, 1)
-        row_max = jnp.max(scores, axis=0, keepdims=True)
-        powers = jnp.exp(scores - row_max)
-        summed = jnp.sum(powers, axis=0, keepdims=True)
-        probs = (powers * (1.0 / summed)).astype(BF)
-        outs.append(dot(values, probs, 0, 0))
-        logs.append(row_max + jnp.log(summed))
-    both = jnp.concatenate([outs[0][:HEAD], outs[1][HEAD:]], axis=0)
-    out_ref[...] = both.T.astype(BF)
-    lse_ref[...] = jnp.concatenate(logs, axis=0)[None]
+    block = qkv_ref.shape[0] // 2
+
+    @pl.loop(0, 2)
+    def _(i):
+        rows = pl.ds(pl.multiple_of(i * block, block), block)
+        queries = qkv_ref[rows, :PAIR]
+        outs, logs = [], []
+        for own in (first, ~first):
+            here = jnp.where(own, queries, jnp.zeros_like(queries))
+            scores = dot(keys_all, here, 1, 1)
+            row_max = jnp.max(scores, axis=0, keepdims=True)
+            powers = jnp.exp(scores - row_max)
+            summed = jnp.sum(powers, axis=0, keepdims=True)
+            probs = (powers * (1.0 / summed)).astype(BF)
+            outs.append(dot(values, probs, 0, 0))
+            logs.append(row_max + jnp.log(summed))
+        both = jnp.concatenate([outs[0][:HEAD], outs[1][HEAD:]], axis=0)
+        out_ref[rows] = both.T.astype(BF)
+        lse_ref[0, :, rows] = jnp.concatenate(logs, axis=0)
 
 
 def attend(qkv, start, count, kept=()):
@@ -245,42 +250,64 @@
     )(qkv, *kept)
 
 
-def attend_back_kernel(qkv_ref, lse_ref, grad_ref, *refs):
-    out_ref, sum_ref = refs[-2:]
-    factor = jnp.asarray(HEAD**-0.5, BF)
-    queries = qkv_ref[:, :PAIR]
-    keys_small = qkv_ref[:, PAIR : 2 * PAIR] * factor
+def attend_back_kernel(block, qkv_ref, lse_ref, grad_ref, *refs):
+    out_ref, sum_ref, d_keys_ref, d_values_ref = refs[-4:]
+    n = qkv_ref.shape[0]
+    keys_small = qkv_ref[:, PAIR : 2 * PAIR] * jnp.asarray(HEAD**-0.5, BF)
     values = qkv_ref[:, 2 * PAIR :]
-    grad = grad_ref[...]
     first = lax.broadcasted_iota(jnp.int32, (1, PAIR), 1) < HEAD
-    parts = []
-    for own in (first, ~first):
-        q_here = jnp.where(own, queries, jnp.zeros_like(queries))
-        g_here = jnp.where(own, grad, jnp.zeros_like(grad))
-        parts.append((q_here, g_here, dot(keys_small, q_here, 1, 1), dot(values, g_here, 1, 1)))
-    d_q, d_k, d_v = [], [], []
-    for head, (q_here, g_here, scores, d_probs) in enumerate(parts):
-        probs = jnp.exp(scores - lse_ref[0, head : head + 1, :])
-        product = probs * d_probs
-        row_sum = jnp.sum(product, axis=0, keepdims=True)
-        d_scores = (product - probs * row_sum).astype(BF)
-        d_v.append(dot(probs.astype(BF), g_here, 1, 0))
-        d_k.append(dot(d_scores, q_here, 1, 0))
-        d_q.append(dot(keys_small, d_scores, 0, 0))
-    queries_t = jnp.concatenate([d_q[0][:HEAD], d_q[1][HEAD:]], axis=0)
-    d_queries = queries_t.T.astype(BF)
-    d_keys = ((d_k[0] + d_k[1]) * HEAD**-0.5).astype(BF)
-    d_values = (d_v[0] + d_v[1]).astype(BF)
-    for i, x in enumerate((d_queries, d_keys, d_values)):
-        out_ref[:, i * PAIR : (i + 1) * PAIR] = x
-        sum_ref[0, :, i * PAIR : (i + 1) * PAIR] = jnp.sum(x.astype(F32), axis=0, keepdims=True)
-
-
-def attend_back(qkv, lse, grad, start, count, kept=()):
+
+    def chunk(here):
+        queries = qkv_ref[here, :PAIR]
+        grad = grad_ref[here]
+        parts = []
+        for own in (first, ~first):
+            q_here = jnp.where(own, queries, jnp.zeros_like(queries))
+            g_here = jnp.where(own, grad, jnp.zeros_like(grad))
+            parts.append(
+                (q_here, g_here, dot(keys_small, q_here, 1, 1), dot(values, g_here, 1, 1))
+            )
+        d_q, d_k, d_v = [], [], []
+        for head, (q_here, g_here, scores, d_probs) in enumerate(parts):
+            probs = jnp.exp(scores - lse_ref[0, head : head + 1, here])
+            product = probs * d_probs
+            row_sum = jnp.sum(product, axis=0, keepdims=True)
+            d_scores = (product - probs * row_sum).astype(BF)
+            d_v.append(dot(probs.astype(BF), g_here, 1, 0))
+            d_k.append(dot(d_scores, q_here, 1, 0))
+            d_q.append(dot(keys_small, d_scores, 0, 0))
+        queries_t = jnp.concatenate([d_q[0][:HEAD], d_q[1][HEAD:]], axis=0)
+        out_ref[here, :PAIR] = queries_t.T.astype(BF)
+        return d_k[0] + d_k[1], d_v[0] + d_v[1]
+
+    def finish(d_keys, d_values):
+        out_ref[:, PAIR : 2 * PAIR] = (d_keys * HEAD**-0.5).astype(BF)
+        out_ref[:, 2 * PAIR :] = d_values.astype(BF)
+        for i in range(0, 3 * PAIR, PAIR):
+            here = slice(i, i + PAIR)
+            sum_ref[0, :, here] = total_rows(out_ref[:, here].astype(F32))
+
+    if block == n:
+        finish(*chunk(slice(None)))
+        return
+
+    d_keys_ref[...] = jnp.zeros_like(d_keys_ref)
+    d_values_ref[...] = jnp.zeros_like(d_values_ref)
+
+    @pl.loop(0, n // block)
+    def _(i):
+        d_keys, d_values = chunk(pl.ds(pl.multiple_of(i * block, block), block))
+        d_keys_ref[...] += d_keys
+        d_values_ref[...] += d_values
+
+    finish(d_keys_ref[...], d_values_ref[...])
+
+
+def attend_back(qkv, lse, grad, start, count, block, kept=()):
     n, width = qkv.shape
     pairs = width // (3 * PAIR)
     return pl.pallas_call(
-        attend_back_kernel,
+        functools.partial(attend_back_kernel, block),
         grid=(count,),
         in_specs=[
             pl.BlockSpec((n, 3 * PAIR), lambda p: (0, p + start)),
@@ -296,6 +323,7 @@
             jax.ShapeDtypeStruct((n, width), BF),
             jax.ShapeDtypeStruct((pairs, 1, 3 * PAIR), F32),
         ],
+        scratch_shapes=[pltpu.VMEM((n, PAIR), F32)] * 2,
         input_output_aliases={3 + i: i for i in range(len(kept))},
         compiler_params=pltpu.CompilerParams(vmem_limit_bytes=BACK_VMEM),
         cost_estimate=FREE,
@@ -303,10 +331,11 @@
     )(qkv, lse, grad, *kept)
 
 
-def rows_call(kernel, out_shape, name):
+def rows_call(kernel, out_shape, name, scratch=()):
     return pl.pallas_call(
         kernel,
         out_shape=out_shape,
+        scratch_shapes=scratch,
         cost_estimate=FREE,
         compiler_params=pltpu.CompilerParams(vmem_limit_bytes=ROWS_VMEM),
         name=name,
@@ -439,8 +468,7 @@
         normed_ref[here] = normed
         qkv_ref[here] = (dot(normed, weight_ref[:, :width], 1, 0) + bias).astype(BF)
 
-    for i in range(0, x_ref.shape[0], ROW_BLOCK):
-        step(pl.ds(i, ROW_BLOCK))
+    each_block(x_ref.shape[0], step)
 
 
 def project(x, first_full, bias, width):
@@ -480,11 +508,13 @@
     return rows_call(mid_norm_kernel, shapes, "mid_norm")(x, mine, vectors, *others)
 
 
-def act_kernel(x_ref, weight_ref, bias_ref, act_ref, slope_ref):
-    bias = bias_ref[...].astype(F32).reshape(1, bias_ref.shape[0])
-    for start in range(0, act_ref.shape[1], ACT_BLOCK):
-        here = slice(start, start + ACT_BLOCK)
-        pre = dot(x_ref[...], weight_ref[:, here], 1, 0) + bias[:, here]
+def act_kernel(x_ref, weight_ref, bias_ref, act_ref, slope_ref, row_ref):
+    row_ref[...] = bias_ref[...].astype(F32).reshape(1, bias_ref.shape[0])
+
+    @pl.loop(0, act_ref.shape[1] // ACT_BLOCK)
+    def _(i):
+        here = pl.ds(pl.multiple_of(i * ACT_BLOCK, ACT_BLOCK), ACT_BLOCK)
+        pre = dot(x_ref[...], weight_ref[:, here], 1, 0) + row_ref[:, here]
         cdf = 0.5 * (1.0 + lax.erf(pre * 0.5**0.5))
         act_ref[:, here] = (pre * cdf).astype(BF)
         slope = cdf + pre * jnp.exp(-0.5 * pre * pre) * 0.3989422804014327
@@ -493,7 +523,8 @@
 
 def act(x, weight, bias):
     shape = jax.ShapeDtypeStruct((x.shape[0], weight.shape[1]), BF)
-    return rows_call(act_kernel, [shape, shape], "act")(x, weight, bias)
+    scratch = [pltpu.VMEM((1, bias.shape[0]), F32)]
+    return rows_call(act_kernel, [shape, shape], "act", scratch)(x, weight, bias)
 
 
 def act_back_kernel(d_out_ref, weight_ref, slope_ref, d_pre_ref, sums_ref):
@@ -561,18 +592,18 @@
 def first_norm_back_kernel(
     qkv_ref, weight_ref, x_ref, d_hidden_ref, vectors_ref, first_ref, second_ref, grad_ref, sums_ref
 ):
-    sums = [jnp.zeros((1, x_ref.shape[1]), F32)] * 2
     width = qkv_ref.shape[1]
-    rows = first_ref.shape[0]
-    for i in range(x_ref.shape[0] // ROW_BLOCK):
-        here = pl.ds(i * ROW_BLOCK, ROW_BLOCK)
-        other_ref = (first_ref, second_ref)[i * ROW_BLOCK // rows]
-        other = other_ref[pl.ds(i * ROW_BLOCK % rows, ROW_BLOCK)].astype(F32)
+    sums_ref[...] = jnp.zeros_like(sums_ref)
+
+    @pl.loop(0, x_ref.shape[0] // ROW_BLOCK)
+    def _(i):
+        here = pl.ds(pl.multiple_of(i * ROW_BLOCK, ROW_BLOCK), ROW_BLOCK)
+        other = jnp.where(i == 0, first_ref[...], second_ref[...]).astype(F32)
         grad = dot(qkv_ref[here], weight_ref[:, :width], 1, 1) + other
         unit, inv_std = standardized(x_ref[here].astype(F32))
         grad_ref[here] = d_hidden_ref[here] + norm_back(unit, inv_std, vectors_ref[0:1], grad)
-        sums = [a + total_rows(b) for a, b in zip(sums, (grad * unit, grad))]
-    sums_ref[...] = jnp.concatenate(sums, axis=0)
+        sums_ref[0:1] += total_rows(grad * unit)
+        sums_ref[1:2] += total_rows(grad)
 
 
 def first_norm_back(d_qkv, first_full, others, x, d_hidden, vectors):
@@ -586,11 +617,16 @@
 def last_terms_kernel(d_qkv_ref, first_ref, act_ref, end_ref, d_other_ref, other_ref, mine_ref):
     half, columns = mine_ref.shape
     width = d_qkv_ref.shape[1]
-    there = pl.ds(half, half)
-    d_other = dot(d_qkv_ref[there], first_ref[:, :width], 1, 1)
-    d_other_ref[...] = d_other.astype(BF)
-    other_ref[...] = dot(act_ref[there], end_ref[...], 1, 1).astype(BF)
-    mine_ref[...] = dot(act_ref[pl.ds(0, half)], end_ref[...], 1, 1)
+    others = pl.ds(half, half)
+    d_qkv, act_other = d_qkv_ref.at[others], act_ref.at[others]
+
+    def step(here):
+        d_other = dot(d_qkv[here], first_ref[:, :width], 1, 1)
+        d_other_ref[here] = d_other.astype(BF)
+        other_ref[here] = dot(act_other[here], end_ref[...], 1, 1).astype(BF)
+        mine_ref[here] = dot(act_ref[here], end_ref[...], 1, 1)
+
+    each_block(half, step)
 
 
 def last_terms(d_qkv, first_full, hidden_act, end_full):
@@ -689,12 +725,12 @@
 
     d_attended, mid_ops = stage(d_attended, mid_ops)
     mid_far = scatter_low_across(mid_ops)
-    d_proj = attend_back(qkv, log_sums, d_attended, 0, pairs - 1)
+    d_proj = attend_back(qkv, log_sums, d_attended, 0, pairs - 1, 2 * half)
 
     d_proj, mid_far, fc2_near = stage(d_proj, mid_far, fc2_near)
     mid_near = scatter_low_near(near_operands(mid_parts, mid_far))
     fc2_sum = scatter_high_step(high_operands(total_of(fc2_near), 0, at), 0)
-    d_qkv, d_sums = attend_back(qkv, log_sums, d_attended, pairs - 1, 1, d_proj)
+    d_qkv, d_sums = attend_back(qkv, log_sums, d_attended, pairs - 1, 1, half, d_proj)
     qkv_grad = mm("fd,fe->de", normed_all, d_qkv).astype(BF)
     qkv_parts, qkv_ops = scatter_operands(qkv_grad, at)
 

time: 200 us -> 196 us (0.980); the launches traced: 196 us -> 196 us
  waiting for transfers between devices: 72 us -> 67.1 us
  Pallas kernels: 54.3 us -> 59 us
    ppermute x37, waiting for transfers between devices: 69.6 us -> 64.6 us  [swap_dp(): return lax.ppermute(x, 'dp', [(i, i ^ step) for i in range(n)])]
    pallas_call x1, Pallas kernels: 10.7 us -> 13.2 us  [attend(): pl.pallas_call(attend_kernel, grid=(count,), in_specs=[pl.BlockSpec((n, 3...]
  transfers between devices with their start and end apart: 47 -> 47, of which waited for: 23 -> 23; matrix products, arithmetic and copies ran while one was open for 10% -> 10% of each run, Pallas kernels for 27% -> 30%
where the time goes in v3:
time: 196 us
  waiting for transfers between devices  67.1 us (34%)
  Pallas kernels  59 us (30%)
  starting transfers between devices  45.2 us (23%)
  matrix products  13.8 us (7%)
  other arithmetic  4.83 us (2%)
  local copies, waits for them, and re-layouts  4.64 us (2%)
    ppermute x37, waiting for transfers between devices, swap_dp(): return lax.ppermute(x, 'dp', [(i, i ^ step) for i in range(n)])  64.6 us
    ppermute x37, starting transfers between devices, swap_dp(): return lax.ppermute(x, 'dp', [(i, i ^ step) for i in range(n)])  42.9 us
    pallas_call x2, Pallas kernels, attend_back(): pl.pallas_call(functools.partial(attend_back_kernel, block), grid=(count,...  19.5 us
    dot_general x7, matrix products, mm(): return jnp.einsum(spec, a, b, preferred_element_type=F32)  13.8 us
    pallas_call x1, Pallas kernels, attend(): pl.pallas_call(attend_kernel, grid=(count,), in_specs=[pl.BlockSpec((n, 3...  13.2 us
    pallas_call x1, Pallas kernels, act(): rows_call(act_kernel, [shape, shape], 'act', scratch)(x, weight, bias)  4.97 us
  transfers between devices with their start and end apart: 47, of which 23 were waited for; matrix products, arithmetic and copies ran while one was open for 10% of the time, Pallas kernels for 30%

profile of v3, /device:TPU:0, one launch (start us, length us, event | category | flops | bytes accessed | tf_op | source)
XLA Modules:
  0.0 195.9 jit_solution(17496684193888728526)
XLA Ops:
  0.7 0.9 copy-done.2
  3.8 5.1 %collective-permute-start = (bf16[1,48,1664]{2,1,0:T(8,128)(2,1)S(1)}, bf16[1,48,1664]{2,1,0:T(8,128)(2,1)S(1)}, u32[]{:S(2)}, u32[]{:S(2)}) collective-permute-start(bf16[1,48,1664]{2,1,0:T(8,128)(2,1)S(1)} %bitcast.178), channel_id=1, source_target_pairs={{0,24},{2,26},{4,28},{6,30},{8,16},{10,18},{12,20},{14,22},{16,8},... | collective-permute-start | bytes 479240 | tf_op jit(solution)/shard_map/ppermute | solution.py:44
  9.5 1.0 maximum_bitcast_fusion.2
  10.5 3.4 %collective-permute-done = bf16[1,48,1664]{2,1,0:T(8,128)(2,1)S(1)} collective-permute-done((bf16[1,48,1664]{2,1,0:T(8,128)(2,1)S(1)}, bf16[1,48,1664]{2,1,0:T(8,128)(2,1)S(1)}, u32[]{:S(2)}, u32[]{:S(2)}) %collective-permute-start) | collective-permute-done | bytes 159776 | tf_op jit(solution)/shard_map/ppermute | solution.py:44
  13.9 8.5 %collective-permute-done.1 = bf16[1,48,1664]{2,1,0:T(8,128)(2,1)S(1)} collective-permute-done((bf16[1,48,1664]{2,1,0:T(8,128)(2,1)S(1)}, bf16[1,48,1664]{2,1,0:T(8,128)(2,1)S(1)}, u32[]{:S(2)}, u32[]{:S(2)}) %collective-permute-start.1) | collective-permute-done | bytes 159776 | tf_op jit(solution)/shard_map/ppermute | solution.py:44
  22.7 1.6 collective-permute-start.4
  24.3 1.5 collective-permute-start.5
  25.8 11.8 %collective-permute-done.8 = bf16[1,48,3072]{2,1,0:T(8,128)(2,1)S(1)} collective-permute-done((bf16[1,48,3072]{2,1,0:T(8,128)(2,1)S(1)}, bf16[1,48,3072]{2,1,0:T(8,128)(2,1)S(1)}, u32[]{:S(2)}, u32[]{:S(2)}) %collective-permute-start.8) | collective-permute-done | bytes 294944 | tf_op jit(solution)/shard_map/ppermute | solution.py:44
  38.2 1.2 collective-permute-done.5.refs_2_
  39.4 1.6 collective-permute-start.6
  41.7 11.4 %collective-permute-done.9 = bf16[2,48,3072]{2,1,0:T(8,128)(2,1)S(1)} collective-permute-done((bf16[2,48,3072]{2,1,0:T(8,128)(2,1)S(1)}, bf16[2,48,3072]{2,1,0:T(8,128)(2,1)S(1)}, u32[]{:S(2)}, u32[]{:S(2)}) %collective-permute-start.9) | collective-permute-done | bytes 589856 | tf_op jit(solution)/shard_map/ppermute | solution.py:44
  53.4 1.6 collective-permute-start.12
  54.9 1.5 collective-permute-start.13
  56.6 3.7 %project.1 = (bf16[1024,768]{1,0:T(8,128)(2,1)S(1)}, bf16[1024,1152]{1,0:T(8,128)(2,1)S(1)}, f32[8,768]{1,0:T(8,128)S(1)}) custom-call(bf16[1024,768]{1,0:T(8,128)(2,1)S(1)} %join.2.x_ref, bf16[768,1664]{1,0:T(8,128)(2,1)S(1)} %bitcast.160, bf16[2,384]{1,0:T(2,128)(2,1)S(1)} %copy-done.5), custom_call_target="tpu_custom_call" | custom-call | tf_op jit(solution)/shard_map/project/pallas_call | solution.py:481
  60.4 13.2 %attend.1 = (bf16[1024,384]{1,0:T(8,128)(2,1)S(1)}, f32[3,2,1024]{2,1,0:T(2,128)S(1)}) custom-call(bf16[1024,1152]{1,0:T(8,128)(2,1)S(1)} %get-tuple-element.146.qkv_ref), custom_call_target="tpu_custom_call" | custom-call | tf_op jit(solution)/shard_map/attend/pallas_call | solution.py:233
  73.6 1.0 convolution_convert_fusion.3.mine_ref
  75.8 1.3 collective-permute-done.10.refs_0_
  77.1 1.1 collective-permute-done.11.refs_1_
  78.2 1.6 mid_norm.1
  80.5 1.2 collective-permute-done.13.refs_2_
  81.7 1.6 collective-permute-start.15
  84.0 5.0 %collective-permute-done.15.refs_3_ = bf16[2,48,1536]{2,1,0:T(8,128)(2,1)S(1)} collective-permute-done((bf16[2,48,1536]{2,1,0:T(8,128)(2,1)S(1)}, bf16[2,48,1536]{2,1,0:T(8,128)(2,1)S(1)}, u32[]{:S(2)}, u32[]{:S(2)}) %collective-permute-start.15) | collective-permute-done | bytes 294944 | tf_op jit(solution)/shard_map/ppermute | solution.py:44
  89.0 1.1 collective-permute-done.16.refs_4_
  90.1 0.8 collective-permute-start.17
  91.7 5.0 %act.1 = (bf16[1024,1536]{1,0:T(8,128)(2,1)S(1)}, bf16[1024,1536]{1,0:T(8,128)(2,1)S(1)}) custom-call(bf16[1024,768]{1,0:T(8,128)(2,1)S(1)} %get-tuple-element.162.x_ref, bf16[768,1536]{1,0:T(8,128)(2,1)S(1)} %bitcast.171, bf16[1536]{0:T(1024)(128)(2,1)S(1)} %copy-done.4), custom_call_target="tpu_custom_call" | custom-call | tf_op jit(solution)/shard_map/act/pallas_call | solution.py:527
  96.7 3.0 %convolution_convert_fusion.1 = bf16[768,1536]{1,0:T(8,128)(2,1)S(1)} fusion(bf16[1024,768]{1,0:T(8,128)(2,1)S(1)} %join.3.d_out_ref, bf16[1024,1536]{1,0:T(8,128)(2,1)S(1)} %get-tuple-element.207.act_ref), kind=kOutput, calls=%fused_computation.1 | convolution fusion | flops 2417098752 | bytes 7077888 | tf_op jit(solution)/shard_map/fd,fh->dh/dot_general | solution.py:641
  99.8 1.5 collective-permute-start.19
  101.3 1.3 collective-permute-start.20
  102.8 3.2 %act_back.1 = (bf16[1024,1536]{1,0:T(8,128)(2,1)S(1)}, f32[1,1536]{1,0:T(1,128)S(1)}) custom-call(bf16[1024,768]{1,0:T(8,128)(2,1)S(1)} %join.3.d_out_ref, bf16[768,1536]{1,0:T(8,128)(2,1)S(1)} %bitcast.165, bf16[1024,1536]{1,0:T(8,128)(2,1)S(1)} %get-tuple-element.177.slope_ref), custom_call_target="tpu_custom_call" | custom-call | tf_op jit(solution)/shard_map/act_back/pallas_call | solution.py:542
  106.0 2.6 %convolution_convert_fusion.4.mine_ref = bf16[1024,768]{1,0:T(8,128)(2,1)S(1)} fusion(bf16[1024,1536]{1,0:T(8,128)(2,1)S(1)} %get-tuple-element.183, bf16[768,1536]{1,0:T(8,128)(2,1)S(1)} %bitcast.172), kind=kOutput, calls=%fused_computation.5 | convolution fusion | flops 2416705536 | bytes 7077888 | tf_op jit(solution)/shard_map/fh,dh->fd/dot_general | solution.py:641
  111.0 3.0 %convolution_convert_fusion = bf16[768,1536]{1,0:T(8,128)(2,1)S(1)} fusion(bf16[1024,768]{1,0:T(8,128)(2,1)S(1)} %get-tuple-element.162.x_ref, bf16[1024,1536]{1,0:T(8,128)(2,1)S(1)} %get-tuple-element.183), kind=kOutput, calls=%fused_computation | convolution fusion | flops 2417098752 | bytes 7077888 | tf_op jit(solution)/shard_map/fd,fh->dh/dot_general | solution.py:641
  114.0 2.7 %mid_norm_back.1 = (bf16[1024,768]{1,0:T(8,128)(2,1)S(1)}, f32[512,768]{1,0:T(8,128)S(1)}, f32[4,768]{1,0:T(4,128)S(1)}) custom-call(bf16[1024,768]{1,0:T(8,128)(2,1)S(1)} %convolution_convert_fusion.4.mine_ref, f32[1024,768]{1,0:T(8,128)S(1)} %get-tuple-element.149.hidden_ref, bf16[1024,768]{1,0:T(8,128)(2,1)S(1)} %join.3.d_out_ref, ...), custom_call_target="tpu_custom_call" | custom-call | tf_op jit(solution)/shard_map/mid_norm_back/pallas_call | solution.py:587
  116.7 1.0 convolution_convert_fusion.5.grad_ref
  117.6 1.0 convolution_convert_fusion.6
  119.0 1.5 collective-permute-start.23
  120.5 1.3 collective-permute-start.24
  121.9 12.5 %attend_back.2 = (bf16[1024,1152]{1,0:T(8,128)(2,1)S(1)}, f32[3,1,384]{2,1,0:T(1,128)S(1)}) custom-call(bf16[1024,1152]{1,0:T(8,128)(2,1)S(1)} %get-tuple-element.146.qkv_ref, f32[3,2,1024]{2,1,0:T(2,128)S(1)} %get-tuple-element.151.lse_ref, bf16[1024,384]{1,0:T(8,128)(2,1)S(1)} %convolution_convert_fusion.5.grad_ref), custom_call_target="tpu_custom_call" | custom-call | tf_op jit(solution)/shard_map/attend_back/pallas_call | solution.py:309
  134.8 0.9 collective-permute-start.27
  137.4 7.0 %attend_back.3 = (bf16[1024,1152]{1,0:T(8,128)(2,1)S(1)}, f32[3,1,384]{2,1,0:T(1,128)S(1)}) custom-call(bf16[1024,1152]{1,0:T(8,128)(2,1)S(1)} %get-tuple-element.146.qkv_ref, f32[3,2,1024]{2,1,0:T(2,128)S(1)} %get-tuple-element.151.lse_ref, bf16[1024,384]{1,0:T(8,128)(2,1)S(1)} %convolution_convert_fusion.5.grad_ref, ...), custom_call_target="tpu_custom_call", output_to_operand_aliasing={{0}: (3, {}), {1}: (4, {})} | custom-call | tf_op jit(solution)/shard_map/attend_back/pallas_call | solution.py:309
  144.4 2.2 %convolution_convert_fusion.2 = bf16[768,1152]{1,0:T(8,128)(2,1)S(1)} fusion(bf16[1024,768]{1,0:T(8,128)(2,1)S(1)} %get-tuple-element.150, bf16[1024,1152]{1,0:T(8,128)(2,1)S(1)} %get-tuple-element.206.d_qkv_ref.qkv_ref), kind=kOutput, calls=%fused_computation.2 | convolution fusion | flops 1812824064 | bytes 5701632 | tf_op jit(solution)/shard_map/fd,fe->de/dot_general | solution.py:641
  146.9 1.5 collective-permute-start.28
  148.4 1.3 collective-permute-start.29
  149.8 1.4 collective-permute-start.32
  151.1 3.9 %last_terms.1 = (bf16[512,768]{1,0:T(8,128)(2,1)S(1)}, bf16[512,768]{1,0:T(8,128)(2,1)S(1)}, f32[512,768]{1,0:T(8,128)S(1)}) custom-call(bf16[1024,1152]{1,0:T(8,128)(2,1)S(1)} %get-tuple-element.206.d_qkv_ref.qkv_ref, bf16[768,1664]{1,0:T(8,128)(2,1)S(1)} %bitcast.163, bf16[1024,1536]{1,0:T(8,128)(2,1)S(1)} %get-tuple-element.207.act_ref, ...), custom_call_target="tpu_custom_call" | custom-call | tf_op jit(solution)/shard_map/last_terms/pallas_call | solution.py:635
  155.0 2.4 %collective-permute-done.32 = bf16[1,48,1536]{2,1,0:T(8,128)(2,1)S(1)} collective-permute-done((bf16[1,48,1536]{2,1,0:T(8,128)(2,1)S(1)}, bf16[1,48,1536]{2,1,0:T(8,128)(2,1)S(1)}, u32[]{:S(2)}, u32[]{:S(2)}) %collective-permute-start.32) | collective-permute-done | bytes 147488 | tf_op jit(solution)/shard_map/ppermute | solution.py:44
  159.5 1.3 collective-permute-start.33
  160.8 1.5 collective-permute-start.34
  163.8 3.3 %first_norm_back.1 = (f32[512,768]{1,0:T(8,128)}, f32[2,768]{1,0:T(2,128)S(1)}) custom-call(bf16[1024,1152]{1,0:T(8,128)(2,1)S(1)} %get-tuple-element.206.d_qkv_ref.qkv_ref, bf16[768,1664]{1,0:T(8,128)(2,1)S(1)} %bitcast.164, bf16[512,768]{1,0:T(8,128)(2,1)S(1)} %bitcast.175, f32[512,768]{1,0:T(8,128)S(1)} %get-tuple-element.223.d_hidden_ref, ...), custom_call_target="tpu_custom_call" | custom-call | tf_op jit(solution)/shard_map/first_norm_back/pallas_call | solution.py:612
  167.6 2.5 %collective-permute-done.33 = bf16[2,48,1920]{2,1,0:T(8,128)(2,1)S(1)} collective-permute-done((bf16[2,48,1920]{2,1,0:T(8,128)(2,1)S(1)}, bf16[2,48,1920]{2,1,0:T(8,128)(2,1)S(1)}, u32[]{:S(2)}, u32[]{:S(2)}) %collective-permute-start.33) | collective-permute-done | bytes 368672 | tf_op jit(solution)/shard_map/ppermute | solution.py:44
  170.2 2.5 %collective-permute-done.34 = bf16[4,48,1152]{2,1,0:T(8,128)(2,1)S(1)} collective-permute-done((bf16[4,48,1152]{2,1,0:T(8,128)(2,1)S(1)}, bf16[4,48,1152]{2,1,0:T(8,128)(2,1)S(1)}, u32[]{:S(2)}, u32[]{:S(2)}) %collective-permute-start.34) | collective-permute-done | bytes 442400 | tf_op jit(solution)/shard_map/ppermute | solution.py:44
  172.7 1.2 collective-permute-done.35
  174.1 0.9 collective-permute-start.39
  175.7 3.5 %collective-permute-done.40 = f32[11,768]{1,0:T(8,128)S(1)} collective-permute-done((f32[11,768]{1,0:T(8,128)S(1)}, f32[11,768]{1,0:T(8,128)S(1)}, u32[]{:S(2)}, u32[]{:S(2)}) %collective-permute-start.40) | collective-permute-done | bytes 33824 | tf_op jit(solution)/shard_map/ppermute | solution.py:44
  179.2 0.8 collective-permute-start.41
  180.0 1.4 collective-permute-start.46
  181.3 2.0 %collective-permute-done.41 = f32[11,768]{1,0:T(8,128)S(1)} collective-permute-done((f32[11,768]{1,0:T(8,128)S(1)}, f32[11,768]{1,0:T(8,128)S(1)}, u32[]{:S(2)}, u32[]{:S(2)}) %collective-permute-start.41) | collective-permute-done | bytes 33824 | tf_op jit(solution)/shard_map/ppermute | solution.py:44
  183.4 1.4 collective-permute-start.43
  184.8 0.8 collective-permute-start.44
  185.6 1.4 add_bitcast_fusion
  187.0 2.3 %collective-permute-done.44 = f32[11,768]{1,0:T(8,128)S(1)} collective-permute-done((f32[11,768]{1,0:T(8,128)S(1)}, f32[11,768]{1,0:T(8,128)S(1)}, u32[]{:S(2)}, u32[]{:S(2)}) %collective-permute-start.44) | collective-permute-done | bytes 33824 | tf_op jit(solution)/shard_map/ppermute | solution.py:44
  189.3 2.3 %collective-permute-start.45 = (f32[11,768]{1,0:T(8,128)S(1)}, f32[11,768]{1,0:T(8,128)S(1)}, u32[]{:S(2)}, u32[]{:S(2)}) collective-permute-start(f32[11,768]{1,0:T(8,128)S(1)} %add.98.sums_ref), channel_id=1, source_target_pairs={{0,16},{2,18},{4,20},{6,22},{8,24},{10,26},{12,28},{14,30},{16,0},... | collective-permute-start | bytes 101384 | tf_op jit(solution)/shard_map/ppermute | solution.py:44
  191.6 1.4 collective-permute-done.46
  192.9 0.8 finish_mid.1
  193.7 1.5 collective-permute-done.45.sums_got_ref
  (130 shorter events, 19.2 us)
Async XLA Ops:
  0.7 0.9 copy-start.2
  1.6 0.8 copy-start.3
  2.3 0.7 copy-start.6
  3.0 0.7 copy-start.7
  3.8 10.1 %collective-permute-start = (bf16[1,48,1664]{2,1,0:T(8,128)(2,1)S(1)}, bf16[1,48,1664]{2,1,0:T(8,128)(2,1)S(1)}, u32[]{:S(2)}, u32[]{:S(2)}) collective-permute-start(bf16[1,48,1664]{2,1,0:T(8,128)(2,1)S(1)} %bitcast.178), channel_id=1, source_target_pairs={{0,24},{2,26},{4,28},{6,30},{8,16},{10,18},{12,20},{14,22},{16,8},... | collective-permute-start | bytes 479240 | tf_op jit(solution)/shard_map/ppermute | solution.py:44
  8.9 13.5 %collective-permute-start.1 = (bf16[1,48,1664]{2,1,0:T(8,128)(2,1)S(1)}, bf16[1,48,1664]{2,1,0:T(8,128)(2,1)S(1)}, u32[]{:S(2)}, u32[]{:S(2)}) collective-permute-start(bf16[1,48,1664]{2,1,0:T(8,128)(2,1)S(1)} %bitcast.179), channel_id=1, source_target_pairs={{0,16},{2,18},{4,20},{6,22},{8,24},{10,26},{12,28},{14,30},{16,0},... | collective-permute-start | bytes 479240 | tf_op jit(solution)/shard_map/ppermute | solution.py:44
  8.9 13.5 %collective-permute-start.2 = (bf16[1,48,1664]{2,1,0:T(8,128)(2,1)S(1)}, bf16[1,48,1664]{2,1,0:T(8,128)(2,1)S(1)}, u32[]{:S(2)}, u32[]{:S(2)}) collective-permute-start(bf16[1,48,1664]{2,1,0:T(8,128)(2,1)S(1)} %bitcast.180), channel_id=1, source_target_pairs={{0,8},{2,10},{4,12},{6,14},{8,0},{10,2},{12,4},{14,6},{16,24},{18,... | collective-permute-start | bytes 479240 | tf_op jit(solution)/shard_map/ppermute | solution.py:44
  9.5 13.1 %collective-permute-start.3 = (bf16[512,768]{1,0:T(8,128)(2,1)}, bf16[512,768]{1,0:T(8,128)(2,1)S(1)}, u32[]{:S(2)}, u32[]{:S(2)}) collective-permute-start(bf16[512,768]{1,0:T(8,128)(2,1)} %bitcast.173), channel_id=1, source_target_pairs={{0,1},{1,0},{2,3},{3,2},{4,5},{5,4},{6,7},{7,6},{8,9},{9,8},{10,11... | collective-permute-start | bytes 2359304 | tf_op jit(solution)/shard_map/ppermute | solution.py:48
  22.5 15.3 %copy-start = (bf16[1,512,768]{2,1,0:T(8,128)(2,1)S(1)}, bf16[1,512,768]{2,1,0:T(8,128)(2,1)}, u32[]{:S(2)}) copy-start(bf16[1,512,768]{2,1,0:T(8,128)(2,1)} %param.10) | copy-start | bytes 2359300
  22.6 15.0 %collective-permute-start.8 = (bf16[1,48,3072]{2,1,0:T(8,128)(2,1)S(1)}, bf16[1,48,3072]{2,1,0:T(8,128)(2,1)S(1)}, u32[]{:S(2)}, u32[]{:S(2)}) collective-permute-start(bf16[1,48,3072]{2,1,0:T(8,128)(2,1)S(1)} %maximum_bitcast_fusion.2), channel_id=1, source_target_pairs={{0,16},{2,18},{4,20},{6,22},{8,24},{10,26},{12,28},{14,30},{16,0},... | collective-permute-start | bytes 884744 | tf_op jit(solution)/shard_map/ppermute | solution.py:44
  22.7 15.5 %collective-permute-start.4 = (bf16[4,48,1664]{2,1,0:T(8,128)(2,1)S(1)}, bf16[4,48,1664]{2,1,0:T(8,128)(2,1)S(1)}, u32[]{:S(2)}, u32[]{:S(2)}) collective-permute-start(bf16[4,48,1664]{2,1,0:T(8,128)(2,1)S(1)} %maximum_bitcast_fusion.refs_0_), channel_id=1, source_target_pairs={{0,2},{2,0},{4,6},{6,4},{8,10},{10,8},{12,14},{14,12},{16,18},{18,... | collective-permute-start | bytes 1916936 | tf_op jit(solution)/shard_map/ppermute | solution.py:44
  24.3 15.2 %collective-permute-start.5 = (bf16[4,48,1664]{2,1,0:T(8,128)(2,1)S(1)}, bf16[4,48,1664]{2,1,0:T(8,128)(2,1)S(1)}, u32[]{:S(2)}, u32[]{:S(2)}) collective-permute-start(bf16[4,48,1664]{2,1,0:T(8,128)(2,1)S(1)} %maximum_bitcast_fusion.refs_0_), channel_id=1, source_target_pairs={{0,4},{2,6},{4,0},{6,2},{8,12},{10,14},{12,8},{14,10},{16,20},{18,... | collective-permute-start | bytes 1916936 | tf_op jit(solution)/shard_map/ppermute | solution.py:44
  37.7 15.3 %collective-permute-start.9 = (bf16[2,48,3072]{2,1,0:T(8,128)(2,1)S(1)}, bf16[2,48,3072]{2,1,0:T(8,128)(2,1)S(1)}, u32[]{:S(2)}, u32[]{:S(2)}) collective-permute-start(bf16[2,48,3072]{2,1,0:T(8,128)(2,1)S(1)} %maximum_bitcast_fusion.1), channel_id=1, source_target_pairs={{0,8},{2,10},{4,12},{6,14},{8,0},{10,2},{12,4},{14,6},{16,24},{18,... | collective-permute-start | bytes 1769480 | tf_op jit(solution)/shard_map/ppermute | solution.py:44
  39.4 13.9 %collective-permute-start.6 = (bf16[2,48,1664]{2,1,0:T(8,128)(2,1)S(1)}, bf16[2,48,1664]{2,1,0:T(8,128)(2,1)S(1)}, u32[]{:S(2)}, u32[]{:S(2)}) collective-permute-start(bf16[2,48,1664]{2,1,0:T(8,128)(2,1)S(1)} %slice.59), channel_id=1, source_target_pairs={{0,4},{2,6},{4,0},{6,2},{8,12},{10,14},{12,8},{14,10},{16,20},{18,... | collective-permute-start | bytes 958472 | tf_op jit(solution)/shard_map/ppermute | solution.py:44
  41.1 12.3 %collective-permute-start.7 = (bf16[2,48,1664]{2,1,0:T(8,128)(2,1)S(1)}, bf16[2,48,1664]{2,1,0:T(8,128)(2,1)S(1)}, u32[]{:S(2)}, u32[]{:S(2)}) collective-permute-start(bf16[2,48,1664]{2,1,0:T(8,128)(2,1)S(1)} %slice.60), channel_id=1, source_target_pairs={{0,2},{2,0},{4,6},{6,4},{8,10},{10,8},{12,14},{14,12},{16,18},{18,... | collective-permute-start | bytes 958472 | tf_op jit(solution)/shard_map/ppermute | solution.py:44
  53.4 3.3 %copy-start.5 = (bf16[2,384]{1,0:T(2,128)(2,1)S(1)}, bf16[2,384]{1,0:T(2,128)(2,1)}, u32[]{:S(2)}) copy-start(bf16[2,384]{1,0:T(2,128)(2,1)} %bias_ref.2) | copy-start | bytes 4612
  53.4 27.1 %collective-permute-start.12 = (bf16[4,48,3072]{2,1,0:T(8,128)(2,1)S(1)}, bf16[4,48,3072]{2,1,0:T(8,128)(2,1)S(1)}, u32[]{:S(2)}, u32[]{:S(2)}) collective-permute-start(bf16[4,48,3072]{2,1,0:T(8,128)(2,1)S(1)} %bitcast.167), channel_id=1, source_target_pairs={{0,2},{2,0},{4,6},{6,4},{8,10},{10,8},{12,14},{14,12},{16,18},{18,... | collective-permute-start | bytes 3538952 | tf_op jit(solution)/shard_map/ppermute | solution.py:44
  54.9 26.8 %collective-permute-start.13 = (bf16[4,48,3072]{2,1,0:T(8,128)(2,1)S(1)}, bf16[4,48,3072]{2,1,0:T(8,128)(2,1)S(1)}, u32[]{:S(2)}, u32[]{:S(2)}) collective-permute-start(bf16[4,48,3072]{2,1,0:T(8,128)(2,1)S(1)} %bitcast.168), channel_id=1, source_target_pairs={{0,4},{2,6},{4,0},{6,2},{8,12},{10,14},{12,8},{14,10},{16,20},{18,... | collective-permute-start | bytes 3538952 | tf_op jit(solution)/shard_map/ppermute | solution.py:44
  74.6 1.1 copy-start.1
  74.7 2.4 %collective-permute-start.10 = (bf16[512,768]{1,0:T(8,128)(2,1)S(1)}, bf16[512,768]{1,0:T(8,128)(2,1)S(1)}, u32[]{:S(2)}, u32[]{:S(2)}) collective-permute-start(bf16[512,768]{1,0:T(8,128)(2,1)S(1)} %get-tuple-element.271), channel_id=1, source_target_pairs={{0,1},{1,0},{2,3},{3,2},{4,5},{5,4},{6,7},{7,6},{8,9},{9,8},{10,11... | collective-permute-start | bytes 2359304 | tf_op jit(solution)/shard_map/ppermute | solution.py:48
  74.8 3.4 %collective-permute-start.11 = (bf16[512,768]{1,0:T(8,128)(2,1)S(1)}, bf16[512,768]{1,0:T(8,128)(2,1)S(1)}, u32[]{:S(2)}, u32[]{:S(2)}) collective-permute-start(bf16[512,768]{1,0:T(8,128)(2,1)S(1)} %get-tuple-element.270), channel_id=1, source_target_pairs={{0,1},{1,0},{2,3},{3,2},{4,5},{5,4},{6,7},{7,6},{8,9},{9,8},{10,11... | collective-permute-start | bytes 2359304 | tf_op jit(solution)/shard_map/ppermute | solution.py:48
  75.7 4.1 %collective-permute-start.14 = (bf16[512,768]{1,0:T(8,128)(2,1)S(1)}, bf16[512,768]{1,0:T(8,128)(2,1)S(1)}, u32[]{:S(2)}, u32[]{:S(2)}) collective-permute-start(bf16[512,768]{1,0:T(8,128)(2,1)S(1)} %bitcast.176), channel_id=1, source_target_pairs={{0,1},{1,0},{2,3},{3,2},{4,5},{5,4},{6,7},{7,6},{8,9},{9,8},{10,11... | collective-permute-start | bytes 2359304 | tf_op jit(solution)/shard_map/ppermute | solution.py:48
  81.7 7.3 %collective-permute-start.15 = (bf16[2,48,1536]{2,1,0:T(8,128)(2,1)S(1)}, bf16[2,48,1536]{2,1,0:T(8,128)(2,1)S(1)}, u32[]{:S(2)}, u32[]{:S(2)}) collective-permute-start(bf16[2,48,1536]{2,1,0:T(8,128)(2,1)S(1)} %slice.65), channel_id=1, source_target_pairs={{0,4},{2,6},{4,0},{6,2},{8,12},{10,14},{12,8},{14,10},{16,20},{18,... | collective-permute-start | bytes 884744 | tf_op jit(solution)/shard_map/ppermute | solution.py:44
  83.3 6.8 %collective-permute-start.16 = (bf16[2,48,1536]{2,1,0:T(8,128)(2,1)S(1)}, bf16[2,48,1536]{2,1,0:T(8,128)(2,1)S(1)}, u32[]{:S(2)}, u32[]{:S(2)}) collective-permute-start(bf16[2,48,1536]{2,1,0:T(8,128)(2,1)S(1)} %slice.66), channel_id=1, source_target_pairs={{0,2},{2,0},{4,6},{6,4},{8,10},{10,8},{12,14},{14,12},{16,18},{18,... | collective-permute-start | bytes 884744 | tf_op jit(solution)/shard_map/ppermute | solution.py:44
  90.1 9.6 %collective-permute-start.17 = (bf16[2,48,1536]{2,1,0:T(8,128)(2,1)S(1)}, bf16[2,48,1536]{2,1,0:T(8,128)(2,1)S(1)}, u32[]{:S(2)}, u32[]{:S(2)}) collective-permute-start(bf16[2,48,1536]{2,1,0:T(8,128)(2,1)S(1)} %slice.67), channel_id=1, source_target_pairs={{0,4},{2,6},{4,0},{6,2},{8,12},{10,14},{12,8},{14,10},{16,20},{18,... | collective-permute-start | bytes 884744 | tf_op jit(solution)/shard_map/ppermute | solution.py:44
  90.9 0.8 copy-start.4
  90.9 8.8 %collective-permute-start.18 = (bf16[2,48,1536]{2,1,0:T(8,128)(2,1)S(1)}, bf16[2,48,1536]{2,1,0:T(8,128)(2,1)S(1)}, u32[]{:S(2)}, u32[]{:S(2)}) collective-permute-start(bf16[2,48,1536]{2,1,0:T(8,128)(2,1)S(1)} %slice.68), channel_id=1, source_target_pairs={{0,2},{2,0},{4,6},{6,4},{8,10},{10,8},{12,14},{14,12},{16,18},{18,... | collective-permute-start | bytes 884744 | tf_op jit(solution)/shard_map/ppermute | solution.py:44
  99.8 8.9 %collective-permute-start.19 = (bf16[2,48,1536]{2,1,0:T(8,128)(2,1)S(1)}, bf16[2,48,1536]{2,1,0:T(8,128)(2,1)S(1)}, u32[]{:S(2)}, u32[]{:S(2)}) collective-permute-start(bf16[2,48,1536]{2,1,0:T(8,128)(2,1)S(1)} %get-tuple-element.179), channel_id=1, source_target_pairs={{0,2},{2,0},{4,6},{6,4},{8,10},{10,8},{12,14},{14,12},{16,18},{18,... | collective-permute-start | bytes 884744 | tf_op jit(solution)/shard_map/ppermute | solution.py:44
  101.3 7.3 %collective-permute-start.20 = (bf16[2,48,1536]{2,1,0:T(8,128)(2,1)S(1)}, bf16[2,48,1536]{2,1,0:T(8,128)(2,1)S(1)}, u32[]{:S(2)}, u32[]{:S(2)}) collective-permute-start(bf16[2,48,1536]{2,1,0:T(8,128)(2,1)S(1)} %get-tuple-element.180), channel_id=1, source_target_pairs={{0,4},{2,6},{4,0},{6,2},{8,12},{10,14},{12,8},{14,10},{16,20},{18,... | collective-permute-start | bytes 884744 | tf_op jit(solution)/shard_map/ppermute | solution.py:44
  108.8 5.2 %collective-permute-start.21 = (bf16[512,768]{1,0:T(8,128)(2,1)S(1)}, bf16[512,768]{1,0:T(8,128)(2,1)S(1)}, u32[]{:S(2)}, u32[]{:S(2)}) collective-permute-start(bf16[512,768]{1,0:T(8,128)(2,1)S(1)} %get-tuple-element.269), channel_id=1, source_target_pairs={{0,1},{1,0},{2,3},{3,2},{4,5},{5,4},{6,7},{7,6},{8,9},{9,8},{10,11... | collective-permute-start | bytes 2359304 | tf_op jit(solution)/shard_map/ppermute | solution.py:48
  108.9 5.1 %collective-permute-start.22 = (bf16[512,768]{1,0:T(8,128)(2,1)S(1)}, bf16[512,768]{1,0:T(8,128)(2,1)S(1)}, u32[]{:S(2)}, u32[]{:S(2)}) collective-permute-start(bf16[512,768]{1,0:T(8,128)(2,1)S(1)} %get-tuple-element.268), channel_id=1, source_target_pairs={{0,1},{1,0},{2,3},{3,2},{4,5},{5,4},{6,7},{7,6},{8,9},{9,8},{10,11... | collective-permute-start | bytes 2359304 | tf_op jit(solution)/shard_map/ppermute | solution.py:48
  109.6 24.9 %collective-permute-start.25 = (bf16[4,48,1536]{2,1,0:T(8,128)(2,1)S(1)}, bf16[4,48,1536]{2,1,0:T(8,128)(2,1)S(1)}, u32[]{:S(2)}, u32[]{:S(2)}) collective-permute-start(bf16[4,48,1536]{2,1,0:T(8,128)(2,1)S(1)} %pad_maximum_fusion.4), channel_id=1, source_target_pairs={{0,2},{2,0},{4,6},{6,4},{8,10},{10,8},{12,14},{14,12},{16,18},{18,... | collective-permute-start | bytes 1769480 | tf_op jit(solution)/shard_map/ppermute | solution.py:44
  110.2 24.2 %collective-permute-start.26 = (bf16[4,48,1536]{2,1,0:T(8,128)(2,1)S(1)}, bf16[4,48,1536]{2,1,0:T(8,128)(2,1)S(1)}, u32[]{:S(2)}, u32[]{:S(2)}) collective-permute-start(bf16[4,48,1536]{2,1,0:T(8,128)(2,1)S(1)} %pad_maximum_fusion.5), channel_id=1, source_target_pairs={{0,4},{2,6},{4,0},{6,2},{8,12},{10,14},{12,8},{14,10},{16,20},{18,... | collective-permute-start | bytes 1769480 | tf_op jit(solution)/shard_map/ppermute | solution.py:44
  119.0 15.5 %collective-permute-start.23 = (bf16[2,48,1920]{2,1,0:T(8,128)(2,1)S(1)}, bf16[2,48,1920]{2,1,0:T(8,128)(2,1)S(1)}, u32[]{:S(2)}, u32[]{:S(2)}) collective-permute-start(bf16[2,48,1920]{2,1,0:T(8,128)(2,1)S(1)} %get-tuple-element.187), channel_id=1, source_target_pairs={{0,2},{2,0},{4,6},{6,4},{8,10},{10,8},{12,14},{14,12},{16,18},{18,... | collective-permute-start | bytes 1105928 | tf_op jit(solution)/shard_map/ppermute | solution.py:44
  120.5 14.0 %collective-permute-start.24 = (bf16[2,48,1920]{2,1,0:T(8,128)(2,1)S(1)}, bf16[2,48,1920]{2,1,0:T(8,128)(2,1)S(1)}, u32[]{:S(2)}, u32[]{:S(2)}) collective-permute-start(bf16[2,48,1920]{2,1,0:T(8,128)(2,1)S(1)} %get-tuple-element.188), channel_id=1, source_target_pairs={{0,4},{2,6},{4,0},{6,2},{8,12},{10,14},{12,8},{14,10},{16,20},{18,... | collective-permute-start | bytes 1105928 | tf_op jit(solution)/shard_map/ppermute | solution.py:44
  134.8 12.0 %collective-permute-start.27 = (bf16[2,48,1536]{2,1,0:T(8,128)(2,1)S(1)}, bf16[2,48,1536]{2,1,0:T(8,128)(2,1)S(1)}, u32[]{:S(2)}, u32[]{:S(2)}) collective-permute-start(bf16[2,48,1536]{2,1,0:T(8,128)(2,1)S(1)} %fusion.9), channel_id=1, source_target_pairs={{0,8},{2,10},{4,12},{6,14},{8,0},{10,2},{12,4},{14,6},{16,24},{18,... | collective-permute-start | bytes 884744 | tf_op jit(solution)/shard_map/ppermute | solution.py:44
  136.0 22.3 %collective-permute-start.30 = (bf16[4,48,1920]{2,1,0:T(8,128)(2,1)S(1)}, bf16[4,48,1920]{2,1,0:T(8,128)(2,1)S(1)}, u32[]{:S(2)}, u32[]{:S(2)}) collective-permute-start(bf16[4,48,1920]{2,1,0:T(8,128)(2,1)S(1)} %pad_maximum_fusion.2), channel_id=1, source_target_pairs={{0,2},{2,0},{4,6},{6,4},{8,10},{10,8},{12,14},{14,12},{16,18},{18,... | collective-permute-start | bytes 2211848 | tf_op jit(solution)/shard_map/ppermute | solution.py:44
  136.7 21.6 %collective-permute-start.31 = (bf16[4,48,1920]{2,1,0:T(8,128)(2,1)S(1)}, bf16[4,48,1920]{2,1,0:T(8,128)(2,1)S(1)}, u32[]{:S(2)}, u32[]{:S(2)}) collective-permute-start(bf16[4,48,1920]{2,1,0:T(8,128)(2,1)S(1)} %pad_maximum_fusion.3), channel_id=1, source_target_pairs={{0,4},{2,6},{4,0},{6,2},{8,12},{10,14},{12,8},{14,10},{16,20},{18,... | collective-permute-start | bytes 2211848 | tf_op jit(solution)/shard_map/ppermute | solution.py:44
  146.9 10.9 %collective-permute-start.28 = (bf16[2,48,1152]{2,1,0:T(8,128)(2,1)S(1)}, bf16[2,48,1152]{2,1,0:T(8,128)(2,1)S(1)}, u32[]{:S(2)}, u32[]{:S(2)}) collective-permute-start(bf16[2,48,1152]{2,1,0:T(8,128)(2,1)S(1)} %get-tuple-element.202), channel_id=1, source_target_pairs={{0,2},{2,0},{4,6},{6,4},{8,10},{10,8},{12,14},{14,12},{16,18},{18,... | collective-permute-start | bytes 663560 | tf_op jit(solution)/shard_map/ppermute | solution.py:44
  148.4 9.9 %collective-permute-start.29 = (bf16[2,48,1152]{2,1,0:T(8,128)(2,1)S(1)}, bf16[2,48,1152]{2,1,0:T(8,128)(2,1)S(1)}, u32[]{:S(2)}, u32[]{:S(2)}) collective-permute-start(bf16[2,48,1152]{2,1,0:T(8,128)(2,1)S(1)} %get-tuple-element.203), channel_id=1, source_target_pairs={{0,4},{2,6},{4,0},{6,2},{8,12},{10,14},{12,8},{14,10},{16,20},{18,... | collective-permute-start | bytes 663560 | tf_op jit(solution)/shard_map/ppermute | solution.py:44
  149.8 7.7 %collective-permute-start.32 = (bf16[1,48,1536]{2,1,0:T(8,128)(2,1)S(1)}, bf16[1,48,1536]{2,1,0:T(8,128)(2,1)S(1)}, u32[]{:S(2)}, u32[]{:S(2)}) collective-permute-start(bf16[1,48,1536]{2,1,0:T(8,128)(2,1)S(1)} %dynamic-slice_convert_fusion.1), channel_id=1, source_target_pairs={{0,16},{2,18},{4,20},{6,22},{8,24},{10,26},{12,28},{14,30},{16,0},... | collective-permute-start | bytes 442376 | tf_op jit(solution)/shard_map/ppermute | solution.py:44
  158.6 5.2 %collective-permute-start.36 = (bf16[256,768]{1,0:T(8,128)(2,1)S(1)}, bf16[256,768]{1,0:T(8,128)(2,1)S(1)}, u32[]{:S(2)}, u32[]{:S(2)}) collective-permute-start(bf16[256,768]{1,0:T(8,128)(2,1)S(1)} %get-tuple-element.275), channel_id=1, source_target_pairs={{0,1},{1,0},{2,3},{3,2},{4,5},{5,4},{6,7},{7,6},{8,9},{9,8},{10,11... | collective-permute-start | bytes 1179656 | tf_op jit(solution)/shard_map/ppermute | solution.py:48
  158.7 5.1 %collective-permute-start.37 = (bf16[256,768]{1,0:T(8,128)(2,1)S(1)}, bf16[256,768]{1,0:T(8,128)(2,1)S(1)}, u32[]{:S(2)}, u32[]{:S(2)}) collective-permute-start(bf16[256,768]{1,0:T(8,128)(2,1)S(1)} %get-tuple-element.274), channel_id=1, source_target_pairs={{0,1},{1,0},{2,3},{3,2},{4,5},{5,4},{6,7},{7,6},{8,9},{9,8},{10,11... | collective-permute-start | bytes 1179656 | tf_op jit(solution)/shard_map/ppermute | solution.py:48
  159.5 10.6 %collective-permute-start.33 = (bf16[2,48,1920]{2,1,0:T(8,128)(2,1)S(1)}, bf16[2,48,1920]{2,1,0:T(8,128)(2,1)S(1)}, u32[]{:S(2)}, u32[]{:S(2)}) collective-permute-start(bf16[2,48,1920]{2,1,0:T(8,128)(2,1)S(1)} %fusion.8), channel_id=1, source_target_pairs={{0,8},{2,10},{4,12},{6,14},{8,0},{10,2},{12,4},{14,6},{16,24},{18,... | collective-permute-start | bytes 1105928 | tf_op jit(solution)/shard_map/ppermute | solution.py:44
  160.8 11.9 %collective-permute-start.34 = (bf16[4,48,1152]{2,1,0:T(8,128)(2,1)S(1)}, bf16[4,48,1152]{2,1,0:T(8,128)(2,1)S(1)}, u32[]{:S(2)}, u32[]{:S(2)}) collective-permute-start(bf16[4,48,1152]{2,1,0:T(8,128)(2,1)S(1)} %pad_maximum_fusion.6), channel_id=1, source_target_pairs={{0,2},{2,0},{4,6},{6,4},{8,10},{10,8},{12,14},{14,12},{16,18},{18,... | collective-permute-start | bytes 1327112 | tf_op jit(solution)/shard_map/ppermute | solution.py:44
  162.3 11.6 %collective-permute-start.35 = (bf16[4,48,1152]{2,1,0:T(8,128)(2,1)S(1)}, bf16[4,48,1152]{2,1,0:T(8,128)(2,1)S(1)}, u32[]{:S(2)}, u32[]{:S(2)}) collective-permute-start(bf16[4,48,1152]{2,1,0:T(8,128)(2,1)S(1)} %pad_maximum_fusion.7), channel_id=1, source_target_pairs={{0,4},{2,6},{4,0},{6,2},{8,12},{10,14},{12,8},{14,10},{16,20},{18,... | collective-permute-start | bytes 1327112 | tf_op jit(solution)/shard_map/ppermute | solution.py:44
  163.8 19.6 %collective-permute-start.42 = (bf16[512,768]{1,0:T(8,128)(2,1)S(1)}, bf16[512,768]{1,0:T(8,128)(2,1)S(1)}, u32[]{:S(2)}, u32[]{:S(2)}) collective-permute-start(bf16[512,768]{1,0:T(8,128)(2,1)S(1)} %get-tuple-element.233), channel_id=1, source_target_pairs={{0,1},{1,0},{2,3},{3,2},{4,5},{5,4},{6,7},{7,6},{8,9},{9,8},{10,11... | collective-permute-start | bytes 2359304 | tf_op jit(solution)/shard_map/ppermute | solution.py:48
  167.1 3.1 %collective-permute-start.38 = (f32[6,768]{1,0:T(8,128)S(1)}, f32[6,768]{1,0:T(8,128)S(1)}, u32[]{:S(2)}, u32[]{:S(2)}) collective-permute-start(f32[6,768]{1,0:T(8,128)S(1)} %pad_maximum_fusion.8), channel_id=1, source_target_pairs={{0,1},{1,0},{2,3},{3,2},{4,5},{5,4},{6,7},{7,6},{8,9},{9,8},{10,11... | collective-permute-start | bytes 55304 | tf_op jit(solution)/shard_map/ppermute | solution.py:48
  174.1 9.2 %collective-permute-start.39 = (bf16[2,48,1152]{2,1,0:T(8,128)(2,1)S(1)}, bf16[2,48,1152]{2,1,0:T(8,128)(2,1)S(1)}, u32[]{:S(2)}, u32[]{:S(2)}) collective-permute-start(bf16[2,48,1152]{2,1,0:T(8,128)(2,1)S(1)} %fusion.10), channel_id=1, source_target_pairs={{0,8},{2,10},{4,12},{6,14},{8,0},{10,2},{12,4},{14,6},{16,24},{18,... | collective-permute-start | bytes 663560 | tf_op jit(solution)/shard_map/ppermute | solution.py:44
  175.0 4.2 %collective-permute-start.40 = (f32[11,768]{1,0:T(8,128)S(1)}, f32[11,768]{1,0:T(8,128)S(1)}, u32[]{:S(2)}, u32[]{:S(2)}) collective-permute-start(f32[11,768]{1,0:T(8,128)S(1)} %fusion.12), channel_id=1, source_target_pairs={{0,2},{2,0},{4,6},{6,4},{8,10},{10,8},{12,14},{14,12},{16,18},{18,... | collective-permute-start | bytes 101384 | tf_op jit(solution)/shard_map/ppermute | solution.py:44
  179.2 4.2 %collective-permute-start.41 = (f32[11,768]{1,0:T(8,128)S(1)}, f32[11,768]{1,0:T(8,128)S(1)}, u32[]{:S(2)}, u32[]{:S(2)}) collective-permute-start(f32[11,768]{1,0:T(8,128)S(1)} %fusion.15), channel_id=1, source_target_pairs={{0,4},{2,6},{4,0},{6,2},{8,12},{10,14},{12,8},{14,10},{16,20},{18,... | collective-permute-start | bytes 101384 | tf_op jit(solution)/shard_map/ppermute | solution.py:44
  180.0 13.0 %collective-permute-start.46 = (bf16[1,48,1920]{2,1,0:T(8,128)(2,1)S(1)}, bf16[1,48,1920]{2,1,0:T(8,128)(2,1)S(1)}, u32[]{:S(2)}, u32[]{:S(2)}) collective-permute-start(bf16[1,48,1920]{2,1,0:T(8,128)(2,1)S(1)} %dynamic-slice_convert_fusion), channel_id=1, source_target_pairs={{0,16},{2,18},{4,20},{6,22},{8,24},{10,26},{12,28},{14,30},{16,0},... | collective-permute-start | bytes 552968 | tf_op jit(solution)/shard_map/ppermute | solution.py:44
  183.4 11.7 %collective-permute-start.43 = (bf16[1,48,1152]{2,1,0:T(8,128)(2,1)S(1)}, bf16[1,48,1152]{2,1,0:T(8,128)(2,1)S(1)}, u32[]{:S(2)}, u32[]{:S(2)}) collective-permute-start(bf16[1,48,1152]{2,1,0:T(8,128)(2,1)S(1)} %dynamic-slice_convert_fusion.2), channel_id=1, source_target_pairs={{0,16},{2,18},{4,20},{6,22},{8,24},{10,26},{12,28},{14,30},{16,0},... | collective-permute-start | bytes 331784 | tf_op jit(solution)/shard_map/ppermute | solution.py:44
  184.8 4.5 %collective-permute-start.44 = (f32[11,768]{1,0:T(8,128)S(1)}, f32[11,768]{1,0:T(8,128)S(1)}, u32[]{:S(2)}, u32[]{:S(2)}) collective-permute-start(f32[11,768]{1,0:T(8,128)S(1)} %add.92), channel_id=1, source_target_pairs={{0,8},{2,10},{4,12},{6,14},{8,0},{10,2},{12,4},{14,6},{16,24},{18,... | collective-permute-start | bytes 101384 | tf_op jit(solution)/shard_map/ppermute | solution.py:44
  189.3 5.9 %collective-permute-start.45 = (f32[11,768]{1,0:T(8,128)S(1)}, f32[11,768]{1,0:T(8,128)S(1)}, u32[]{:S(2)}, u32[]{:S(2)}) collective-permute-start(f32[11,768]{1,0:T(8,128)S(1)} %add.98.sums_ref), channel_id=1, source_target_pairs={{0,16},{2,18},{4,20},{6,22},{8,24},{10,26},{12,28},{14,30},{16,0},... | collective-permute-start | bytes 101384 | tf_op jit(solution)/shard_map/ppermute | solution.py:44

commit v4 on v3

--- a/solution.py
+++ b/solution.py
@@ -348,7 +348,7 @@
         step(pl.ds(pl.multiple_of(i * ROW_BLOCK, ROW_BLOCK), ROW_BLOCK))
 
 
-def pack_kernel(qkv_ref, out_ref, gains_ref, shifts_ref, packed_ref, small_ref):
+def pack_kernel(qkv_ref, out_ref, vectors_ref, packed_ref, small_ref):
     rows, wide = out_ref.shape
     for pair in range(wide // PAIR):
         for i in range(3):
@@ -356,15 +356,14 @@
             packed_ref[:, start : start + PAIR] = qkv_ref[i, :, pair * PAIR : (pair + 1) * PAIR]
     packed_ref[:, 3 * wide : 4 * wide] = out_ref[...]
     small_ref[...] = jnp.zeros_like(small_ref)
-    small_ref[0:2, :rows] = gains_ref[...].astype(F32)
-    small_ref[2:6, :rows] = shifts_ref[...].astype(F32)
+    small_ref[0:6, :rows] = vectors_ref[...].astype(F32)
     packed_ref[:, 4 * wide :] = jnp.zeros_like(packed_ref[:, 4 * wide :])
     packed_ref[:, 4 * wide : 4 * wide + 8] = small_ref[...].T[:rows].astype(BF)
 
 
 def pack(qkv_weight, out_weight, gains, shifts):
     rows, wide = out_weight.shape
-    args = (qkv_weight, out_weight, gains, shifts)
+    args = (qkv_weight, out_weight, jnp.concatenate([gains, shifts], axis=0))
     shape = (rows, 4 * wide + PAIR)
     return pl.pallas_call(
         pack_kernel,
@@ -713,8 +712,9 @@
     d_two = mm("fh,dh->fd", d_pre, mid_full).astype(BF)
 
     d_two, fc2_far, d_pre = stage(d_two, fc2_far, d_pre)
-    fc2_near = scatter_low_near(near_operands(fc2_parts, fc2_far))
-    d_two_other = swap_pieces(d_two, PIECES)
+    fc2_ops = near_operands(fc2_parts, fc2_far)
+    fc2_near = scatter_low_near(fc2_ops)
+    d_two_other = swap_pieces(after(d_two, fc2_ops), PIECES)
     fc1_grad = mm("fd,fh->dh", normed_two_all, d_pre).astype(BF)
     d_branch_all, d_hidden, mid_sums = mid_norm_back(
         d_two, d_two_other, hidden_all, d_out_all, vectors
@@ -728,7 +728,9 @@
     d_proj = attend_back(qkv, log_sums, d_attended, 0, pairs - 1, 2 * half)
 
     d_proj, mid_far, fc2_near = stage(d_proj, mid_far, fc2_near)
-    mid_near = scatter_low_near(near_operands(mid_parts, mid_far))
+    mid_ops = near_operands(mid_parts, mid_far)
+    mid_near = scatter_low_near(mid_ops)
+    fc2_near = after(fc2_near, mid_ops)
     fc2_sum = scatter_high_step(high_operands(total_of(fc2_near), 0, at), 0)
     d_qkv, d_sums = attend_back(qkv, log_sums, d_attended, pairs - 1, 1, half, d_proj)
     qkv_grad = mm("fd,fe->de", normed_all, d_qkv).astype(BF)

time: 196 us -> 195 us (level)
  transfers between devices with their start and end apart: 47 -> 47, of which waited for: 23 -> 21; matrix products, arithmetic and copies ran while one was open for 10% -> 10% of each run, Pallas kernels for 30% -> 30%
where the time goes in v4:
time: 195 us; the launch traced here: 194 us
  waiting for transfers between devices  66.6 us (34%)
  Pallas kernels  58.9 us (30%)
  starting transfers between devices  44.7 us (23%)
  matrix products  13.8 us (7%)
  other arithmetic  5.5 us (3%)
  local copies, waits for them, and re-layouts  3.32 us (2%)
    ppermute x37, waiting for transfers between devices, swap_dp(): return lax.ppermute(x, 'dp', [(i, i ^ step) for i in range(n)])  64.1 us
    ppermute x37, starting transfers between devices, swap_dp(): return lax.ppermute(x, 'dp', [(i, i ^ step) for i in range(n)])  42.4 us
    pallas_call x2, Pallas kernels, attend_back(): pl.pallas_call(functools.partial(attend_back_kernel, block), grid=(count,...  19.4 us
    dot_general x7, matrix products, mm(): return jnp.einsum(spec, a, b, preferred_element_type=F32)  13.8 us
    pallas_call x1, Pallas kernels, attend(): pl.pallas_call(attend_kernel, grid=(count,), in_specs=[pl.BlockSpec((n, 3...  13.2 us
    pallas_call x1, Pallas kernels, act(): rows_call(act_kernel, [shape, shape], 'act', scratch)(x, weight, bias)  4.97 us
  transfers between devices with their start and end apart: 47, of which 21 were waited for; matrix products, arithmetic and copies ran while one was open for 10% of the time, Pallas kernels for 30%

profile of v4, /device:TPU:0, one launch (start us, length us, event | category | flops | bytes accessed | tf_op | source)
XLA Modules:
  0.0 194.3 jit_solution(8790475160853954071)
XLA Ops:
  1.4 0.9 copy-done.2
  2.3 0.8 copy-done.3
  3.1 5.1 %collective-permute-start = (bf16[1,48,1664]{2,1,0:T(8,128)(2,1)S(1)}, bf16[1,48,1664]{2,1,0:T(8,128)(2,1)S(1)}, u32[]{:S(2)}, u32[]{:S(2)}) collective-permute-start(bf16[1,48,1664]{2,1,0:T(8,128)(2,1)S(1)} %bitcast.178), channel_id=1, source_target_pairs={{0,24},{2,26},{4,28},{6,30},{8,16},{10,18},{12,20},{14,22},{16,8},... | collective-permute-start | bytes 479240 | tf_op jit(solution)/shard_map/ppermute | solution.py:44
  8.9 1.0 maximum_bitcast_fusion.2
  9.9 3.4 %collective-permute-done = bf16[1,48,1664]{2,1,0:T(8,128)(2,1)S(1)} collective-permute-done((bf16[1,48,1664]{2,1,0:T(8,128)(2,1)S(1)}, bf16[1,48,1664]{2,1,0:T(8,128)(2,1)S(1)}, u32[]{:S(2)}, u32[]{:S(2)}) %collective-permute-start) | collective-permute-done | bytes 159776 | tf_op jit(solution)/shard_map/ppermute | solution.py:44
  13.3 8.5 %collective-permute-done.1 = bf16[1,48,1664]{2,1,0:T(8,128)(2,1)S(1)} collective-permute-done((bf16[1,48,1664]{2,1,0:T(8,128)(2,1)S(1)}, bf16[1,48,1664]{2,1,0:T(8,128)(2,1)S(1)}, u32[]{:S(2)}, u32[]{:S(2)}) %collective-permute-start.1) | collective-permute-done | bytes 159776 | tf_op jit(solution)/shard_map/ppermute | solution.py:44
  22.1 1.6 collective-permute-start.4
  23.6 1.5 collective-permute-start.5
  25.1 11.8 %collective-permute-done.8 = bf16[1,48,3072]{2,1,0:T(8,128)(2,1)S(1)} collective-permute-done((bf16[1,48,3072]{2,1,0:T(8,128)(2,1)S(1)}, bf16[1,48,3072]{2,1,0:T(8,128)(2,1)S(1)}, u32[]{:S(2)}, u32[]{:S(2)}) %collective-permute-start.8) | collective-permute-done | bytes 294944 | tf_op jit(solution)/shard_map/ppermute | solution.py:44
  37.6 1.2 collective-permute-done.5.refs_2_
  38.8 1.6 collective-permute-start.6
  41.0 11.4 %collective-permute-done.9 = bf16[2,48,3072]{2,1,0:T(8,128)(2,1)S(1)} collective-permute-done((bf16[2,48,3072]{2,1,0:T(8,128)(2,1)S(1)}, bf16[2,48,3072]{2,1,0:T(8,128)(2,1)S(1)}, u32[]{:S(2)}, u32[]{:S(2)}) %collective-permute-start.9) | collective-permute-done | bytes 589856 | tf_op jit(solution)/shard_map/ppermute | solution.py:44
  52.7 1.6 collective-permute-start.12
  54.3 1.5 collective-permute-start.13
  56.0 3.7 %project.1 = (bf16[1024,768]{1,0:T(8,128)(2,1)S(1)}, bf16[1024,1152]{1,0:T(8,128)(2,1)S(1)}, f32[8,768]{1,0:T(8,128)S(1)}) custom-call(bf16[1024,768]{1,0:T(8,128)(2,1)S(1)} %join.2.x_ref, bf16[768,1664]{1,0:T(8,128)(2,1)S(1)} %bitcast.160, bf16[2,384]{1,0:T(2,128)(2,1)S(1)} %copy-done.5), custom_call_target="tpu_custom_call" | custom-call | tf_op jit(solution)/shard_map/project/pallas_call | solution.py:480
  59.7 13.2 %attend.1 = (bf16[1024,384]{1,0:T(8,128)(2,1)S(1)}, f32[3,2,1024]{2,1,0:T(2,128)S(1)}) custom-call(bf16[1024,1152]{1,0:T(8,128)(2,1)S(1)} %get-tuple-element.150.qkv_ref), custom_call_target="tpu_custom_call" | custom-call | tf_op jit(solution)/shard_map/attend/pallas_call | solution.py:233
  73.0 1.0 convolution_convert_fusion.3.mine_ref
  75.1 1.3 collective-permute-done.10.refs_0_
  76.4 1.1 collective-permute-done.11.refs_1_
  77.6 1.6 mid_norm.1
  79.8 1.2 collective-permute-done.13.refs_2_
  81.1 1.6 collective-permute-start.15
  83.4 4.9 %collective-permute-done.15.refs_3_ = bf16[2,48,1536]{2,1,0:T(8,128)(2,1)S(1)} collective-permute-done((bf16[2,48,1536]{2,1,0:T(8,128)(2,1)S(1)}, bf16[2,48,1536]{2,1,0:T(8,128)(2,1)S(1)}, u32[]{:S(2)}, u32[]{:S(2)}) %collective-permute-start.15) | collective-permute-done | bytes 294944 | tf_op jit(solution)/shard_map/ppermute | solution.py:44
  88.3 1.1 collective-permute-done.16.refs_4_
  91.1 5.0 %act.1 = (bf16[1024,1536]{1,0:T(8,128)(2,1)S(1)}, bf16[1024,1536]{1,0:T(8,128)(2,1)S(1)}) custom-call(bf16[1024,768]{1,0:T(8,128)(2,1)S(1)} %get-tuple-element.166.x_ref, bf16[768,1536]{1,0:T(8,128)(2,1)S(1)} %bitcast.171, bf16[1536]{0:T(1024)(128)(2,1)S(1)} %copy-done.4), custom_call_target="tpu_custom_call" | custom-call | tf_op jit(solution)/shard_map/act/pallas_call | solution.py:526
  96.0 3.0 %convolution_convert_fusion.1 = bf16[768,1536]{1,0:T(8,128)(2,1)S(1)} fusion(bf16[1024,768]{1,0:T(8,128)(2,1)S(1)} %join.3.d_out_ref, bf16[1024,1536]{1,0:T(8,128)(2,1)S(1)} %get-tuple-element.215.act_ref), kind=kOutput, calls=%fused_computation.1 | convolution fusion | flops 2417098752 | bytes 7077888 | tf_op jit(solution)/shard_map/fd,fh->dh/dot_general | solution.py:640
  99.2 1.5 collective-permute-start.19
  100.7 1.3 collective-permute-start.20
  102.2 3.2 %act_back.1 = (bf16[1024,1536]{1,0:T(8,128)(2,1)S(1)}, f32[1,1536]{1,0:T(1,128)S(1)}) custom-call(bf16[1024,768]{1,0:T(8,128)(2,1)S(1)} %join.3.d_out_ref, bf16[768,1536]{1,0:T(8,128)(2,1)S(1)} %bitcast.165, bf16[1024,1536]{1,0:T(8,128)(2,1)S(1)} %get-tuple-element.181.slope_ref), custom_call_target="tpu_custom_call" | custom-call | tf_op jit(solution)/shard_map/act_back/pallas_call | solution.py:541
  105.4 2.6 %convolution_convert_fusion.4.mine_ref = bf16[1024,768]{1,0:T(8,128)(2,1)S(1)} fusion(bf16[1024,1536]{1,0:T(8,128)(2,1)S(1)} %get-tuple-element.193, bf16[768,1536]{1,0:T(8,128)(2,1)S(1)} %bitcast.172), kind=kOutput, calls=%fused_computation.5 | convolution fusion | flops 2416705536 | bytes 7077888 | tf_op jit(solution)/shard_map/fh,dh->fd/dot_general | solution.py:640
  110.3 3.0 %convolution_convert_fusion = bf16[768,1536]{1,0:T(8,128)(2,1)S(1)} fusion(bf16[1024,768]{1,0:T(8,128)(2,1)S(1)} %get-tuple-element.166.x_ref, bf16[1024,1536]{1,0:T(8,128)(2,1)S(1)} %get-tuple-element.193), kind=kOutput, calls=%fused_computation | convolution fusion | flops 2417098752 | bytes 7077888 | tf_op jit(solution)/shard_map/fd,fh->dh/dot_general | solution.py:640
  113.3 2.7 %mid_norm_back.1 = (bf16[1024,768]{1,0:T(8,128)(2,1)S(1)}, f32[512,768]{1,0:T(8,128)S(1)}, f32[4,768]{1,0:T(4,128)S(1)}) custom-call(bf16[1024,768]{1,0:T(8,128)(2,1)S(1)} %convolution_convert_fusion.4.mine_ref, f32[1024,768]{1,0:T(8,128)S(1)} %get-tuple-element.153.hidden_ref, bf16[1024,768]{1,0:T(8,128)(2,1)S(1)} %join.3.d_out_ref, ...), custom_call_target="tpu_custom_call" | custom-call | tf_op jit(solution)/shard_map/mid_norm_back/pallas_call | solution.py:586
  116.0 1.0 convolution_convert_fusion.5.grad_ref
  116.9 1.0 convolution_convert_fusion.6
  118.3 1.5 collective-permute-start.23
  119.8 1.3 collective-permute-start.24
  121.2 12.5 %attend_back.2 = (bf16[1024,1152]{1,0:T(8,128)(2,1)S(1)}, f32[3,1,384]{2,1,0:T(1,128)S(1)}) custom-call(bf16[1024,1152]{1,0:T(8,128)(2,1)S(1)} %get-tuple-element.150.qkv_ref, f32[3,2,1024]{2,1,0:T(2,128)S(1)} %get-tuple-element.155.lse_ref, bf16[1024,384]{1,0:T(8,128)(2,1)S(1)} %convolution_convert_fusion.5.grad_ref), custom_call_target="tpu_custom_call" | custom-call | tf_op jit(solution)/shard_map/attend_back/pallas_call | solution.py:309
  134.7 0.8 collective-permute-start.31
  135.8 0.9 collective-permute-start.27
  136.6 7.0 %attend_back.3 = (bf16[1024,1152]{1,0:T(8,128)(2,1)S(1)}, f32[3,1,384]{2,1,0:T(1,128)S(1)}) custom-call(bf16[1024,1152]{1,0:T(8,128)(2,1)S(1)} %get-tuple-element.150.qkv_ref, f32[3,2,1024]{2,1,0:T(2,128)S(1)} %get-tuple-element.155.lse_ref, bf16[1024,384]{1,0:T(8,128)(2,1)S(1)} %convolution_convert_fusion.5.grad_ref, ...), custom_call_target="tpu_custom_call", output_to_operand_aliasing={{0}: (3, {}), {1}: (4, {})} | custom-call | tf_op jit(solution)/shard_map/attend_back/pallas_call | solution.py:309
  143.6 2.2 %convolution_convert_fusion.2 = bf16[768,1152]{1,0:T(8,128)(2,1)S(1)} fusion(bf16[1024,768]{1,0:T(8,128)(2,1)S(1)} %get-tuple-element.154, bf16[1024,1152]{1,0:T(8,128)(2,1)S(1)} %get-tuple-element.214.d_qkv_ref.qkv_ref), kind=kOutput, calls=%fused_computation.2 | convolution fusion | flops 1812824064 | bytes 5701632 | tf_op jit(solution)/shard_map/fd,fe->de/dot_general | solution.py:640
  146.1 1.5 collective-permute-start.28
  147.6 1.3 collective-permute-start.29
  149.0 1.4 collective-permute-start.32
  150.3 3.9 %last_terms.1 = (bf16[512,768]{1,0:T(8,128)(2,1)S(1)}, bf16[512,768]{1,0:T(8,128)(2,1)S(1)}, f32[512,768]{1,0:T(8,128)S(1)}) custom-call(bf16[1024,1152]{1,0:T(8,128)(2,1)S(1)} %get-tuple-element.214.d_qkv_ref.qkv_ref, bf16[768,1664]{1,0:T(8,128)(2,1)S(1)} %bitcast.163, bf16[1024,1536]{1,0:T(8,128)(2,1)S(1)} %get-tuple-element.215.act_ref, ...), custom_call_target="tpu_custom_call" | custom-call | tf_op jit(solution)/shard_map/last_terms/pallas_call | solution.py:634
  154.3 2.4 %collective-permute-done.32 = bf16[1,48,1536]{2,1,0:T(8,128)(2,1)S(1)} collective-permute-done((bf16[1,48,1536]{2,1,0:T(8,128)(2,1)S(1)}, bf16[1,48,1536]{2,1,0:T(8,128)(2,1)S(1)}, u32[]{:S(2)}, u32[]{:S(2)}) %collective-permute-start.32) | collective-permute-done | bytes 147488 | tf_op jit(solution)/shard_map/ppermute | solution.py:44
  157.9 0.8 collective-permute-start.33
  158.8 1.5 collective-permute-start.34
  161.7 3.3 %first_norm_back.1 = (f32[512,768]{1,0:T(8,128)}, f32[2,768]{1,0:T(2,128)S(1)}) custom-call(bf16[1024,1152]{1,0:T(8,128)(2,1)S(1)} %get-tuple-element.214.d_qkv_ref.qkv_ref, bf16[768,1664]{1,0:T(8,128)(2,1)S(1)} %bitcast.164, bf16[512,768]{1,0:T(8,128)(2,1)S(1)} %bitcast.175, f32[512,768]{1,0:T(8,128)S(1)} %get-tuple-element.231.d_hidden_ref, ...), custom_call_target="tpu_custom_call" | custom-call | tf_op jit(solution)/shard_map/first_norm_back/pallas_call | solution.py:611
  165.6 3.0 %collective-permute-done.33 = bf16[2,48,1920]{2,1,0:T(8,128)(2,1)S(1)} collective-permute-done((bf16[2,48,1920]{2,1,0:T(8,128)(2,1)S(1)}, bf16[2,48,1920]{2,1,0:T(8,128)(2,1)S(1)}, u32[]{:S(2)}, u32[]{:S(2)}) %collective-permute-start.33) | collective-permute-done | bytes 368672 | tf_op jit(solution)/shard_map/ppermute | solution.py:44
  168.6 2.0 %collective-permute-done.34 = bf16[4,48,1152]{2,1,0:T(8,128)(2,1)S(1)} collective-permute-done((bf16[4,48,1152]{2,1,0:T(8,128)(2,1)S(1)}, bf16[4,48,1152]{2,1,0:T(8,128)(2,1)S(1)}, u32[]{:S(2)}, u32[]{:S(2)}) %collective-permute-start.34) | collective-permute-done | bytes 442400 | tf_op jit(solution)/shard_map/ppermute | solution.py:44
  170.7 1.2 collective-permute-done.35
  172.1 1.3 collective-permute-start.39
  174.1 3.4 %collective-permute-done.40 = f32[11,768]{1,0:T(8,128)S(1)} collective-permute-done((f32[11,768]{1,0:T(8,128)S(1)}, f32[11,768]{1,0:T(8,128)S(1)}, u32[]{:S(2)}, u32[]{:S(2)}) %collective-permute-start.40) | collective-permute-done | bytes 33824 | tf_op jit(solution)/shard_map/ppermute | solution.py:44
  178.3 0.9 collective-permute-start.46
  179.3 2.4 %collective-permute-done.41 = f32[11,768]{1,0:T(8,128)S(1)} collective-permute-done((f32[11,768]{1,0:T(8,128)S(1)}, f32[11,768]{1,0:T(8,128)S(1)}, u32[]{:S(2)}, u32[]{:S(2)}) %collective-permute-start.41) | collective-permute-done | bytes 33824 | tf_op jit(solution)/shard_map/ppermute | solution.py:44
  181.8 0.9 collective-permute-start.43
  182.8 1.2 collective-permute-start.44
  184.0 1.4 add_bitcast_fusion
  185.4 1.8 collective-permute-done.44
  187.2 2.3 %collective-permute-start.45 = (f32[11,768]{1,0:T(8,128)S(1)}, f32[11,768]{1,0:T(8,128)S(1)}, u32[]{:S(2)}, u32[]{:S(2)}) collective-permute-start(f32[11,768]{1,0:T(8,128)S(1)} %add.98.sums_ref), channel_id=1, source_target_pairs={{0,16},{2,18},{4,20},{6,22},{8,24},{10,26},{12,28},{14,30},{16,0},... | collective-permute-start | bytes 101384 | tf_op jit(solution)/shard_map/ppermute | solution.py:44
  189.5 1.4 collective-permute-done.46
  190.9 0.8 finish_mid.1
  191.7 1.9 collective-permute-done.45.sums_got_ref
  (127 shorter events, 17.7 us)
Async XLA Ops:
  1.4 0.9 copy-start.2
  2.3 0.8 copy-start.3
  3.1 10.1 %collective-permute-start = (bf16[1,48,1664]{2,1,0:T(8,128)(2,1)S(1)}, bf16[1,48,1664]{2,1,0:T(8,128)(2,1)S(1)}, u32[]{:S(2)}, u32[]{:S(2)}) collective-permute-start(bf16[1,48,1664]{2,1,0:T(8,128)(2,1)S(1)} %bitcast.178), channel_id=1, source_target_pairs={{0,24},{2,26},{4,28},{6,30},{8,16},{10,18},{12,20},{14,22},{16,8},... | collective-permute-start | bytes 479240 | tf_op jit(solution)/shard_map/ppermute | solution.py:44
  8.2 13.5 %collective-permute-start.1 = (bf16[1,48,1664]{2,1,0:T(8,128)(2,1)S(1)}, bf16[1,48,1664]{2,1,0:T(8,128)(2,1)S(1)}, u32[]{:S(2)}, u32[]{:S(2)}) collective-permute-start(bf16[1,48,1664]{2,1,0:T(8,128)(2,1)S(1)} %bitcast.179), channel_id=1, source_target_pairs={{0,16},{2,18},{4,20},{6,22},{8,24},{10,26},{12,28},{14,30},{16,0},... | collective-permute-start | bytes 479240 | tf_op jit(solution)/shard_map/ppermute | solution.py:44
  8.2 13.5 %collective-permute-start.2 = (bf16[1,48,1664]{2,1,0:T(8,128)(2,1)S(1)}, bf16[1,48,1664]{2,1,0:T(8,128)(2,1)S(1)}, u32[]{:S(2)}, u32[]{:S(2)}) collective-permute-start(bf16[1,48,1664]{2,1,0:T(8,128)(2,1)S(1)} %bitcast.180), channel_id=1, source_target_pairs={{0,8},{2,10},{4,12},{6,14},{8,0},{10,2},{12,4},{14,6},{16,24},{18,... | collective-permute-start | bytes 479240 | tf_op jit(solution)/shard_map/ppermute | solution.py:44
  8.9 13.1 %collective-permute-start.3 = (bf16[512,768]{1,0:T(8,128)(2,1)}, bf16[512,768]{1,0:T(8,128)(2,1)S(1)}, u32[]{:S(2)}, u32[]{:S(2)}) collective-permute-start(bf16[512,768]{1,0:T(8,128)(2,1)} %bitcast.173), channel_id=1, source_target_pairs={{0,1},{1,0},{2,3},{3,2},{4,5},{5,4},{6,7},{7,6},{8,9},{9,8},{10,11... | collective-permute-start | bytes 2359304 | tf_op jit(solution)/shard_map/ppermute | solution.py:48
  21.8 15.3 %copy-start = (bf16[1,512,768]{2,1,0:T(8,128)(2,1)S(1)}, bf16[1,512,768]{2,1,0:T(8,128)(2,1)}, u32[]{:S(2)}) copy-start(bf16[1,512,768]{2,1,0:T(8,128)(2,1)} %param.10) | copy-start | bytes 2359300
  22.0 15.0 %collective-permute-start.8 = (bf16[1,48,3072]{2,1,0:T(8,128)(2,1)S(1)}, bf16[1,48,3072]{2,1,0:T(8,128)(2,1)S(1)}, u32[]{:S(2)}, u32[]{:S(2)}) collective-permute-start(bf16[1,48,3072]{2,1,0:T(8,128)(2,1)S(1)} %maximum_bitcast_fusion.2), channel_id=1, source_target_pairs={{0,16},{2,18},{4,20},{6,22},{8,24},{10,26},{12,28},{14,30},{16,0},... | collective-permute-start | bytes 884744 | tf_op jit(solution)/shard_map/ppermute | solution.py:44
  22.1 15.5 %collective-permute-start.4 = (bf16[4,48,1664]{2,1,0:T(8,128)(2,1)S(1)}, bf16[4,48,1664]{2,1,0:T(8,128)(2,1)S(1)}, u32[]{:S(2)}, u32[]{:S(2)}) collective-permute-start(bf16[4,48,1664]{2,1,0:T(8,128)(2,1)S(1)} %maximum_bitcast_fusion.refs_0_), channel_id=1, source_target_pairs={{0,2},{2,0},{4,6},{6,4},{8,10},{10,8},{12,14},{14,12},{16,18},{18,... | collective-permute-start | bytes 1916936 | tf_op jit(solution)/shard_map/ppermute | solution.py:44
  23.6 15.2 %collective-permute-start.5 = (bf16[4,48,1664]{2,1,0:T(8,128)(2,1)S(1)}, bf16[4,48,1664]{2,1,0:T(8,128)(2,1)S(1)}, u32[]{:S(2)}, u32[]{:S(2)}) collective-permute-start(bf16[4,48,1664]{2,1,0:T(8,128)(2,1)S(1)} %maximum_bitcast_fusion.refs_0_), channel_id=1, source_target_pairs={{0,4},{2,6},{4,0},{6,2},{8,12},{10,14},{12,8},{14,10},{16,20},{18,... | collective-permute-start | bytes 1916936 | tf_op jit(solution)/shard_map/ppermute | solution.py:44
  37.1 15.3 %collective-permute-start.9 = (bf16[2,48,3072]{2,1,0:T(8,128)(2,1)S(1)}, bf16[2,48,3072]{2,1,0:T(8,128)(2,1)S(1)}, u32[]{:S(2)}, u32[]{:S(2)}) collective-permute-start(bf16[2,48,3072]{2,1,0:T(8,128)(2,1)S(1)} %maximum_bitcast_fusion.1), channel_id=1, source_target_pairs={{0,8},{2,10},{4,12},{6,14},{8,0},{10,2},{12,4},{14,6},{16,24},{18,... | collective-permute-start | bytes 1769480 | tf_op jit(solution)/shard_map/ppermute | solution.py:44
  38.8 13.9 %collective-permute-start.6 = (bf16[2,48,1664]{2,1,0:T(8,128)(2,1)S(1)}, bf16[2,48,1664]{2,1,0:T(8,128)(2,1)S(1)}, u32[]{:S(2)}, u32[]{:S(2)}) collective-permute-start(bf16[2,48,1664]{2,1,0:T(8,128)(2,1)S(1)} %slice.59), channel_id=1, source_target_pairs={{0,4},{2,6},{4,0},{6,2},{8,12},{10,14},{12,8},{14,10},{16,20},{18,... | collective-permute-start | bytes 958472 | tf_op jit(solution)/shard_map/ppermute | solution.py:44
  40.4 12.3 %collective-permute-start.7 = (bf16[2,48,1664]{2,1,0:T(8,128)(2,1)S(1)}, bf16[2,48,1664]{2,1,0:T(8,128)(2,1)S(1)}, u32[]{:S(2)}, u32[]{:S(2)}) collective-permute-start(bf16[2,48,1664]{2,1,0:T(8,128)(2,1)S(1)} %slice.60), channel_id=1, source_target_pairs={{0,2},{2,0},{4,6},{6,4},{8,10},{10,8},{12,14},{14,12},{16,18},{18,... | collective-permute-start | bytes 958472 | tf_op jit(solution)/shard_map/ppermute | solution.py:44
  52.7 3.3 %copy-start.5 = (bf16[2,384]{1,0:T(2,128)(2,1)S(1)}, bf16[2,384]{1,0:T(2,128)(2,1)}, u32[]{:S(2)}) copy-start(bf16[2,384]{1,0:T(2,128)(2,1)} %bias_ref.2) | copy-start | bytes 4612
  52.7 27.1 %collective-permute-start.12 = (bf16[4,48,3072]{2,1,0:T(8,128)(2,1)S(1)}, bf16[4,48,3072]{2,1,0:T(8,128)(2,1)S(1)}, u32[]{:S(2)}, u32[]{:S(2)}) collective-permute-start(bf16[4,48,3072]{2,1,0:T(8,128)(2,1)S(1)} %bitcast.167), channel_id=1, source_target_pairs={{0,2},{2,0},{4,6},{6,4},{8,10},{10,8},{12,14},{14,12},{16,18},{18,... | collective-permute-start | bytes 3538952 | tf_op jit(solution)/shard_map/ppermute | solution.py:44
  54.3 26.8 %collective-permute-start.13 = (bf16[4,48,3072]{2,1,0:T(8,128)(2,1)S(1)}, bf16[4,48,3072]{2,1,0:T(8,128)(2,1)S(1)}, u32[]{:S(2)}, u32[]{:S(2)}) collective-permute-start(bf16[4,48,3072]{2,1,0:T(8,128)(2,1)S(1)} %bitcast.168), channel_id=1, source_target_pairs={{0,4},{2,6},{4,0},{6,2},{8,12},{10,14},{12,8},{14,10},{16,20},{18,... | collective-permute-start | bytes 3538952 | tf_op jit(solution)/shard_map/ppermute | solution.py:44
  74.0 1.1 copy-start.1
  74.1 2.4 %collective-permute-start.10 = (bf16[512,768]{1,0:T(8,128)(2,1)S(1)}, bf16[512,768]{1,0:T(8,128)(2,1)S(1)}, u32[]{:S(2)}, u32[]{:S(2)}) collective-permute-start(bf16[512,768]{1,0:T(8,128)(2,1)S(1)} %get-tuple-element.279), channel_id=1, source_target_pairs={{0,1},{1,0},{2,3},{3,2},{4,5},{5,4},{6,7},{7,6},{8,9},{9,8},{10,11... | collective-permute-start | bytes 2359304 | tf_op jit(solution)/shard_map/ppermute | solution.py:48
  74.2 3.4 %collective-permute-start.11 = (bf16[512,768]{1,0:T(8,128)(2,1)S(1)}, bf16[512,768]{1,0:T(8,128)(2,1)S(1)}, u32[]{:S(2)}, u32[]{:S(2)}) collective-permute-start(bf16[512,768]{1,0:T(8,128)(2,1)S(1)} %get-tuple-element.278), channel_id=1, source_target_pairs={{0,1},{1,0},{2,3},{3,2},{4,5},{5,4},{6,7},{7,6},{8,9},{9,8},{10,11... | collective-permute-start | bytes 2359304 | tf_op jit(solution)/shard_map/ppermute | solution.py:48
  75.1 4.1 %collective-permute-start.14 = (bf16[512,768]{1,0:T(8,128)(2,1)S(1)}, bf16[512,768]{1,0:T(8,128)(2,1)S(1)}, u32[]{:S(2)}, u32[]{:S(2)}) collective-permute-start(bf16[512,768]{1,0:T(8,128)(2,1)S(1)} %bitcast.176), channel_id=1, source_target_pairs={{0,1},{1,0},{2,3},{3,2},{4,5},{5,4},{6,7},{7,6},{8,9},{9,8},{10,11... | collective-permute-start | bytes 2359304 | tf_op jit(solution)/shard_map/ppermute | solution.py:48
  81.1 7.3 %collective-permute-start.15 = (bf16[2,48,1536]{2,1,0:T(8,128)(2,1)S(1)}, bf16[2,48,1536]{2,1,0:T(8,128)(2,1)S(1)}, u32[]{:S(2)}, u32[]{:S(2)}) collective-permute-start(bf16[2,48,1536]{2,1,0:T(8,128)(2,1)S(1)} %slice.65), channel_id=1, source_target_pairs={{0,4},{2,6},{4,0},{6,2},{8,12},{10,14},{12,8},{14,10},{16,20},{18,... | collective-permute-start | bytes 884744 | tf_op jit(solution)/shard_map/ppermute | solution.py:44
  82.7 6.8 %collective-permute-start.16 = (bf16[2,48,1536]{2,1,0:T(8,128)(2,1)S(1)}, bf16[2,48,1536]{2,1,0:T(8,128)(2,1)S(1)}, u32[]{:S(2)}, u32[]{:S(2)}) collective-permute-start(bf16[2,48,1536]{2,1,0:T(8,128)(2,1)S(1)} %slice.66), channel_id=1, source_target_pairs={{0,2},{2,0},{4,6},{6,4},{8,10},{10,8},{12,14},{14,12},{16,18},{18,... | collective-permute-start | bytes 884744 | tf_op jit(solution)/shard_map/ppermute | solution.py:44
  89.5 9.7 %collective-permute-start.17 = (bf16[2,48,1536]{2,1,0:T(8,128)(2,1)S(1)}, bf16[2,48,1536]{2,1,0:T(8,128)(2,1)S(1)}, u32[]{:S(2)}, u32[]{:S(2)}) collective-permute-start(bf16[2,48,1536]{2,1,0:T(8,128)(2,1)S(1)} %slice.67), channel_id=1, source_target_pairs={{0,4},{2,6},{4,0},{6,2},{8,12},{10,14},{12,8},{14,10},{16,20},{18,... | collective-permute-start | bytes 884744 | tf_op jit(solution)/shard_map/ppermute | solution.py:44
  90.3 0.8 copy-start.4
  90.3 8.9 %collective-permute-start.18 = (bf16[2,48,1536]{2,1,0:T(8,128)(2,1)S(1)}, bf16[2,48,1536]{2,1,0:T(8,128)(2,1)S(1)}, u32[]{:S(2)}, u32[]{:S(2)}) collective-permute-start(bf16[2,48,1536]{2,1,0:T(8,128)(2,1)S(1)} %slice.68), channel_id=1, source_target_pairs={{0,2},{2,0},{4,6},{6,4},{8,10},{10,8},{12,14},{14,12},{16,18},{18,... | collective-permute-start | bytes 884744 | tf_op jit(solution)/shard_map/ppermute | solution.py:44
  99.2 8.9 %collective-permute-start.19 = (bf16[2,48,1536]{2,1,0:T(8,128)(2,1)S(1)}, bf16[2,48,1536]{2,1,0:T(8,128)(2,1)S(1)}, u32[]{:S(2)}, u32[]{:S(2)}) collective-permute-start(bf16[2,48,1536]{2,1,0:T(8,128)(2,1)S(1)} %get-tuple-element.183), channel_id=1, source_target_pairs={{0,2},{2,0},{4,6},{6,4},{8,10},{10,8},{12,14},{14,12},{16,18},{18,... | collective-permute-start | bytes 884744 | tf_op jit(solution)/shard_map/ppermute | solution.py:44
  100.7 7.3 %collective-permute-start.20 = (bf16[2,48,1536]{2,1,0:T(8,128)(2,1)S(1)}, bf16[2,48,1536]{2,1,0:T(8,128)(2,1)S(1)}, u32[]{:S(2)}, u32[]{:S(2)}) collective-permute-start(bf16[2,48,1536]{2,1,0:T(8,128)(2,1)S(1)} %get-tuple-element.184), channel_id=1, source_target_pairs={{0,4},{2,6},{4,0},{6,2},{8,12},{10,14},{12,8},{14,10},{16,20},{18,... | collective-permute-start | bytes 884744 | tf_op jit(solution)/shard_map/ppermute | solution.py:44
  108.5 4.8 %collective-permute-start.21 = (bf16[512,768]{1,0:T(8,128)(2,1)S(1)}, bf16[512,768]{1,0:T(8,128)(2,1)S(1)}, u32[]{:S(2)}, u32[]{:S(2)}) collective-permute-start(bf16[512,768]{1,0:T(8,128)(2,1)S(1)} %get-tuple-element.277), channel_id=1, source_target_pairs={{0,1},{1,0},{2,3},{3,2},{4,5},{5,4},{6,7},{7,6},{8,9},{9,8},{10,11... | collective-permute-start | bytes 2359304 | tf_op jit(solution)/shard_map/ppermute | solution.py:48
  108.6 4.7 %collective-permute-start.22 = (bf16[512,768]{1,0:T(8,128)(2,1)S(1)}, bf16[512,768]{1,0:T(8,128)(2,1)S(1)}, u32[]{:S(2)}, u32[]{:S(2)}) collective-permute-start(bf16[512,768]{1,0:T(8,128)(2,1)S(1)} %get-tuple-element.276), channel_id=1, source_target_pairs={{0,1},{1,0},{2,3},{3,2},{4,5},{5,4},{6,7},{7,6},{8,9},{9,8},{10,11... | collective-permute-start | bytes 2359304 | tf_op jit(solution)/shard_map/ppermute | solution.py:48
  109.1 24.6 %collective-permute-start.25 = (bf16[4,48,1536]{2,1,0:T(8,128)(2,1)S(1)}, bf16[4,48,1536]{2,1,0:T(8,128)(2,1)S(1)}, u32[]{:S(2)}, u32[]{:S(2)}) collective-permute-start(bf16[4,48,1536]{2,1,0:T(8,128)(2,1)S(1)} %pad_maximum_fusion.4), channel_id=1, source_target_pairs={{0,2},{2,0},{4,6},{6,4},{8,10},{10,8},{12,14},{14,12},{16,18},{18,... | collective-permute-start | bytes 1769480 | tf_op jit(solution)/shard_map/ppermute | solution.py:44
  109.6 24.1 %collective-permute-start.26 = (bf16[4,48,1536]{2,1,0:T(8,128)(2,1)S(1)}, bf16[4,48,1536]{2,1,0:T(8,128)(2,1)S(1)}, u32[]{:S(2)}, u32[]{:S(2)}) collective-permute-start(bf16[4,48,1536]{2,1,0:T(8,128)(2,1)S(1)} %pad_maximum_fusion.5), channel_id=1, source_target_pairs={{0,4},{2,6},{4,0},{6,2},{8,12},{10,14},{12,8},{14,10},{16,20},{18,... | collective-permute-start | bytes 1769480 | tf_op jit(solution)/shard_map/ppermute | solution.py:44
  118.3 15.4 %collective-permute-start.23 = (bf16[2,48,1920]{2,1,0:T(8,128)(2,1)S(1)}, bf16[2,48,1920]{2,1,0:T(8,128)(2,1)S(1)}, u32[]{:S(2)}, u32[]{:S(2)}) collective-permute-start(bf16[2,48,1920]{2,1,0:T(8,128)(2,1)S(1)} %get-tuple-element.197), channel_id=1, source_target_pairs={{0,2},{2,0},{4,6},{6,4},{8,10},{10,8},{12,14},{14,12},{16,18},{18,... | collective-permute-start | bytes 1105928 | tf_op jit(solution)/shard_map/ppermute | solution.py:44
  119.8 13.9 %collective-permute-start.24 = (bf16[2,48,1920]{2,1,0:T(8,128)(2,1)S(1)}, bf16[2,48,1920]{2,1,0:T(8,128)(2,1)S(1)}, u32[]{:S(2)}, u32[]{:S(2)}) collective-permute-start(bf16[2,48,1920]{2,1,0:T(8,128)(2,1)S(1)} %get-tuple-element.198), channel_id=1, source_target_pairs={{0,4},{2,6},{4,0},{6,2},{8,12},{10,14},{12,8},{14,10},{16,20},{18,... | collective-permute-start | bytes 1105928 | tf_op jit(solution)/shard_map/ppermute | solution.py:44
  134.0 22.6 %collective-permute-start.30 = (bf16[4,48,1920]{2,1,0:T(8,128)(2,1)S(1)}, bf16[4,48,1920]{2,1,0:T(8,128)(2,1)S(1)}, u32[]{:S(2)}, u32[]{:S(2)}) collective-permute-start(bf16[4,48,1920]{2,1,0:T(8,128)(2,1)S(1)} %pad_maximum_fusion.2), channel_id=1, source_target_pairs={{0,2},{2,0},{4,6},{6,4},{8,10},{10,8},{12,14},{14,12},{16,18},{18,... | collective-permute-start | bytes 2211848 | tf_op jit(solution)/shard_map/ppermute | solution.py:44
  134.7 22.0 %collective-permute-start.31 = (bf16[4,48,1920]{2,1,0:T(8,128)(2,1)S(1)}, bf16[4,48,1920]{2,1,0:T(8,128)(2,1)S(1)}, u32[]{:S(2)}, u32[]{:S(2)}) collective-permute-start(bf16[4,48,1920]{2,1,0:T(8,128)(2,1)S(1)} %pad_maximum_fusion.3), channel_id=1, source_target_pairs={{0,4},{2,6},{4,0},{6,2},{8,12},{10,14},{12,8},{14,10},{16,20},{18,... | collective-permute-start | bytes 2211848 | tf_op jit(solution)/shard_map/ppermute | solution.py:44
  135.8 10.3 %collective-permute-start.27 = (bf16[2,48,1536]{2,1,0:T(8,128)(2,1)S(1)}, bf16[2,48,1536]{2,1,0:T(8,128)(2,1)S(1)}, u32[]{:S(2)}, u32[]{:S(2)}) collective-permute-start(bf16[2,48,1536]{2,1,0:T(8,128)(2,1)S(1)} %fusion.9), channel_id=1, source_target_pairs={{0,8},{2,10},{4,12},{6,14},{8,0},{10,2},{12,4},{14,6},{16,24},{18,... | collective-permute-start | bytes 884744 | tf_op jit(solution)/shard_map/ppermute | solution.py:44
  146.1 10.6 %collective-permute-start.28 = (bf16[2,48,1152]{2,1,0:T(8,128)(2,1)S(1)}, bf16[2,48,1152]{2,1,0:T(8,128)(2,1)S(1)}, u32[]{:S(2)}, u32[]{:S(2)}) collective-permute-start(bf16[2,48,1152]{2,1,0:T(8,128)(2,1)S(1)} %get-tuple-element.212), channel_id=1, source_target_pairs={{0,2},{2,0},{4,6},{6,4},{8,10},{10,8},{12,14},{14,12},{16,18},{18,... | collective-permute-start | bytes 663560 | tf_op jit(solution)/shard_map/ppermute | solution.py:44
  147.6 9.0 %collective-permute-start.29 = (bf16[2,48,1152]{2,1,0:T(8,128)(2,1)S(1)}, bf16[2,48,1152]{2,1,0:T(8,128)(2,1)S(1)}, u32[]{:S(2)}, u32[]{:S(2)}) collective-permute-start(bf16[2,48,1152]{2,1,0:T(8,128)(2,1)S(1)} %get-tuple-element.213), channel_id=1, source_target_pairs={{0,4},{2,6},{4,0},{6,2},{8,12},{10,14},{12,8},{14,10},{16,20},{18,... | collective-permute-start | bytes 663560 | tf_op jit(solution)/shard_map/ppermute | solution.py:44
  149.0 7.7 %collective-permute-start.32 = (bf16[1,48,1536]{2,1,0:T(8,128)(2,1)S(1)}, bf16[1,48,1536]{2,1,0:T(8,128)(2,1)S(1)}, u32[]{:S(2)}, u32[]{:S(2)}) collective-permute-start(bf16[1,48,1536]{2,1,0:T(8,128)(2,1)S(1)} %dynamic-slice_convert_fusion.1), channel_id=1, source_target_pairs={{0,16},{2,18},{4,20},{6,22},{8,24},{10,26},{12,28},{14,30},{16,0},... | collective-permute-start | bytes 442376 | tf_op jit(solution)/shard_map/ppermute | solution.py:44
  157.0 4.7 %collective-permute-start.36 = (bf16[256,768]{1,0:T(8,128)(2,1)S(1)}, bf16[256,768]{1,0:T(8,128)(2,1)S(1)}, u32[]{:S(2)}, u32[]{:S(2)}) collective-permute-start(bf16[256,768]{1,0:T(8,128)(2,1)S(1)} %get-tuple-element.283), channel_id=1, source_target_pairs={{0,1},{1,0},{2,3},{3,2},{4,5},{5,4},{6,7},{7,6},{8,9},{9,8},{10,11... | collective-permute-start | bytes 1179656 | tf_op jit(solution)/shard_map/ppermute | solution.py:48
  157.1 4.7 %collective-permute-start.37 = (bf16[256,768]{1,0:T(8,128)(2,1)S(1)}, bf16[256,768]{1,0:T(8,128)(2,1)S(1)}, u32[]{:S(2)}, u32[]{:S(2)}) collective-permute-start(bf16[256,768]{1,0:T(8,128)(2,1)S(1)} %get-tuple-element.282), channel_id=1, source_target_pairs={{0,1},{1,0},{2,3},{3,2},{4,5},{5,4},{6,7},{7,6},{8,9},{9,8},{10,11... | collective-permute-start | bytes 1179656 | tf_op jit(solution)/shard_map/ppermute | solution.py:48
  157.9 10.6 %collective-permute-start.33 = (bf16[2,48,1920]{2,1,0:T(8,128)(2,1)S(1)}, bf16[2,48,1920]{2,1,0:T(8,128)(2,1)S(1)}, u32[]{:S(2)}, u32[]{:S(2)}) collective-permute-start(bf16[2,48,1920]{2,1,0:T(8,128)(2,1)S(1)} %fusion.8), channel_id=1, source_target_pairs={{0,8},{2,10},{4,12},{6,14},{8,0},{10,2},{12,4},{14,6},{16,24},{18,... | collective-permute-start | bytes 1105928 | tf_op jit(solution)/shard_map/ppermute | solution.py:44
  158.8 11.9 %collective-permute-start.34 = (bf16[4,48,1152]{2,1,0:T(8,128)(2,1)S(1)}, bf16[4,48,1152]{2,1,0:T(8,128)(2,1)S(1)}, u32[]{:S(2)}, u32[]{:S(2)}) collective-permute-start(bf16[4,48,1152]{2,1,0:T(8,128)(2,1)S(1)} %pad_maximum_fusion.6), channel_id=1, source_target_pairs={{0,2},{2,0},{4,6},{6,4},{8,10},{10,8},{12,14},{14,12},{16,18},{18,... | collective-permute-start | bytes 1327112 | tf_op jit(solution)/shard_map/ppermute | solution.py:44
  160.3 11.6 %collective-permute-start.35 = (bf16[4,48,1152]{2,1,0:T(8,128)(2,1)S(1)}, bf16[4,48,1152]{2,1,0:T(8,128)(2,1)S(1)}, u32[]{:S(2)}, u32[]{:S(2)}) collective-permute-start(bf16[4,48,1152]{2,1,0:T(8,128)(2,1)S(1)} %pad_maximum_fusion.7), channel_id=1, source_target_pairs={{0,4},{2,6},{4,0},{6,2},{8,12},{10,14},{12,8},{14,10},{16,20},{18,... | collective-permute-start | bytes 1327112 | tf_op jit(solution)/shard_map/ppermute | solution.py:44
  161.7 20.1 %collective-permute-start.42 = (bf16[512,768]{1,0:T(8,128)(2,1)S(1)}, bf16[512,768]{1,0:T(8,128)(2,1)S(1)}, u32[]{:S(2)}, u32[]{:S(2)}) collective-permute-start(bf16[512,768]{1,0:T(8,128)(2,1)S(1)} %get-tuple-element.241), channel_id=1, source_target_pairs={{0,1},{1,0},{2,3},{3,2},{4,5},{5,4},{6,7},{7,6},{8,9},{9,8},{10,11... | collective-permute-start | bytes 2359304 | tf_op jit(solution)/shard_map/ppermute | solution.py:48
  165.0 3.6 %collective-permute-start.38 = (f32[6,768]{1,0:T(8,128)S(1)}, f32[6,768]{1,0:T(8,128)S(1)}, u32[]{:S(2)}, u32[]{:S(2)}) collective-permute-start(f32[6,768]{1,0:T(8,128)S(1)} %pad_maximum_fusion.8), channel_id=1, source_target_pairs={{0,1},{1,0},{2,3},{3,2},{4,5},{5,4},{6,7},{7,6},{8,9},{9,8},{10,11... | collective-permute-start | bytes 55304 | tf_op jit(solution)/shard_map/ppermute | solution.py:48
  172.1 9.7 %collective-permute-start.39 = (bf16[2,48,1152]{2,1,0:T(8,128)(2,1)S(1)}, bf16[2,48,1152]{2,1,0:T(8,128)(2,1)S(1)}, u32[]{:S(2)}, u32[]{:S(2)}) collective-permute-start(bf16[2,48,1152]{2,1,0:T(8,128)(2,1)S(1)} %fusion.10), channel_id=1, source_target_pairs={{0,8},{2,10},{4,12},{6,14},{8,0},{10,2},{12,4},{14,6},{16,24},{18,... | collective-permute-start | bytes 663560 | tf_op jit(solution)/shard_map/ppermute | solution.py:44
  173.4 4.2 %collective-permute-start.40 = (f32[11,768]{1,0:T(8,128)S(1)}, f32[11,768]{1,0:T(8,128)S(1)}, u32[]{:S(2)}, u32[]{:S(2)}) collective-permute-start(f32[11,768]{1,0:T(8,128)S(1)} %fusion.12), channel_id=1, source_target_pairs={{0,2},{2,0},{4,6},{6,4},{8,10},{10,8},{12,14},{14,12},{16,18},{18,... | collective-permute-start | bytes 101384 | tf_op jit(solution)/shard_map/ppermute | solution.py:44
  177.6 4.2 %collective-permute-start.41 = (f32[11,768]{1,0:T(8,128)S(1)}, f32[11,768]{1,0:T(8,128)S(1)}, u32[]{:S(2)}, u32[]{:S(2)}) collective-permute-start(f32[11,768]{1,0:T(8,128)S(1)} %fusion.15), channel_id=1, source_target_pairs={{0,4},{2,6},{4,0},{6,2},{8,12},{10,14},{12,8},{14,10},{16,20},{18,... | collective-permute-start | bytes 101384 | tf_op jit(solution)/shard_map/ppermute | solution.py:44
  178.3 12.6 %collective-permute-start.46 = (bf16[1,48,1920]{2,1,0:T(8,128)(2,1)S(1)}, bf16[1,48,1920]{2,1,0:T(8,128)(2,1)S(1)}, u32[]{:S(2)}, u32[]{:S(2)}) collective-permute-start(bf16[1,48,1920]{2,1,0:T(8,128)(2,1)S(1)} %dynamic-slice_convert_fusion), channel_id=1, source_target_pairs={{0,16},{2,18},{4,20},{6,22},{8,24},{10,26},{12,28},{14,30},{16,0},... | collective-permute-start | bytes 552968 | tf_op jit(solution)/shard_map/ppermute | solution.py:44
  181.8 11.7 %collective-permute-start.43 = (bf16[1,48,1152]{2,1,0:T(8,128)(2,1)S(1)}, bf16[1,48,1152]{2,1,0:T(8,128)(2,1)S(1)}, u32[]{:S(2)}, u32[]{:S(2)}) collective-permute-start(bf16[1,48,1152]{2,1,0:T(8,128)(2,1)S(1)} %dynamic-slice_convert_fusion.2), channel_id=1, source_target_pairs={{0,16},{2,18},{4,20},{6,22},{8,24},{10,26},{12,28},{14,30},{16,0},... | collective-permute-start | bytes 331784 | tf_op jit(solution)/shard_map/ppermute | solution.py:44
  182.8 4.5 %collective-permute-start.44 = (f32[11,768]{1,0:T(8,128)S(1)}, f32[11,768]{1,0:T(8,128)S(1)}, u32[]{:S(2)}, u32[]{:S(2)}) collective-permute-start(f32[11,768]{1,0:T(8,128)S(1)} %add.92), channel_id=1, source_target_pairs={{0,8},{2,10},{4,12},{6,14},{8,0},{10,2},{12,4},{14,6},{16,24},{18,... | collective-permute-start | bytes 101384 | tf_op jit(solution)/shard_map/ppermute | solution.py:44
  187.2 6.3 %collective-permute-start.45 = (f32[11,768]{1,0:T(8,128)S(1)}, f32[11,768]{1,0:T(8,128)S(1)}, u32[]{:S(2)}, u32[]{:S(2)}) collective-permute-start(f32[11,768]{1,0:T(8,128)S(1)} %add.98.sums_ref), channel_id=1, source_target_pairs={{0,16},{2,18},{4,20},{6,22},{8,24},{10,26},{12,28},{14,30},{16,0},... | collective-permute-start | bytes 101384 | tf_op jit(solution)/shard_map/ppermute | solution.py:44
